TPU v7x, 128 devices: a whole 4x4x4 slice. The times are simulated.
128 devices in a mesh: wide: 16 (over z_hi, y, core), narrow: 8 (over x, z_lo).
Axes of the slice: x: 4, y: 4, z: 4 (z_hi: 2, z_lo: 2; z = z_hi * 2 + z_lo), core: 2. Of those that a mesh axis runs over, the one named last changes fastest.
Arguments:
- detail: bfloat16 [2048, 1024, 128], P('wide', 'narrow'), may hold values from -120 to 120
- coarse: bfloat16 [512, 256, 128], P('wide', 'narrow'), may hold values from -6 to 6
- diagonal: float32 [2048, 1024], P('wide', 'narrow'), may hold values from 0.5 to 4
- parents: int32 [256, 128], P('wide', 'narrow'), may hold values from 0 to 8191
- tile_mask: int32 [256, 128], P('wide', 'narrow'), may hold values 0 or 1
Outputs:
- embedding: float32 [2048, 1024, 128], P('wide', 'narrow')
Inputs may be any that keep to these rules, and one draw needn't show every extreme that they name: `parents`: A tile in row a names a coarse cell of the coarse rows band * 32 to band * 32 + 31, band = a // 16, any coarse column.
All inputs are finite; a program needn't handle non-finite values. No bound on the sum of `tile_mask` on one device may be relied on, other than what follows from the above.
Results may differ from a plain program's by a relative error of at most 0.0003.
Values may be sent and summed in bfloat16 or wider, within the bound.
A program may use at most 128 MiB of HBM per device.

v0:
```python
import jax
import jax.numpy as jnp
from jax import lax
from jax.sharding import PartitionSpec as P

TS = 8


CENTER = 7.5
HALF_WIDTH = 4.5
EPSILON = 1e-06


def padded_2(array, sides, width):
    for axis, dim in sides:
        count, length = (lax.axis_size(axis), array.shape[dim])
        up = [(i, (i + 1) % count) for i in range(count - 1)]
        down = [(j, i) for i, j in up]
        last = lax.slice_in_dim(array, length - width, length, axis=dim)
        leading = lax.slice_in_dim(array, 0, width, axis=dim)
        before = lax.ppermute(last, axis, up)
        after = lax.ppermute(leading, axis, down)
        array = jnp.concatenate([before, array, after], axis=dim)
    return array


def apply_single(field, diagonal, cell_mask):
    padded = padded_2(field, (("wide", 0), ("narrow", 1)), 1)
    neighbours = padded[2:, 1:-1] + padded[:-2, 1:-1]
    neighbours = neighbours + padded[1:-1, 2:] + padded[1:-1, :-2]
    return cell_mask[..., None] * ((4.0 + diagonal)[..., None] * field - neighbours)


def local(detail, coarse, diagonal, parents, tile_mask):
    tiles_x, tiles_y = parents.shape
    cells_x, cells_y, columns = detail.shape
    total_cells = cells_x * lax.axis_size("wide") * cells_y * lax.axis_size("narrow")
    mask_float = tile_mask.astype(jnp.float32)
    cell_mask = jnp.broadcast_to(mask_float[:, None, :, None], (tiles_x, TS, tiles_y, TS)).reshape(
        cells_x, cells_y
    )
    panels = lax.all_gather(coarse, "narrow", axis=1, tiled=True)
    flat_panel = panels.reshape(-1, columns)
    parent_flat = parents.reshape(-1)
    onehot = (
        parent_flat[:, None] == jnp.arange(flat_panel.shape[0], dtype=jnp.int32)[None, :]
    ).astype(jnp.bfloat16)
    tile_values = jnp.dot(onehot, flat_panel, preferred_element_type=jnp.float32)
    spread = jnp.broadcast_to(
        tile_values.reshape(tiles_x, 1, tiles_y, 1, columns), (tiles_x, TS, tiles_y, TS, columns)
    )
    cells = spread.reshape(cells_x, cells_y, columns)
    cheb_zero = cell_mask[..., None] * (cells + detail.astype(jnp.float32))
    cheb_one = (apply_single(cheb_zero, diagonal, cell_mask) - CENTER * cheb_zero) / HALF_WIDTH
    cheb_two = (
        2.0 * (apply_single(cheb_one, diagonal, cell_mask) - CENTER * cheb_one) / HALF_WIDTH
        - cheb_zero
    )
    cheb_three = (
        2.0 * (apply_single(cheb_two, diagonal, cell_mask) - CENTER * cheb_two) / HALF_WIDTH
        - cheb_one
    )
    local_squares = jnp.sum(cheb_three * cheb_three, axis=(0, 1))
    squares = lax.psum(local_squares, ("wide", "narrow"))
    return cheb_three / jnp.sqrt(squares / total_cells + EPSILON)


def solution(mesh):
    in_specs = (
        P("wide", "narrow", None),
        P("wide", "narrow", None),
        P("wide", "narrow"),
        P("wide", "narrow"),
        P("wide", "narrow"),
    )
    out_specs = P("wide", "narrow", None)
    return jax.shard_map(local, mesh=mesh, in_specs=in_specs, out_specs=out_specs, check_vma=False)
```

profile of v0, /device:TPU:1, one launch (start us, length us, event | category | flops | bytes accessed | tf_op | source)
XLA Modules:
  0.0 310.3 jit_solution(15181172751365269129)
XLA Ops:
  6.5 0.0 all-gather.2.cloned.1.call-start
  6.5 0.7 all-gather.2.cloned.1.call-update
  7.3 0.7 convert_element_type.7
  8.0 0.1 broadcast_in_dim.4
  8.1 0.5 mul.70
  8.6 0.1 copy.6
  8.7 53.1 %all-gather.2.cloned.1.call-done = bf16[32,256,128]{2,1,0:T(8,128)(2,1)} async-done(((bf16[32,32,128]{2,1,0:T(8,128)(2,1)}), bf16[32,256,128]{2,1,0:T(8,128)(2,1)}) %all-gather.2.cloned.1.call-update) | async-done | bytes 2097168 | tf_op jit(solution)/shard_map/all_gather | solution.py:42
  61.8 0.0 copy-start.2
  61.8 3.1 fusion.23
  64.9 1.0 broadcast_in_dim.5
  66.0 0.0 copy-done.2
  66.0 9.7 %add_multiply_fusion = f32[128,128,128]{2,0,1:T(8,128)S(1)} fusion(f32[128,128,128]{2,0,1:T(8,128)S(1)} %bitcast.10, bf16[128,128,128]{2,1,0:T(8,128)(2,1)S(1)} %copy-done.2, f32[128,128]{0,1:T(8,128)S(1)} %copy.6), kind=kLoop, calls=%fused_computation.47 | loop fusion | flops 6291456 | bytes 21037056 | tf_op jit(solution)/shard_map/mul | solution.py:53
  75.7 0.0 copy-start
  75.7 0.0 copy-start.3
  75.7 0.1 fusion.29
  75.8 5.7 %collective-permute-start.1 = (f32[1,128,128]{2,0,1:T(1,128)S(1)}, f32[1,128,128]{2,0,1:T(1,128)S(1)}, u32[]{:S(2)}, u32[]{:S(2)}) collective-permute-start(f32[1,128,128]{2,0,1:T(1,128)S(1)} %get-tuple-element.17), channel_id=1, source_target_pairs={{0,8},{8,16},{16,24},{24,32},{32,40},{40,48},{48,56},{56,64},{64,7... | collective-permute-start | bytes 196616 | tf_op jit(solution)/shard_map/ppermute | solution.py:21
  81.5 1.9 collective-permute-start
  83.4 0.0 collective-permute-done.1
  83.4 3.6 %collective-permute-done = f32[1,128,128]{2,0,1:T(1,128)S(1)} collective-permute-done((f32[1,128,128]{2,0,1:T(1,128)S(1)}, f32[1,128,128]{2,0,1:T(1,128)S(1)}, u32[]{:S(2)}, u32[]{:S(2)}) %collective-permute-start) | collective-permute-done | bytes 65568 | tf_op jit(solution)/shard_map/ppermute | solution.py:22
  87.0 0.0 copy-done
  87.1 1.3 collective-permute-start.2
  88.4 4.0 %collective-permute-start.3 = (f32[130,1,128]{2,0,1:T(8,128)S(1)}, f32[130,1,128]{2,0,1:T(8,128)S(1)}, u32[]{:S(2)}, u32[]{:S(2)}) collective-permute-start(f32[130,1,128]{2,0,1:T(8,128)S(1)} %get-tuple-element.12), channel_id=1, source_target_pairs={{0,1},{1,2},{2,3},{3,4},{4,5},{5,6},{6,7},{8,9},{9,10},{10,11},{11... | collective-permute-start | bytes 199688 | tf_op jit(solution)/shard_map/ppermute | solution.py:21
  92.4 0.0 copy-done.3
  92.4 0.1 copy.7
  92.5 0.0 collective-permute-done.2
  92.5 1.2 collective-permute-done.3
  93.7 17.4 %broadcast_multiply_fusion = f32[128,128,128]{2,0,1:T(8,128)S(1)} fusion(f32[128,128,128]{2,0,1:T(8,128)} %copy-done, f32[1,128,128]{2,0,1:T(1,128)S(1)} %collective-permute-done, f32[1,128,128]{2,0,1:T(1,128)S(1)} %collective-permute-done.1, f32[130,1,128]{2,0,1:T(8,128)S(1)} %collective-permute-done.3, f32[130,1,128]{2,0,1:T(8,128)S(1)} %collective-permute-done.2, ...), kind=kLoop, calls=%fused_computation.52 | loop fusion | flops 35651584 | bytes 17172480 | tf_op jit(solution)/shard_map/div | solution.py:54
  111.1 0.0 copy-start.1
  111.1 0.1 fusion.28
  111.2 3.2 %collective-permute-start.5 = (f32[1,128,128]{2,0,1:T(1,128)S(1)}, f32[1,128,128]{2,0,1:T(1,128)S(1)}, u32[]{:S(2)}, u32[]{:S(2)}) collective-permute-start(f32[1,128,128]{2,0,1:T(1,128)S(1)} %get-tuple-element.15), channel_id=1, source_target_pairs={{0,8},{8,16},{16,24},{24,32},{32,40},{40,48},{48,56},{56,64},{64,7... | collective-permute-start | bytes 196616 | tf_op jit(solution)/shard_map/ppermute | solution.py:21
  114.5 1.9 collective-permute-start.4
  116.4 0.0 collective-permute-done.5
  116.4 3.6 %collective-permute-done.4 = f32[1,128,128]{2,0,1:T(1,128)S(1)} collective-permute-done((f32[1,128,128]{2,0,1:T(1,128)S(1)}, f32[1,128,128]{2,0,1:T(1,128)S(1)}, u32[]{:S(2)}, u32[]{:S(2)}) %collective-permute-start.4) | collective-permute-done | bytes 65568 | tf_op jit(solution)/shard_map/ppermute | solution.py:22
  120.0 0.0 copy-done.1
  120.1 1.3 collective-permute-start.6
  121.4 4.7 %collective-permute-start.7 = (f32[130,1,128]{2,0,1:T(8,128)S(1)}, f32[130,1,128]{2,0,1:T(8,128)S(1)}, u32[]{:S(2)}, u32[]{:S(2)}) collective-permute-start(f32[130,1,128]{2,0,1:T(8,128)S(1)} %get-tuple-element.10), channel_id=1, source_target_pairs={{0,1},{1,2},{2,3},{3,4},{4,5},{5,6},{6,7},{8,9},{9,10},{10,11},{11... | collective-permute-start | bytes 199688 | tf_op jit(solution)/shard_map/ppermute | solution.py:21
  126.1 0.1 copy.10
  126.2 0.0 collective-permute-done.6
  126.2 1.2 collective-permute-done.7
  127.5 30.9 %fusion.13 = f32[128,128,128]{2,0,1:T(8,128)} fusion(f32[128,128,128]{2,0,1:T(8,128)} %copy-done, f32[130,1,128]{2,0,1:T(8,128)S(1)} %collective-permute-done.7, f32[1,128,128]{2,0,1:T(1,128)S(1)} %collective-permute-done.4, f32[128,128,128]{2,0,1:T(8,128)} %copy-done.1, f32[1,128,128]{2,0,1:T(1,128)S(1)} %collective-permute-done.5, ...), kind=kLoop, calls=%fused_computation.22 | loop fusion | flops 71303168 | bytes 25890816 | tf_op jit(solution)/shard_map/sub | solution.py:56
  158.3 1.3 fusion.27
  159.6 3.7 %collective-permute-start.9 = (f32[1,128,128]{2,0,1:T(1,128)S(1)}, f32[1,128,128]{2,0,1:T(1,128)S(1)}, u32[]{:S(2)}, u32[]{:S(2)}) collective-permute-start(f32[1,128,128]{2,0,1:T(1,128)S(1)} %get-tuple-element.13), channel_id=1, source_target_pairs={{0,8},{8,16},{16,24},{24,32},{32,40},{40,48},{48,56},{56,64},{64,7... | collective-permute-start | bytes 196616 | tf_op jit(solution)/shard_map/ppermute | solution.py:21
  163.4 1.9 collective-permute-start.8
  165.3 0.0 collective-permute-done.9
  165.3 3.6 %collective-permute-done.8 = f32[1,128,128]{2,0,1:T(1,128)S(1)} collective-permute-done((f32[1,128,128]{2,0,1:T(1,128)S(1)}, f32[1,128,128]{2,0,1:T(1,128)S(1)}, u32[]{:S(2)}, u32[]{:S(2)}) %collective-permute-start.8) | collective-permute-done | bytes 65568 | tf_op jit(solution)/shard_map/ppermute | solution.py:22
  169.0 0.9 pad_maximum_fusion.26
  169.9 1.3 collective-permute-start.10
  171.2 4.7 %collective-permute-start.11 = (f32[130,1,128]{2,0,1:T(8,128)S(1)}, f32[130,1,128]{2,0,1:T(8,128)S(1)}, u32[]{:S(2)}, u32[]{:S(2)}) collective-permute-start(f32[130,1,128]{2,0,1:T(8,128)S(1)} %get-tuple-element.8), channel_id=1, source_target_pairs={{0,1},{1,2},{2,3},{3,4},{4,5},{5,6},{6,7},{8,9},{9,10},{10,11},{11... | collective-permute-start | bytes 199688 | tf_op jit(solution)/shard_map/ppermute | solution.py:21
  175.9 0.0 collective-permute-done.10
  175.9 1.3 collective-permute-done.11
  177.3 33.9 %multiply_reduce_fusion = (f32[128]{0:T(128)S(1)}, f32[128,128,128]{2,0,1:T(8,128)}) fusion(f32[128,128,128]{2,0,1:T(8,128)} %copy-done, f32[1,128,128]{2,0,1:T(1,128)S(1)} %collective-permute-done, f32[1,128,128]{2,0,1:T(1,128)S(1)} %collective-permute-done.1, f32[130,1,128]{2,0,1:T(8,128)S(1)} %collective-permute-done.3, ...), kind=kLoop, calls=%fused_computation.46 | loop fusion | flops 77594496 | bytes 25825792 | tf_op jit(solution)/shard_map/reduce_sum | solution.py:63
  211.2 79.7 %psum.7 = f32[128]{0:T(128)S(1)} all-reduce(f32[128]{0:T(128)S(1)} %get-tuple-element.5), channel_id=1, replica_groups=mesh['wide'=16,'narrow'=8] {'wide','narrow'}, use_global_device_ids=true, to_apply=%region_1.0 | all-reduce | flops 128 | bytes 1024 | tf_op jit(solution)/shard_map/psum | solution.py:64
  290.9 4.2 %broadcast_divide_fusion = f32[128,128,128]{2,0,1:T(8,128)S(1)} fusion(f32[128,128,128]{2,0,1:T(8,128)} %get-tuple-element.6, f32[128]{0:T(128)S(1)} %add_sqrt_fusion), kind=kLoop, calls=%fused_computation.51 | loop fusion | flops 2097152 | bytes 16777728 | tf_op jit(solution)/shard_map/div | solution.py:65
  295.2 8.3 %copy.11 = f32[128,128,128]{2,1,0:T(8,128)} copy(f32[128,128,128]{2,0,1:T(8,128)S(1)} %broadcast_divide_fusion) | data formatting | bytes 16777216 | tf_op jit(solution)/shard_map/div | solution.py:65
  (5 shorter events, 0.1 us)
Async XLA Ops:
  6.5 55.3 %all-gather.2.cloned.1.call-start = ((), (), s32[]{:S(2)}) async-start(), calls=%async_computation | async-start | bytes 2359296 | tf_op jit(solution)/shard_map/all_gather | solution.py:42
  61.8 4.2 %copy-start.2 = (bf16[128,128,128]{2,1,0:T(8,128)(2,1)S(1)}, bf16[128,128,128]{2,1,0:T(8,128)(2,1)}, u32[]{:S(2)}) copy-start(bf16[128,128,128]{2,1,0:T(8,128)(2,1)} %param.5) | copy-start | bytes 12582916
  75.7 11.4 %copy-start = (f32[128,128,128]{2,0,1:T(8,128)}, f32[128,128,128]{2,0,1:T(8,128)S(1)}, u32[]{:S(2)}) copy-start(f32[128,128,128]{2,0,1:T(8,128)S(1)} %add_multiply_fusion) | copy-start | bytes 25165828
  75.7 16.7 %copy-start.3 = (f32[128,128]{1,0:T(8,128)S(1)}, f32[128,128]{1,0:T(8,128)}, u32[]{:S(2)}) copy-start(f32[128,128]{1,0:T(8,128)} %param.7) | copy-start | bytes 196612
  75.8 7.6 %collective-permute-start.1 = (f32[1,128,128]{2,0,1:T(1,128)S(1)}, f32[1,128,128]{2,0,1:T(1,128)S(1)}, u32[]{:S(2)}, u32[]{:S(2)}) collective-permute-start(f32[1,128,128]{2,0,1:T(1,128)S(1)} %get-tuple-element.17), channel_id=1, source_target_pairs={{0,8},{8,16},{16,24},{24,32},{32,40},{40,48},{48,56},{56,64},{64,7... | collective-permute-start | bytes 196616 | tf_op jit(solution)/shard_map/ppermute | solution.py:21
  81.5 5.6 %collective-permute-start = (f32[1,128,128]{2,0,1:T(1,128)S(1)}, f32[1,128,128]{2,0,1:T(1,128)S(1)}, u32[]{:S(2)}, u32[]{:S(2)}) collective-permute-start(f32[1,128,128]{2,0,1:T(1,128)S(1)} %get-tuple-element.18), channel_id=1, source_target_pairs={{8,0},{16,8},{24,16},{32,24},{40,32},{48,40},{56,48},{64,56},{72,6... | collective-permute-start | bytes 196616 | tf_op jit(solution)/shard_map/ppermute | solution.py:22
  87.1 5.4 %collective-permute-start.2 = (f32[130,1,128]{2,0,1:T(8,128)S(1)}, f32[130,1,128]{2,0,1:T(8,128)S(1)}, u32[]{:S(2)}, u32[]{:S(2)}) collective-permute-start(f32[130,1,128]{2,0,1:T(8,128)S(1)} %get-tuple-element.11), channel_id=1, source_target_pairs={{1,0},{2,1},{3,2},{4,3},{5,4},{6,5},{7,6},{9,8},{10,9},{11,10},{12... | collective-permute-start | bytes 199688 | tf_op jit(solution)/shard_map/ppermute | solution.py:22
  88.4 5.3 %collective-permute-start.3 = (f32[130,1,128]{2,0,1:T(8,128)S(1)}, f32[130,1,128]{2,0,1:T(8,128)S(1)}, u32[]{:S(2)}, u32[]{:S(2)}) collective-permute-start(f32[130,1,128]{2,0,1:T(8,128)S(1)} %get-tuple-element.12), channel_id=1, source_target_pairs={{0,1},{1,2},{2,3},{3,4},{4,5},{5,6},{6,7},{8,9},{9,10},{10,11},{11... | collective-permute-start | bytes 199688 | tf_op jit(solution)/shard_map/ppermute | solution.py:21
  111.1 8.9 %copy-start.1 = (f32[128,128,128]{2,0,1:T(8,128)}, f32[128,128,128]{2,0,1:T(8,128)S(1)}, u32[]{:S(2)}) copy-start(f32[128,128,128]{2,0,1:T(8,128)S(1)} %broadcast_multiply_fusion) | copy-start | bytes 25165828
  111.2 5.2 %collective-permute-start.5 = (f32[1,128,128]{2,0,1:T(1,128)S(1)}, f32[1,128,128]{2,0,1:T(1,128)S(1)}, u32[]{:S(2)}, u32[]{:S(2)}) collective-permute-start(f32[1,128,128]{2,0,1:T(1,128)S(1)} %get-tuple-element.15), channel_id=1, source_target_pairs={{0,8},{8,16},{16,24},{24,32},{32,40},{40,48},{48,56},{56,64},{64,7... | collective-permute-start | bytes 196616 | tf_op jit(solution)/shard_map/ppermute | solution.py:21
  114.5 5.6 %collective-permute-start.4 = (f32[1,128,128]{2,0,1:T(1,128)S(1)}, f32[1,128,128]{2,0,1:T(1,128)S(1)}, u32[]{:S(2)}, u32[]{:S(2)}) collective-permute-start(f32[1,128,128]{2,0,1:T(1,128)S(1)} %get-tuple-element.16), channel_id=1, source_target_pairs={{8,0},{16,8},{24,16},{32,24},{40,32},{48,40},{56,48},{64,56},{72,6... | collective-permute-start | bytes 196616 | tf_op jit(solution)/shard_map/ppermute | solution.py:22
  120.1 6.1 %collective-permute-start.6 = (f32[130,1,128]{2,0,1:T(8,128)S(1)}, f32[130,1,128]{2,0,1:T(8,128)S(1)}, u32[]{:S(2)}, u32[]{:S(2)}) collective-permute-start(f32[130,1,128]{2,0,1:T(8,128)S(1)} %get-tuple-element.9), channel_id=1, source_target_pairs={{1,0},{2,1},{3,2},{4,3},{5,4},{6,5},{7,6},{9,8},{10,9},{11,10},{12... | collective-permute-start | bytes 199688 | tf_op jit(solution)/shard_map/ppermute | solution.py:22
  121.4 6.1 %collective-permute-start.7 = (f32[130,1,128]{2,0,1:T(8,128)S(1)}, f32[130,1,128]{2,0,1:T(8,128)S(1)}, u32[]{:S(2)}, u32[]{:S(2)}) collective-permute-start(f32[130,1,128]{2,0,1:T(8,128)S(1)} %get-tuple-element.10), channel_id=1, source_target_pairs={{0,1},{1,2},{2,3},{3,4},{4,5},{5,6},{6,7},{8,9},{9,10},{10,11},{11... | collective-permute-start | bytes 199688 | tf_op jit(solution)/shard_map/ppermute | solution.py:21
  159.6 5.7 %collective-permute-start.9 = (f32[1,128,128]{2,0,1:T(1,128)S(1)}, f32[1,128,128]{2,0,1:T(1,128)S(1)}, u32[]{:S(2)}, u32[]{:S(2)}) collective-permute-start(f32[1,128,128]{2,0,1:T(1,128)S(1)} %get-tuple-element.13), channel_id=1, source_target_pairs={{0,8},{8,16},{16,24},{24,32},{32,40},{40,48},{48,56},{56,64},{64,7... | collective-permute-start | bytes 196616 | tf_op jit(solution)/shard_map/ppermute | solution.py:21
  163.4 5.6 %collective-permute-start.8 = (f32[1,128,128]{2,0,1:T(1,128)S(1)}, f32[1,128,128]{2,0,1:T(1,128)S(1)}, u32[]{:S(2)}, u32[]{:S(2)}) collective-permute-start(f32[1,128,128]{2,0,1:T(1,128)S(1)} %get-tuple-element.14), channel_id=1, source_target_pairs={{8,0},{16,8},{24,16},{32,24},{40,32},{48,40},{56,48},{64,56},{72,6... | collective-permute-start | bytes 196616 | tf_op jit(solution)/shard_map/ppermute | solution.py:22
  169.9 6.0 %collective-permute-start.10 = (f32[130,1,128]{2,0,1:T(8,128)S(1)}, f32[130,1,128]{2,0,1:T(8,128)S(1)}, u32[]{:S(2)}, u32[]{:S(2)}) collective-permute-start(f32[130,1,128]{2,0,1:T(8,128)S(1)} %get-tuple-element.7), channel_id=1, source_target_pairs={{1,0},{2,1},{3,2},{4,3},{5,4},{6,5},{7,6},{9,8},{10,9},{11,10},{12... | collective-permute-start | bytes 199688 | tf_op jit(solution)/shard_map/ppermute | solution.py:22
  171.2 6.1 %collective-permute-start.11 = (f32[130,1,128]{2,0,1:T(8,128)S(1)}, f32[130,1,128]{2,0,1:T(8,128)S(1)}, u32[]{:S(2)}, u32[]{:S(2)}) collective-permute-start(f32[130,1,128]{2,0,1:T(8,128)S(1)} %get-tuple-element.8), channel_id=1, source_target_pairs={{0,1},{1,2},{2,3},{3,4},{4,5},{5,6},{6,7},{8,9},{9,10},{10,11},{11... | collective-permute-start | bytes 199688 | tf_op jit(solution)/shard_map/ppermute | solution.py:21
Sparse Core Ops, SparseCore 0:
  9.0 52.7 all-gather.1
where the time goes:
time: 311 us; the launch traced here: 310 us
  other arithmetic  97.7 us (31%)
  blocking collectives  79.7 us (26%)
  waiting for transfers between devices  68.6 us (22%)
  starting transfers between devices  35.8 us (12%)
  between operations  13.7 us (4%)
  local copies, waits for them, and re-layouts  11.7 us (4%)
    psum x1, blocking collectives, local(): squares = lax.psum(local_squares, ('wide', 'narrow'))  79.7 us
    all_gather x1, waiting for transfers between devices, local(): panels = lax.all_gather(coarse, 'narrow', axis=1, tiled=True)  53.1 us
    reduce_sum x1, other arithmetic, local(): local_squares = jnp.sum(cheb_three * cheb_three, axis=(0, 1))  33.9 us
    sub x1, other arithmetic, local(): 2.0 * (apply_single(cheb_one, diagonal, cell_mask) - CENTER * cheb_one)  30.9 us
    ppermute x6, starting transfers between devices, padded_2(): before = lax.ppermute(last, axis, up)  26.1 us
    div x1, other arithmetic, local(): (apply_single(cheb_zero, diagonal, cell_mask) - CENTER * cheb_zero) / HAL...  17.4 us
    ppermute x6, waiting for transfers between devices, padded_2(): after = lax.ppermute(leading, axis, down)  10.9 us
    mul x1, other arithmetic, local(): cheb_zero = cell_mask[..., None] * (cells + detail.astype(jnp.float32))  9.67 us
  transfers between devices with their start and end apart: 13, of which 7 were waited for; matrix products, arithmetic and copies ran while one was open for 1% of the time, Pallas kernels for 0%

commit v1 on v0

v1 whole, which is shorter than its diff:
```python
import functools

import jax
import jax.numpy as jnp
from jax import lax
from jax.experimental import pallas as pl
from jax.experimental.pallas import tpu as pltpu
from jax.sharding import PartitionSpec as P

TS = 8
CENTER = 7.5
HALF_WIDTH = 4.5
EPSILON = 1e-06

HALO = 3
LPAD = 8
RING = 16
ROWS = 8


def shift_pairs(dw, dn, nw, nn):
    pairs = []
    for w in range(nw):
        for n in range(nn):
            tw, tn = w + dw, n + dn
            if 0 <= tw < nw and 0 <= tn < nn:
                pairs.append((w * nn + n, tw * nn + tn))
    return pairs


def exchange(pieces, dw, dn, nw, nn):
    flat = jnp.concatenate([p.reshape(-1) for p in pieces])
    got = lax.ppermute(flat, ("wide", "narrow"), shift_pairs(dw, dn, nw, nn))
    out, at = [], 0
    for p in pieces:
        out.append(got[at : at + p.size].reshape(p.shape))
        at += p.size
    return out


def stencil_kernel(det_ref, cm_ref, m_ref, top_ref, bot_ref, left_ref, right_ref, g_ref, h_ref,
                   out_ref, ss_ref, r0, r1, r2):
    i = pl.program_id(0)
    cx = det_ref.shape[0]
    width = g_ref.shape[1]
    ext_rows = g_ref.shape[0]
    cy = det_ref.shape[1]

    def c0_row(x):
        s = x % RING

        @pl.when(x < HALO)
        def _():
            r0[s] = top_ref[jnp.minimum(x, HALO - 1)]

        @pl.when(x >= HALO + cx)
        def _():
            r0[s] = bot_ref[jnp.maximum(x - HALO - cx, 0)]

        @pl.when(jnp.logical_and(x >= HALO, x < HALO + cx))
        def _():
            b = jnp.clip(x - HALO, 0, cx - 1)
            t = b // TS
            r0[s, 0:LPAD] = left_ref[b]
            r0[s, LPAD:LPAD + cy] = cm_ref[t] + m_ref[t] * det_ref[b].astype(jnp.float32)
            r0[s, LPAD + cy:width] = right_ref[b]

    def apply_b(src, x):
        v = src[x % RING]
        nb = src[(x + 1) % RING] + src[(x + RING - 1) % RING]
        nb = nb + pltpu.roll(v, width - 1, 0) + pltpu.roll(v, 1, 0)
        return g_ref[x] * v - h_ref[(x + TS - HALO) // TS] * nb

    def c1_row(x):
        r1[x % RING] = apply_b(r0, x)

    def c2_row(x):
        r2[x % RING] = 2.0 * apply_b(r1, x) - r0[x % RING]

    def c3_row(x):
        c3 = 2.0 * apply_b(r2, x) - r1[x % RING]
        c3 = c3[LPAD:LPAD + cy]
        out_ref[x - HALO - ROWS * i] = c3
        sq = c3 * c3
        ss_ref[...] += jnp.sum(sq.reshape(cy // 8, 8, sq.shape[-1]), axis=0)

    def rows(fn, lo, n):
        def body(k, carry):
            fn(lo + k)
            return carry
        lax.fori_loop(0, n, body, 0)

    @pl.when(i == 0)
    def _():
        ss_ref[...] = jnp.zeros_like(ss_ref)
        rows(c0_row, 0, 2 * HALO)
        rows(c1_row, 1, 2 * HALO - 2)
        rows(c2_row, 2, 2 * HALO - 4)

    base = ROWS * i
    rows(c0_row, base + 2 * HALO, ROWS)
    rows(c1_row, base + 2 * HALO - 1, ROWS)
    rows(c2_row, base + 2 * HALO - 2, ROWS)
    rows(c3_row, base + HALO, ROWS)


def run_stencil(det, cm, m, top, bot, left, right, g, h):
    cx, cy, k = det.shape
    width = g.shape[1]
    steps = cx // ROWS
    vmem = pl.BlockSpec(memory_space=pltpu.VMEM)
    ops = cx * cy * k * 3 * 12
    return pl.pallas_call(
        stencil_kernel,
        grid=(steps,),
        in_specs=[vmem] * 9,
        out_specs=[
            pl.BlockSpec((ROWS, cy, k), lambda i: (i, 0, 0)),
            pl.BlockSpec((8, k), lambda i: (0, 0)),
        ],
        out_shape=[
            jax.ShapeDtypeStruct((cx, cy, k), jnp.float32),
            jax.ShapeDtypeStruct((8, k), jnp.float32),
        ],
        scratch_shapes=[pltpu.VMEM((RING, width, k), jnp.float32) for _ in range(3)],
        compiler_params=pltpu.CompilerParams(
            dimension_semantics=("arbitrary",), vmem_limit_bytes=56 * 1024 * 1024
        ),
        cost_estimate=pl.CostEstimate(
            flops=ops, transcendentals=0, bytes_accessed=det.size * 2 + cx * cy * k * 4 + g.size * 4
        ),
    )(det, cm, m, top, bot, left, right, g, h)


def local(detail, coarse, diagonal, parents, tile_mask):
    tiles_x, tiles_y = parents.shape
    cells_x, cells_y, columns = detail.shape
    nw, nn = lax.axis_size("wide"), lax.axis_size("narrow")
    total_cells = cells_x * nw * cells_y * nn
    mask_float = tile_mask.astype(jnp.float32)

    panels = lax.all_gather(coarse, "narrow", axis=1, tiled=True)
    flat_panel = panels.reshape(-1, columns)
    parent_flat = parents.reshape(-1)
    onehot = (
        parent_flat[:, None] == jnp.arange(flat_panel.shape[0], dtype=jnp.int32)[None, :]
    ).astype(jnp.bfloat16)
    tile_values = jnp.dot(onehot, flat_panel, preferred_element_type=jnp.float32)
    tv = tile_values.reshape(tiles_x, tiles_y, columns)

    m_rows = jnp.repeat(mask_float, TS, axis=1)
    m0 = jnp.broadcast_to(m_rows[:, :, None], (tiles_x, cells_y, columns))
    cm0 = m0 * jnp.repeat(tv, TS, axis=1)

    det_f = detail.astype(jnp.float32)
    h = HALO
    c0_top = cm0[0][None] + m0[0][None] * det_f[:h]
    c0_bot = cm0[-1][None] + m0[-1][None] * det_f[-h:]
    cm_rep = jnp.repeat(cm0, TS, axis=0)
    m_rep = jnp.repeat(m0, TS, axis=0)
    c0_left = cm_rep[:, :h] + m_rep[:, :h] * det_f[:, :h]
    c0_right = cm_rep[:, -h:] + m_rep[:, -h:] * det_f[:, -h:]

    d = diagonal
    mf = mask_float
    top_c, top_d, top_m = exchange([c0_bot, d[-h:], mf[-1:]], 1, 0, nw, nn)
    bot_c, bot_d, bot_m = exchange([c0_top, d[:h], mf[:1]], -1, 0, nw, nn)
    lft_c, lft_d, lft_m = exchange([c0_right, d[:, -h:], mf[:, -1:]], 0, 1, nw, nn)
    rgt_c, rgt_d, rgt_m = exchange([c0_left, d[:, :h], mf[:, :1]], 0, -1, nw, nn)
    tl_c, tl_d, tl_m = exchange([c0_bot[:, -h:], d[-h:, -h:], mf[-1:, -1:]], 1, 1, nw, nn)
    tr_c, tr_d, tr_m = exchange([c0_bot[:, :h], d[-h:, :h], mf[-1:, :1]], 1, -1, nw, nn)
    bl_c, bl_d, bl_m = exchange([c0_top[:, -h:], d[:h, -h:], mf[:1, -1:]], -1, 1, nw, nn)
    br_c, br_d, br_m = exchange([c0_top[:, :h], d[:h, :h], mf[:1, :1]], -1, -1, nw, nn)

    rpad = LPAD - h
    z3 = jnp.zeros((h, rpad, columns), jnp.float32)
    top = jnp.concatenate([z3, tl_c, top_c, tr_c, z3], axis=1)
    bot = jnp.concatenate([z3, bl_c, bot_c, br_c, z3], axis=1)
    zc = jnp.zeros((cells_x, rpad, columns), jnp.float32)
    left = jnp.concatenate([zc, lft_c], axis=1)
    right = jnp.concatenate([rgt_c, zc], axis=1)

    zd3 = jnp.zeros((h, rpad), jnp.float32)
    zdc = jnp.zeros((cells_x, rpad), jnp.float32)
    diag_ext = jnp.concatenate(
        [
            jnp.concatenate([zd3, tl_d, top_d, tr_d, zd3], axis=1),
            jnp.concatenate([zdc, lft_d, d, rgt_d, zdc], axis=1),
            jnp.concatenate([zd3, bl_d, bot_d, br_d, zd3], axis=1),
        ],
        axis=0,
    )
    mask_ext = jnp.concatenate(
        [
            jnp.concatenate([tl_m, top_m, tr_m], axis=1),
            jnp.concatenate([lft_m, mf, rgt_m], axis=1),
            jnp.concatenate([bl_m, bot_m, br_m], axis=1),
        ],
        axis=0,
    )
    reps = [h] + [TS] * tiles_x + [h]
    cell_mask_ext = jnp.repeat(
        jnp.repeat(mask_ext, jnp.array(reps), axis=0, total_repeat_length=cells_x + 2 * h), TS, axis=1
    )
    g = (cell_mask_ext * (4.0 + diag_ext) - CENTER) / HALF_WIDTH
    width = cells_y + 2 * LPAD
    g_b = jnp.broadcast_to(g[:, :, None], (cells_x + 2 * h, width, columns))
    h_t = jnp.repeat(mask_ext / HALF_WIDTH, TS, axis=1)
    h_b = jnp.broadcast_to(h_t[:, :, None], (tiles_x + 2, width, columns))

    cheb_three, ss = run_stencil(detail, cm0, m0, top, bot, left, right, g_b, h_b)
    local_squares = jnp.sum(ss, axis=0)
    squares = lax.psum(local_squares, ("wide", "narrow"))
    return cheb_three / jnp.sqrt(squares / total_cells + EPSILON)


def solution(mesh):
    in_specs = (
        P("wide", "narrow", None),
        P("wide", "narrow", None),
        P("wide", "narrow"),
        P("wide", "narrow"),
        P("wide", "narrow"),
    )
    out_specs = P("wide", "narrow", None)
    return jax.shard_map(local, mesh=mesh, in_specs=in_specs, out_specs=out_specs, check_vma=False)
```

time: 311 us -> 237 us (0.76)
  other arithmetic: 97.7 us -> 22.6 us
  Pallas kernels: 0 us -> 28.3 us
  waiting for transfers between devices: 68.6 us -> 47.1 us
  local copies, waits for them, and re-layouts: 11.7 us -> 30.2 us
  blocking collectives: 79.7 us -> 67.4 us
  starting transfers between devices: 35.8 us -> 24.1 us
    reduce_sum x1, other arithmetic: 33.9 us -> 0.7 us  [local(): local_squares = jnp.sum(ss, axis=0)]
    sub x1 -> x0, other arithmetic: 30.9 us -> none  [local(): 2.0 * (apply_single(cheb_one, diagonal, cell_mask) - CENTER * cheb_one)]
    pallas_call x0 -> x1, Pallas kernels: none -> 28.3 us  [run_stencil(): pl.pallas_call(stencil_kernel, grid=(steps,), in_specs=[vmem] * 9, out_sp...]
    div x1 -> x2, other arithmetic: 17.4 us -> 2.67 us  [the longest x1 2.52 us: local(): h_t = jnp.repeat(mask_ext / HALF_WIDTH, TS, axis=1)]
    psum x1, blocking collectives: 79.7 us -> 67.4 us  [local(): squares = lax.psum(local_squares, ('wide', 'narrow'))]
    ppermute x12 -> x8, starting transfers between devices: 35.8 us -> 24.1 us  [exchange(): got = lax.ppermute(flat, ('wide', 'narrow'), shift_pairs(dw, dn, nw, nn))]
    all_gather x1, waiting for transfers between devices: 53.1 us -> 41.6 us  [local(): panels = lax.all_gather(coarse, 'narrow', axis=1, tiled=True)]
    broadcast_in_dim x2 -> x14, local copies, waits for them, and re-layouts: 1.18 us -> 11.3 us  [the longest x1 6.89 us: local(): g_b = jnp.broadcast_to(g[:, :, None], (cells_x + 2 * h, width, columns))]
  transfers between devices with their start and end apart: 13 -> 9, of which waited for: 7 -> 2; matrix products, arithmetic and copies ran while one was open for 1% -> 9% of each run, Pallas kernels for 0% -> 0%
where the time goes in v1:
time: 237 us; the launch traced here: 236 us
  blocking collectives  67.4 us (28%)
  waiting for transfers between devices  47.1 us (20%)
  local copies, waits for them, and re-layouts  30.2 us (13%)
  Pallas kernels  28.3 us (12%)
  starting transfers between devices  24.1 us (10%)
  other arithmetic  22.6 us (10%)
  between operations  13.8 us (6%)
  matrix products  2.89 us (1%)
    psum x1, blocking collectives, local(): squares = lax.psum(local_squares, ('wide', 'narrow'))  67.4 us
    all_gather x1, waiting for transfers between devices, local(): panels = lax.all_gather(coarse, 'narrow', axis=1, tiled=True)  41.6 us
    pallas_call x1, Pallas kernels, run_stencil(): pl.pallas_call(stencil_kernel, grid=(steps,), in_specs=[vmem] * 9, out_sp...  28.3 us
    ppermute x8, starting transfers between devices, exchange(): got = lax.ppermute(flat, ('wide', 'narrow'), shift_pairs(dw, dn, nw, nn))  24.1 us
    div x1, other arithmetic, local(): return cheb_three / jnp.sqrt(squares / total_cells + EPSILON)  8.41 us
    broadcast_in_dim x1, local copies, waits for them, and re-layouts, local(): g_b = jnp.broadcast_to(g[:, :, None], (cells_x + 2 * h, width, columns))  6.89 us
    convert_element_type x1, other arithmetic, local(): det_f = detail.astype(jnp.float32)  6.66 us
    ppermute x8, waiting for transfers between devices, exchange(): got = lax.ppermute(flat, ('wide', 'narrow'), shift_pairs(dw, dn, nw, nn))  4.78 us
  transfers between devices with their start and end apart: 9, of which 2 were waited for; matrix products, arithmetic and copies ran while one was open for 9% of the time, Pallas kernels for 0%

profile of v1, /device:TPU:1, one launch (start us, length us, event | category | flops | bytes accessed | tf_op | source)
XLA Modules:
  0.0 236.3 jit_solution(1359700884958259825)
XLA Ops:
  6.5 0.7 all-gather.2.cloned.1.call-update
  7.3 0.7 convert_element_type.7
  8.1 0.1 broadcast_in_dim.76
  8.3 0.1 broadcast_in_dim.74
  8.4 0.9 copy.50
  9.3 0.9 fusion.15
  10.6 1.0 fusion.14
  11.6 0.2 reshape.317
  11.8 0.2 reshape.313
  12.0 6.7 %convert_element_type.8 = f32[128,128,128]{2,1,0:T(8,128)} convert(bf16[128,128,128]{2,1,0:T(8,128)(2,1)} %det_ref.1) | non-fusion elementwise | flops 2097152 | bytes 12582912 | tf_op jit(solution)/shard_map/convert_element_type | solution.py:155
  18.7 0.2 slice_reduce_fusion
  18.8 0.7 fusion.16
  19.5 0.7 slice_bitcast_fusion.4
  20.3 41.6 %all-gather.2.cloned.1.call-done = bf16[32,256,128]{2,1,0:T(8,128)(2,1)} async-done(((bf16[32,32,128]{2,1,0:T(8,128)(2,1)}), bf16[32,256,128]{2,1,0:T(8,128)(2,1)}) %all-gather.2.cloned.1.call-update) | async-done | bytes 2097168 | tf_op jit(solution)/shard_map/all_gather | solution.py:142
  61.9 2.9 %fusion.1 = f32[16,16,128]{2,1,0:T(8,128)S(1)} fusion(bf16[8192,128,1]{1,0,2:T(8,128)(2,1)} %bitcast.67, s32[16,16]{1,0:T(8,128)S(1)} %copy-done.2), kind=kOutput, calls=%fused_computation.3 | convolution fusion | flops 538968064 | bytes 2229248 | tf_op jit(solution)/shard_map/dot_general | solution.py:148
  64.8 0.3 bitcast_multiply_fusion.cm_ref
  65.1 1.5 fusion.6
  66.7 0.8 concatenate.72
  67.5 1.3 collective-permute-start.2
  68.8 0.6 concatenate.70
  69.4 6.5 %collective-permute-start = (f32[1162]{0:T(1024)S(1)}, f32[1162]{0:T(1024)S(1)}, u32[]{:S(2)}, u32[]{:S(2)}) collective-permute-start(f32[1162]{0:T(1024)S(1)} %concatenate.70), channel_id=1, source_target_pairs={{0,9},{1,10},{2,11},{3,12},{4,13},{5,14},{6,15},{8,17},{9,18},{10,... | collective-permute-start | bytes 13952 | tf_op jit(solution)/shard_map/ppermute | solution.py:33
  75.9 0.7 concatenate.74
  76.6 4.5 %collective-permute-start.3 = (f32[1162]{0:T(1024)S(1)}, f32[1162]{0:T(1024)S(1)}, u32[]{:S(2)}, u32[]{:S(2)}) collective-permute-start(f32[1162]{0:T(1024)S(1)} %concatenate.74), channel_id=1, source_target_pairs={{8,1},{9,2},{10,3},{11,4},{12,5},{13,6},{14,7},{16,9},{17,10},{18,... | collective-permute-start | bytes 13952 | tf_op jit(solution)/shard_map/ppermute | solution.py:33
  81.1 0.6 concatenate.76
  81.8 1.3 collective-permute-start.5
  83.1 1.9 collective-permute-start.4
  85.0 1.0 broadcast_in_dim.77
  86.1 1.5 fusion.4
  87.6 0.1 reshape.316
  87.7 0.1 reshape.312
  87.9 3.6 %collective-permute-start.1 = (f32[49552]{0:T(1024)S(1)}, f32[49552]{0:T(1024)S(1)}, u32[]{:S(2)}, u32[]{:S(2)}) collective-permute-start(f32[49552]{0:T(1024)S(1)} %pad_maximum_fusion), channel_id=1, source_target_pairs={{0,8},{1,9},{2,10},{3,11},{4,12},{5,13},{6,14},{7,15},{8,16},{9,17... | collective-permute-start | bytes 594632 | tf_op jit(solution)/shard_map/ppermute | solution.py:33
  91.6 3.7 %collective-permute-start.6 = (f32[49552]{0:T(1024)S(1)}, f32[49552]{0:T(1024)S(1)}, u32[]{:S(2)}, u32[]{:S(2)}) collective-permute-start(f32[49552]{0:T(1024)S(1)} %pad_maximum_fusion.2), channel_id=1, source_target_pairs={{0,1},{1,2},{2,3},{3,4},{4,5},{5,6},{6,7},{8,9},{9,10},{10,11},{11... | collective-permute-start | bytes 594632 | tf_op jit(solution)/shard_map/ppermute | solution.py:33
  95.5 1.3 collective-permute-start.7
  96.9 0.1 reshape.339
  97.0 0.6 slice.299
  97.6 0.6 slice.297
  98.1 0.6 slice.302
  98.8 0.6 slice.304
  99.4 0.1 concatenate.89
  99.5 0.1 copy.53
  99.6 0.1 concatenate.87
  99.7 0.1 copy.52
  99.8 0.1 copy.46
  99.9 0.2 reshape.335
  100.3 4.8 %collective-permute-done.7 = f32[49552]{0:T(1024)S(1)} collective-permute-done((f32[49552]{0:T(1024)S(1)}, f32[49552]{0:T(1024)S(1)}, u32[]{:S(2)}, u32[]{:S(2)}) %collective-permute-start.7) | collective-permute-done | bytes 198240 | tf_op jit(solution)/shard_map/ppermute | solution.py:33
  105.1 0.1 copy.47
  105.2 2.5 %broadcast_multiply_fusion = (f32[18,18]{1,0:T(8,128)S(1)}, f32[18,18]{1,0:T(8,128)S(1)}) fusion(f32[1,1]{1,0:T(1,128)} %bitcast.28, f32[1,16]{1,0:T(1,128)S(1)} %slice_bitcast_fusion.6, f32[1,1]{1,0:T(1,128)} %bitcast.26, f32[16,1]{1,0:T(8,128)S(1)} %copy.47, f32[16,16]{1,0:T(8,128)S(1)} %convert_element_type.7, f32[16,1]{1,0:T(8,128)S(1)} %copy.46, ...), kind=kLoop, calls=%fused_computation.31 | loop fusion | flops 2916 | bytes 3888 | tf_op jit(solution)/shard_map/div | solution.py:208
  107.7 0.1 copy.55
  107.8 0.1 copy.56
  107.9 0.2 reshape.336
  108.2 0.7 gather_fusion
  109.0 0.1 fusion.10
  109.1 0.1 copy.54
  109.4 0.8 concatenate.81.right_ref
  110.2 0.9 concatenate.79.left_ref
  111.1 1.9 concatenate.77.bot_ref
  113.0 1.9 concatenate.73.top_ref
  114.9 1.4 broadcast_in_dim.70.m_ref
  116.3 1.5 broadcast_in_dim.87.h_ref
  117.8 6.9 %broadcast_in_dim.84.g_ref = f32[134,144,128]{2,1,0:T(8,128)} broadcast(f32[134,144]{1,0:T(8,128)S(1)} %copy.54), dimensions={0,1} | broadcast | bytes 9956736 | tf_op jit(solution)/shard_map/broadcast_in_dim | solution.py:207
  124.7 28.3 %shard_map.64 = (f32[128,128,128]{2,1,0:T(8,128)}, f32[8,128]{1,0:T(8,128)}) custom-call(bf16[128,128,128]{2,1,0:T(8,128)(2,1)} %det_ref.1, f32[16,128,128]{2,1,0:T(8,128)} %copy-done, f32[16,128,128]{2,1,0:T(8,128)} %broadcast_in_dim.70.m_ref, f32[3,144,128]{2,1,0:T(8,128)} %concatenate.73.top_ref, f32[3,144,128]{2,1,0:T(8,128)} %concatenate.77.bot_ref, ...), custom_call_target="tpu_custom_call" | custom-call | flops 75497472 | bytes 22462464 | tf_op jit(solution)/shard_map/pallas_call | solution.py:113
  152.9 0.7 reduce_sum.9
  153.6 67.4 %psum.7 = f32[128]{0:T(128)S(1)} all-reduce(f32[128]{0:T(128)S(1)} %reduce_sum.9), channel_id=1, replica_groups=mesh['wide'=16,'narrow'=8] {'wide','narrow'}, use_global_device_ids=true, to_apply=%region_5.6 | all-reduce | flops 128 | bytes 1024 | tf_op jit(solution)/shard_map/psum | solution.py:213
  221.1 8.4 %broadcast_divide_fusion = f32[128,128,128]{2,1,0:T(8,128)} fusion(f32[128,128,128]{2,1,0:T(8,128)} %get-tuple-element.19, f32[128]{0:T(128)S(1)} %add_sqrt_fusion), kind=kLoop, calls=%fused_computation.4 | loop fusion | flops 2097152 | bytes 16777728 | tf_op jit(solution)/shard_map/div | solution.py:214
  (71 shorter events, 1.7 us)
Async XLA Ops:
  6.5 12.1 %copy-start.1 = (s32[134]{0:T(256)S(1)}, s32[134]{0:T(256)}, u32[]{:S(2)}) copy-start(s32[134]{0:T(256)} %constant.117) | copy-start | bytes 1612
  6.5 55.3 %copy-start.2 = (s32[16,16]{1,0:T(8,128)S(1)}, s32[16,16]{1,0:T(8,128)}, u32[]{:S(2)}) copy-start(s32[16,16]{1,0:T(8,128)} %param.11) | copy-start | bytes 3076
  6.5 55.3 %all-gather.2.cloned.1.call-start = ((), (), s32[]{:S(2)}) async-start(), calls=%async_computation | async-start | bytes 2359296 | tf_op jit(solution)/shard_map/all_gather | solution.py:142
  65.1 43.1 %copy-start = (f32[16,128,128]{2,1,0:T(8,128)}, f32[16,128,128]{2,1,0:T(8,128)S(1)}, u32[]{:S(2)}) copy-start(f32[16,128,128]{2,1,0:T(8,128)S(1)} %bitcast_multiply_fusion.cm_ref) | copy-start | bytes 3145732
  67.5 20.4 %collective-permute-start.2 = (f32[1162]{0:T(1024)S(1)}, f32[1162]{0:T(1024)S(1)}, u32[]{:S(2)}, u32[]{:S(2)}) collective-permute-start(f32[1162]{0:T(1024)S(1)} %concatenate.72), channel_id=1, source_target_pairs={{1,8},{2,9},{3,10},{4,11},{5,12},{6,13},{7,14},{9,16},{10,17},{11,... | collective-permute-start | bytes 13952 | tf_op jit(solution)/shard_map/ppermute | solution.py:33
  69.4 22.2 %collective-permute-start = (f32[1162]{0:T(1024)S(1)}, f32[1162]{0:T(1024)S(1)}, u32[]{:S(2)}, u32[]{:S(2)}) collective-permute-start(f32[1162]{0:T(1024)S(1)} %concatenate.70), channel_id=1, source_target_pairs={{0,9},{1,10},{2,11},{3,12},{4,13},{5,14},{6,15},{8,17},{9,18},{10,... | collective-permute-start | bytes 13952 | tf_op jit(solution)/shard_map/ppermute | solution.py:33
  76.6 18.9 %collective-permute-start.3 = (f32[1162]{0:T(1024)S(1)}, f32[1162]{0:T(1024)S(1)}, u32[]{:S(2)}, u32[]{:S(2)}) collective-permute-start(f32[1162]{0:T(1024)S(1)} %concatenate.74), channel_id=1, source_target_pairs={{8,1},{9,2},{10,3},{11,4},{12,5},{13,6},{14,7},{16,9},{17,10},{18,... | collective-permute-start | bytes 13952 | tf_op jit(solution)/shard_map/ppermute | solution.py:33
  81.8 15.1 %collective-permute-start.5 = (f32[1162]{0:T(1024)S(1)}, f32[1162]{0:T(1024)S(1)}, u32[]{:S(2)}, u32[]{:S(2)}) collective-permute-start(f32[1162]{0:T(1024)S(1)} %concatenate.76), channel_id=1, source_target_pairs={{9,0},{10,1},{11,2},{12,3},{13,4},{14,5},{15,6},{17,8},{18,9},{19,... | collective-permute-start | bytes 13952 | tf_op jit(solution)/shard_map/ppermute | solution.py:33
  83.1 16.3 %collective-permute-start.4 = (f32[49552]{0:T(1024)S(1)}, f32[49552]{0:T(1024)S(1)}, u32[]{:S(2)}, u32[]{:S(2)}) collective-permute-start(f32[49552]{0:T(1024)S(1)} %pad_maximum_fusion.1), channel_id=1, source_target_pairs={{8,0},{9,1},{10,2},{11,3},{12,4},{13,5},{14,6},{15,7},{16,8},{17,9... | collective-permute-start | bytes 594632 | tf_op jit(solution)/shard_map/ppermute | solution.py:33
  87.9 11.7 %collective-permute-start.1 = (f32[49552]{0:T(1024)S(1)}, f32[49552]{0:T(1024)S(1)}, u32[]{:S(2)}, u32[]{:S(2)}) collective-permute-start(f32[49552]{0:T(1024)S(1)} %pad_maximum_fusion), channel_id=1, source_target_pairs={{0,8},{1,9},{2,10},{3,11},{4,12},{5,13},{6,14},{7,15},{8,16},{9,17... | collective-permute-start | bytes 594632 | tf_op jit(solution)/shard_map/ppermute | solution.py:33
  91.6 8.2 %collective-permute-start.6 = (f32[49552]{0:T(1024)S(1)}, f32[49552]{0:T(1024)S(1)}, u32[]{:S(2)}, u32[]{:S(2)}) collective-permute-start(f32[49552]{0:T(1024)S(1)} %pad_maximum_fusion.2), channel_id=1, source_target_pairs={{0,1},{1,2},{2,3},{3,4},{4,5},{5,6},{6,7},{8,9},{9,10},{10,11},{11... | collective-permute-start | bytes 594632 | tf_op jit(solution)/shard_map/ppermute | solution.py:33
  95.5 9.6 %collective-permute-start.7 = (f32[49552]{0:T(1024)S(1)}, f32[49552]{0:T(1024)S(1)}, u32[]{:S(2)}, u32[]{:S(2)}) collective-permute-start(f32[49552]{0:T(1024)S(1)} %pad_maximum_fusion.3), channel_id=1, source_target_pairs={{1,0},{2,1},{3,2},{4,3},{5,4},{6,5},{7,6},{9,8},{10,9},{11,10},{12... | collective-permute-start | bytes 594632 | tf_op jit(solution)/shard_map/ppermute | solution.py:33
Sparse Core Ops, SparseCore 0:
  9.0 52.8 all-gather.1

commit v2 on v1

--- a/solution.py
+++ b/solution.py
@@ -132,6 +132,60 @@
     )(det, cm, m, top, bot, left, right, g, h)
 
 
+def allreduce_kernel(nw, nn, x_ref, o_ref, r1, r2, s1, q1, s2, q2):
+    me_w = lax.axis_index("wide")
+    me_n = lax.axis_index("narrow")
+    mesh_id = pl.DeviceIdType.MESH
+    barrier = pltpu.get_barrier_semaphore()
+    for k in range(1, nn):
+        pl.semaphore_signal(barrier, inc=1, device_id=(me_w, (me_n + k) % nn), device_id_type=mesh_id)
+    for k in range(1, nw):
+        pl.semaphore_signal(barrier, inc=1, device_id=((me_w + k) % nw, me_n), device_id_type=mesh_id)
+    pl.semaphore_wait(barrier, nn - 1 + nw - 1)
+
+    def phase(src, slots, send, recv, me, n, peer_of):
+        copies = []
+        for k in range(1, n):
+            c = pltpu.make_async_remote_copy(
+                src_ref=src, dst_ref=slots.at[me], send_sem=send.at[k], recv_sem=recv.at[me],
+                device_id=peer_of((me + k) % n), device_id_type=mesh_id)
+            c.start()
+            copies.append(c)
+        slots[me] = src[...]
+        for k in range(1, n):
+            other = (me + k) % n
+            pltpu.make_async_remote_copy(
+                src_ref=src, dst_ref=slots.at[other], send_sem=send.at[k], recv_sem=recv.at[other],
+                device_id=peer_of(other), device_id_type=mesh_id).wait_recv()
+        for c in copies:
+            c.wait_send()
+        return jnp.sum(slots[...], axis=0)
+
+    part = phase(x_ref, r1, s1, q1, me_n, nn, lambda j: (me_w, j))
+    o_ref[...] = part
+    o_ref[...] = phase(o_ref, r2, s2, q2, me_w, nw, lambda j: (j, me_n))
+
+
+def allreduce(x, nw, nn):
+    k = x.shape[-1]
+    vmem = pl.BlockSpec(memory_space=pltpu.VMEM)
+    return pl.pallas_call(
+        functools.partial(allreduce_kernel, nw, nn),
+        in_specs=[vmem],
+        out_specs=vmem,
+        out_shape=jax.ShapeDtypeStruct((1, k), jnp.float32),
+        scratch_shapes=[
+            pltpu.VMEM((nn, 1, k), jnp.float32),
+            pltpu.VMEM((nw, 1, k), jnp.float32),
+            pltpu.SemaphoreType.DMA((nn,)),
+            pltpu.SemaphoreType.DMA((nn,)),
+            pltpu.SemaphoreType.DMA((nw,)),
+            pltpu.SemaphoreType.DMA((nw,)),
+        ],
+        compiler_params=pltpu.CompilerParams(collective_id=0, has_side_effects=True),
+    )(x)
+
+
 def local(detail, coarse, diagonal, parents, tile_mask):
     tiles_x, tiles_y = parents.shape
     cells_x, cells_y, columns = detail.shape
@@ -209,8 +263,8 @@
     h_b = jnp.broadcast_to(h_t[:, :, None], (tiles_x + 2, width, columns))
 
     cheb_three, ss = run_stencil(detail, cm0, m0, top, bot, left, right, g_b, h_b)
-    local_squares = jnp.sum(ss, axis=0)
-    squares = lax.psum(local_squares, ("wide", "narrow"))
+    local_squares = jnp.sum(ss, axis=0, keepdims=True)
+    squares = allreduce(local_squares, nw, nn)[0]
     return cheb_three / jnp.sqrt(squares / total_cells + EPSILON)
 
 

time: 237 us -> 189 us (0.80)
  blocking collectives: 67.4 us -> 0 us
  Pallas kernels: 28.3 us -> 45.7 us
    psum x1 -> x0, blocking collectives: 67.4 us -> none  [local(): squares = lax.psum(local_squares, ('wide', 'narrow'))]
    pallas_call x0 -> x1, Pallas kernels: none -> 17.4 us  [allreduce(): pl.pallas_call(functools.partial(allreduce_kernel, nw, nn), in_specs=[vme...]
  transfers between devices with their start and end apart: 9 -> 9, of which waited for: 2 -> 2; matrix products, arithmetic and copies ran while one was open for 9% -> 12% of each run, Pallas kernels for 0% -> 0%
where the time goes in v2:
time: 189 us; the launch traced here: 188 us
  waiting for transfers between devices  47 us (25%)
  Pallas kernels  45.7 us (24%)
  local copies, waits for them, and re-layouts  30.4 us (16%)
  starting transfers between devices  24.1 us (13%)
  other arithmetic  24 us (13%)
  between operations  13.8 us (7%)
  matrix products  2.89 us (2%)
    all_gather x1, waiting for transfers between devices, local(): panels = lax.all_gather(coarse, 'narrow', axis=1, tiled=True)  41.6 us
    pallas_call x1, Pallas kernels, run_stencil(): pl.pallas_call(stencil_kernel, grid=(steps,), in_specs=[vmem] * 9, out_sp...  28.3 us
    ppermute x8, starting transfers between devices, exchange(): got = lax.ppermute(flat, ('wide', 'narrow'), shift_pairs(dw, dn, nw, nn))  24.1 us
    pallas_call x1, Pallas kernels, allreduce(): pl.pallas_call(functools.partial(allreduce_kernel, nw, nn), in_specs=[vme...  17.4 us
    div x1, other arithmetic, local(): return cheb_three / jnp.sqrt(squares / total_cells + EPSILON)  8.41 us
    broadcast_in_dim x1, local copies, waits for them, and re-layouts, local(): g_b = jnp.broadcast_to(g[:, :, None], (cells_x + 2 * h, width, columns))  6.97 us
    convert_element_type x1, other arithmetic, local(): det_f = detail.astype(jnp.float32)  6.66 us
    ppermute x8, waiting for transfers between devices, exchange(): got = lax.ppermute(flat, ('wide', 'narrow'), shift_pairs(dw, dn, nw, nn))  4.68 us
  transfers between devices with their start and end apart: 9, of which 2 were waited for; matrix products, arithmetic and copies ran while one was open for 12% of the time, Pallas kernels for 0%

profile of v2, /device:TPU:1, one launch (start us, length us, event | category | flops | bytes accessed | tf_op | source)
XLA Modules:
  0.0 187.8 jit_solution(10448009126371600582)
XLA Ops:
  6.5 0.7 all-gather.2.cloned.1.call-update
  7.3 0.7 convert_element_type.7
  8.1 0.1 broadcast_in_dim.79
  8.3 0.1 broadcast_in_dim.77
  8.4 0.9 copy.50
  9.3 0.9 fusion.15
  10.6 1.0 fusion.14
  11.6 0.2 reshape.328
  11.8 0.2 reshape.324
  12.0 6.7 %convert_element_type.8 = f32[128,128,128]{2,1,0:T(8,128)} convert(bf16[128,128,128]{2,1,0:T(8,128)(2,1)} %det_ref.1) | non-fusion elementwise | flops 2097152 | bytes 12582912 | tf_op jit(solution)/shard_map/convert_element_type | solution.py:209
  18.7 0.2 slice_reduce_fusion
  18.8 0.7 fusion.16
  19.5 0.7 slice_bitcast_fusion.4
  20.3 41.6 %all-gather.2.cloned.1.call-done = bf16[32,256,128]{2,1,0:T(8,128)(2,1)} async-done(((bf16[32,32,128]{2,1,0:T(8,128)(2,1)}), bf16[32,256,128]{2,1,0:T(8,128)(2,1)}) %all-gather.2.cloned.1.call-update) | async-done | bytes 2097168 | tf_op jit(solution)/shard_map/all_gather | solution.py:196
  61.9 2.9 %fusion.1 = f32[16,16,128]{2,1,0:T(8,128)S(1)} fusion(bf16[8192,128,1]{1,0,2:T(8,128)(2,1)} %bitcast.71, s32[16,16]{1,0:T(8,128)S(1)} %copy-done.2), kind=kOutput, calls=%fused_computation.3 | convolution fusion | flops 538968064 | bytes 2229248 | tf_op jit(solution)/shard_map/dot_general | solution.py:202
  64.8 0.3 bitcast_multiply_fusion.cm_ref
  65.1 1.5 fusion.6
  66.7 0.6 concatenate.72
  67.3 1.3 collective-permute-start.2
  68.6 0.7 concatenate.70
  69.3 6.5 %collective-permute-start = (f32[1162]{0:T(1024)S(1)}, f32[1162]{0:T(1024)S(1)}, u32[]{:S(2)}, u32[]{:S(2)}) collective-permute-start(f32[1162]{0:T(1024)S(1)} %concatenate.70), channel_id=1, source_target_pairs={{0,9},{1,10},{2,11},{3,12},{4,13},{5,14},{6,15},{8,17},{9,18},{10,... | collective-permute-start | bytes 13952 | tf_op jit(solution)/shard_map/ppermute | solution.py:33
  75.8 0.8 concatenate.74
  76.6 4.5 %collective-permute-start.3 = (f32[1162]{0:T(1024)S(1)}, f32[1162]{0:T(1024)S(1)}, u32[]{:S(2)}, u32[]{:S(2)}) collective-permute-start(f32[1162]{0:T(1024)S(1)} %concatenate.74), channel_id=1, source_target_pairs={{8,1},{9,2},{10,3},{11,4},{12,5},{13,6},{14,7},{16,9},{17,10},{18,... | collective-permute-start | bytes 13952 | tf_op jit(solution)/shard_map/ppermute | solution.py:33
  81.1 0.6 concatenate.76
  81.8 1.3 collective-permute-start.5
  83.1 1.9 %collective-permute-start.4 = (f32[49552]{0:T(1024)S(1)}, f32[49552]{0:T(1024)S(1)}, u32[]{:S(2)}, u32[]{:S(2)}) collective-permute-start(f32[49552]{0:T(1024)S(1)} %pad_maximum_fusion.1), channel_id=1, source_target_pairs={{8,0},{9,1},{10,2},{11,3},{12,4},{13,5},{14,6},{15,7},{16,8},{17,9... | collective-permute-start | bytes 594632 | tf_op jit(solution)/shard_map/ppermute | solution.py:33
  85.0 1.0 broadcast_in_dim.80
  86.0 1.5 fusion.4
  87.6 0.1 reshape.327
  87.7 0.1 reshape.323
  87.9 3.6 %collective-permute-start.1 = (f32[49552]{0:T(1024)S(1)}, f32[49552]{0:T(1024)S(1)}, u32[]{:S(2)}, u32[]{:S(2)}) collective-permute-start(f32[49552]{0:T(1024)S(1)} %pad_maximum_fusion), channel_id=1, source_target_pairs={{0,8},{1,9},{2,10},{3,11},{4,12},{5,13},{6,14},{7,15},{8,16},{9,17... | collective-permute-start | bytes 594632 | tf_op jit(solution)/shard_map/ppermute | solution.py:33
  91.6 3.7 %collective-permute-start.6 = (f32[49552]{0:T(1024)S(1)}, f32[49552]{0:T(1024)S(1)}, u32[]{:S(2)}, u32[]{:S(2)}) collective-permute-start(f32[49552]{0:T(1024)S(1)} %pad_maximum_fusion.2), channel_id=1, source_target_pairs={{0,1},{1,2},{2,3},{3,4},{4,5},{5,6},{6,7},{8,9},{9,10},{10,11},{11... | collective-permute-start | bytes 594632 | tf_op jit(solution)/shard_map/ppermute | solution.py:33
  95.5 1.3 collective-permute-start.7
  96.9 0.1 reshape.350
  97.0 0.7 slice.299
  97.6 0.6 slice.297
  98.2 0.7 slice.302
  98.9 0.6 slice.304
  99.5 0.1 concatenate.89
  99.6 0.1 copy.53
  99.7 0.1 concatenate.87
  99.8 0.1 copy.52
  99.9 0.1 copy.46
  100.0 0.2 reshape.346
  100.4 4.7 %collective-permute-done.7 = f32[49552]{0:T(1024)S(1)} collective-permute-done((f32[49552]{0:T(1024)S(1)}, f32[49552]{0:T(1024)S(1)}, u32[]{:S(2)}, u32[]{:S(2)}) %collective-permute-start.7) | collective-permute-done | bytes 198240 | tf_op jit(solution)/shard_map/ppermute | solution.py:33
  105.1 0.1 copy.47
  105.2 2.7 %broadcast_multiply_fusion = (f32[18,18]{1,0:T(8,128)S(1)}, f32[18,18]{1,0:T(8,128)S(1)}) fusion(f32[1,1]{1,0:T(1,128)} %bitcast.28, f32[1,16]{1,0:T(1,128)S(1)} %slice_bitcast_fusion.6, f32[1,1]{1,0:T(1,128)} %bitcast.26, f32[16,1]{1,0:T(8,128)S(1)} %copy.47, f32[16,16]{1,0:T(8,128)S(1)} %convert_element_type.7, f32[16,1]{1,0:T(8,128)S(1)} %copy.46, ...), kind=kLoop, calls=%fused_computation.31 | loop fusion | flops 2916 | bytes 3888 | tf_op jit(solution)/shard_map/div | solution.py:262
  107.8 0.1 copy.55
  108.0 0.2 reshape.347
  108.3 0.7 gather_fusion
  109.1 0.1 fusion.10
  109.3 0.1 copy.54
  109.5 0.8 concatenate.81.right_ref
  110.3 0.8 concatenate.79.left_ref
  111.2 1.9 %concatenate.77.bot_ref = f32[3,144,128]{2,1,0:T(8,128)} concatenate(f32[3,5,128]{2,1,0:T(8,128)S(1)} %broadcast_in_dim.75, f32[3,3,128]{2,1,0:T(4,128)S(1)} %reshape.314, f32[3,128,128]{2,1,0:T(8,128)S(1)} %bitcast.64, f32[3,3,128]{2,1,0:T(4,128)S(1)} %reshape.321, f32[3,5,128]{2,1,0:T(8,128)S(1)} %broadcast_in_dim.75), dimensions={1} | concatenate | bytes 442368 | tf_op jit(solution)/shard_map/concatenate | solution.py:232
  113.1 1.9 %concatenate.73.top_ref = f32[3,144,128]{2,1,0:T(8,128)} concatenate(f32[3,5,128]{2,1,0:T(8,128)S(1)} %broadcast_in_dim.75, f32[3,3,128]{2,1,0:T(4,128)S(1)} %reshape.303, f32[3,128,128]{2,1,0:T(8,128)S(1)} %bitcast.65, f32[3,3,128]{2,1,0:T(4,128)S(1)} %reshape.310, f32[3,5,128]{2,1,0:T(8,128)S(1)} %broadcast_in_dim.75), dimensions={1} | concatenate | bytes 442368 | tf_op jit(solution)/shard_map/concatenate | solution.py:231
  115.1 1.4 broadcast_in_dim.73.m_ref
  116.4 1.5 broadcast_in_dim.90.h_ref
  117.9 7.0 %broadcast_in_dim.87.g_ref = f32[134,144,128]{2,1,0:T(8,128)} broadcast(f32[134,144]{1,0:T(8,128)S(1)} %copy.54), dimensions={0,1} | broadcast | bytes 9956736 | tf_op jit(solution)/shard_map/broadcast_in_dim | solution.py:261
  124.9 28.3 %shard_map.64 = (f32[128,128,128]{2,1,0:T(8,128)}, f32[8,128]{1,0:T(8,128)}) custom-call(bf16[128,128,128]{2,1,0:T(8,128)(2,1)} %det_ref.1, f32[16,128,128]{2,1,0:T(8,128)} %copy-done, f32[16,128,128]{2,1,0:T(8,128)} %broadcast_in_dim.73.m_ref, f32[3,144,128]{2,1,0:T(8,128)} %concatenate.73.top_ref, f32[3,144,128]{2,1,0:T(8,128)} %concatenate.77.bot_ref, ...), custom_call_target="tpu_custom_call" | custom-call | flops 75497472 | bytes 22462464 | tf_op jit(solution)/shard_map/pallas_call | solution.py:113
  153.2 1.3 reduce_sum.9
  154.4 17.4 %shard_map.65 = f32[1,128]{1,0:T(1,128)} custom-call(f32[1,128]{1,0:T(1,128)} %bitcast.70), custom_call_target="tpu_custom_call" | custom-call | tf_op jit(solution)/shard_map/pallas_call | solution.py:172
  171.9 0.7 sqrt_bitcast_fusion
  172.6 8.4 %broadcast_divide_fusion = f32[128,128,128]{2,1,0:T(8,128)} fusion(f32[128,128,128]{2,1,0:T(8,128)} %get-tuple-element.19, f32[128]{0:T(128)S(1)} %sqrt_bitcast_fusion), kind=kLoop, calls=%fused_computation.4 | loop fusion | flops 2097152 | bytes 16777728 | tf_op jit(solution)/shard_map/div | solution.py:268
  (71 shorter events, 1.7 us)
Async XLA Ops:
  6.5 12.1 %copy-start.1 = (s32[134]{0:T(256)S(1)}, s32[134]{0:T(256)}, u32[]{:S(2)}) copy-start(s32[134]{0:T(256)} %constant.117) | copy-start | bytes 1612
  6.5 55.3 %copy-start.2 = (s32[16,16]{1,0:T(8,128)S(1)}, s32[16,16]{1,0:T(8,128)}, u32[]{:S(2)}) copy-start(s32[16,16]{1,0:T(8,128)} %param.11) | copy-start | bytes 3076
  6.5 55.3 %all-gather.2.cloned.1.call-start = ((), (), s32[]{:S(2)}) async-start(), calls=%async_computation | async-start | bytes 2359296 | tf_op jit(solution)/shard_map/all_gather | solution.py:196
  65.1 43.2 %copy-start = (f32[16,128,128]{2,1,0:T(8,128)}, f32[16,128,128]{2,1,0:T(8,128)S(1)}, u32[]{:S(2)}) copy-start(f32[16,128,128]{2,1,0:T(8,128)S(1)} %bitcast_multiply_fusion.cm_ref) | copy-start | bytes 3145732
  67.3 20.5 %collective-permute-start.2 = (f32[1162]{0:T(1024)S(1)}, f32[1162]{0:T(1024)S(1)}, u32[]{:S(2)}, u32[]{:S(2)}) collective-permute-start(f32[1162]{0:T(1024)S(1)} %concatenate.72), channel_id=1, source_target_pairs={{1,8},{2,9},{3,10},{4,11},{5,12},{6,13},{7,14},{9,16},{10,17},{11,... | collective-permute-start | bytes 13952 | tf_op jit(solution)/shard_map/ppermute | solution.py:33
  69.3 22.3 %collective-permute-start = (f32[1162]{0:T(1024)S(1)}, f32[1162]{0:T(1024)S(1)}, u32[]{:S(2)}, u32[]{:S(2)}) collective-permute-start(f32[1162]{0:T(1024)S(1)} %concatenate.70), channel_id=1, source_target_pairs={{0,9},{1,10},{2,11},{3,12},{4,13},{5,14},{6,15},{8,17},{9,18},{10,... | collective-permute-start | bytes 13952 | tf_op jit(solution)/shard_map/ppermute | solution.py:33
  76.6 18.9 %collective-permute-start.3 = (f32[1162]{0:T(1024)S(1)}, f32[1162]{0:T(1024)S(1)}, u32[]{:S(2)}, u32[]{:S(2)}) collective-permute-start(f32[1162]{0:T(1024)S(1)} %concatenate.74), channel_id=1, source_target_pairs={{8,1},{9,2},{10,3},{11,4},{12,5},{13,6},{14,7},{16,9},{17,10},{18,... | collective-permute-start | bytes 13952 | tf_op jit(solution)/shard_map/ppermute | solution.py:33
  81.8 15.1 %collective-permute-start.5 = (f32[1162]{0:T(1024)S(1)}, f32[1162]{0:T(1024)S(1)}, u32[]{:S(2)}, u32[]{:S(2)}) collective-permute-start(f32[1162]{0:T(1024)S(1)} %concatenate.76), channel_id=1, source_target_pairs={{9,0},{10,1},{11,2},{12,3},{13,4},{14,5},{15,6},{17,8},{18,9},{19,... | collective-permute-start | bytes 13952 | tf_op jit(solution)/shard_map/ppermute | solution.py:33
  83.1 16.4 %collective-permute-start.4 = (f32[49552]{0:T(1024)S(1)}, f32[49552]{0:T(1024)S(1)}, u32[]{:S(2)}, u32[]{:S(2)}) collective-permute-start(f32[49552]{0:T(1024)S(1)} %pad_maximum_fusion.1), channel_id=1, source_target_pairs={{8,0},{9,1},{10,2},{11,3},{12,4},{13,5},{14,6},{15,7},{16,8},{17,9... | collective-permute-start | bytes 594632 | tf_op jit(solution)/shard_map/ppermute | solution.py:33
  87.9 11.8 %collective-permute-start.1 = (f32[49552]{0:T(1024)S(1)}, f32[49552]{0:T(1024)S(1)}, u32[]{:S(2)}, u32[]{:S(2)}) collective-permute-start(f32[49552]{0:T(1024)S(1)} %pad_maximum_fusion), channel_id=1, source_target_pairs={{0,8},{1,9},{2,10},{3,11},{4,12},{5,13},{6,14},{7,15},{8,16},{9,17... | collective-permute-start | bytes 594632 | tf_op jit(solution)/shard_map/ppermute | solution.py:33
  91.6 8.3 %collective-permute-start.6 = (f32[49552]{0:T(1024)S(1)}, f32[49552]{0:T(1024)S(1)}, u32[]{:S(2)}, u32[]{:S(2)}) collective-permute-start(f32[49552]{0:T(1024)S(1)} %pad_maximum_fusion.2), channel_id=1, source_target_pairs={{0,1},{1,2},{2,3},{3,4},{4,5},{5,6},{6,7},{8,9},{9,10},{10,11},{11... | collective-permute-start | bytes 594632 | tf_op jit(solution)/shard_map/ppermute | solution.py:33
  95.5 9.6 %collective-permute-start.7 = (f32[49552]{0:T(1024)S(1)}, f32[49552]{0:T(1024)S(1)}, u32[]{:S(2)}, u32[]{:S(2)}) collective-permute-start(f32[49552]{0:T(1024)S(1)} %pad_maximum_fusion.3), channel_id=1, source_target_pairs={{1,0},{2,1},{3,2},{4,3},{5,4},{6,5},{7,6},{9,8},{10,9},{11,10},{12... | collective-permute-start | bytes 594632 | tf_op jit(solution)/shard_map/ppermute | solution.py:33
Sparse Core Ops, SparseCore 0:
  9.0 52.8 all-gather.1

commit v3 on v2

--- a/solution.py
+++ b/solution.py
@@ -186,6 +186,86 @@
     )(x)
 
 
+def gather_kernel(nn, cols, par_ref, ct_ref, o_ref, pslots, stage, tslots, ps, pq, ts, tq):
+    me_w = lax.axis_index("wide")
+    me_n = lax.axis_index("narrow")
+    mesh_id = pl.DeviceIdType.MESH
+    barrier = pltpu.get_barrier_semaphore()
+    for k in range(1, nn):
+        pl.semaphore_signal(barrier, inc=1, device_id=(me_w, (me_n + k) % nn), device_id_type=mesh_id)
+    pl.semaphore_wait(barrier, nn - 1)
+
+    def par_copy(k, other, slot):
+        return pltpu.make_async_remote_copy(
+            src_ref=par_ref, dst_ref=pslots.at[slot], send_sem=ps.at[k], recv_sem=pq.at[slot],
+            device_id=(me_w, other), device_id_type=mesh_id)
+
+    sent = []
+    for k in range(1, nn):
+        c = par_copy(k, (me_n + k) % nn, me_n)
+        c.start()
+        sent.append(c)
+
+    local_cells = ct_ref.shape[1]
+    ncols = local_cells // cols
+
+    def contribution(par):
+        col = par % (ncols * nn)
+        idx = (par // (ncols * nn)) * ncols + col % ncols
+        idx = jnp.where(col // ncols == me_n, idx, -1)
+        rows = lax.broadcasted_iota(jnp.int32, (local_cells, par.shape[-1]), 0)
+        onehot = (rows == idx).astype(jnp.bfloat16)
+        got = jnp.dot(ct_ref[...], onehot, preferred_element_type=jnp.float32)
+        return got.astype(jnp.bfloat16)
+
+    tslots[me_n] = contribution(par_ref[...])
+    out_copies = []
+    for k in range(1, nn):
+        other = (me_n + k) % nn
+        par_copy(k, other, other).wait_recv()
+        stage[k] = contribution(pslots[other])
+        c = pltpu.make_async_remote_copy(
+            src_ref=stage.at[k], dst_ref=tslots.at[me_n], send_sem=ts.at[k], recv_sem=tq.at[me_n],
+            device_id=(me_w, other), device_id_type=mesh_id)
+        c.start()
+        out_copies.append(c)
+    for k in range(1, nn):
+        other = (me_n + k) % nn
+        pltpu.make_async_remote_copy(
+            src_ref=stage.at[k], dst_ref=tslots.at[other], send_sem=ts.at[k], recv_sem=tq.at[other],
+            device_id=(me_w, other), device_id_type=mesh_id).wait_recv()
+    for c in sent + out_copies:
+        c.wait_send()
+    total = tslots[0].astype(jnp.float32)
+    for j in range(1, nn):
+        total = total + tslots[j].astype(jnp.float32)
+    o_ref[...] = total
+
+
+def gather_tiles(parents, coarse, nn):
+    ccx, ccy, k = coarse.shape
+    par = parents.reshape(1, -1)
+    n_t = par.shape[-1]
+    ct = coarse.reshape(ccx * ccy, k).T
+    vmem = pl.BlockSpec(memory_space=pltpu.VMEM)
+    return pl.pallas_call(
+        functools.partial(gather_kernel, nn, ccx),
+        in_specs=[vmem, vmem],
+        out_specs=vmem,
+        out_shape=jax.ShapeDtypeStruct((k, n_t), jnp.float32),
+        scratch_shapes=[
+            pltpu.VMEM((nn, 1, n_t), jnp.int32),
+            pltpu.VMEM((nn, k, n_t), jnp.bfloat16),
+            pltpu.VMEM((nn, k, n_t), jnp.bfloat16),
+            pltpu.SemaphoreType.DMA((nn,)),
+            pltpu.SemaphoreType.DMA((nn,)),
+            pltpu.SemaphoreType.DMA((nn,)),
+            pltpu.SemaphoreType.DMA((nn,)),
+        ],
+        compiler_params=pltpu.CompilerParams(collective_id=1, has_side_effects=True),
+    )(par, ct)
+
+
 def local(detail, coarse, diagonal, parents, tile_mask):
     tiles_x, tiles_y = parents.shape
     cells_x, cells_y, columns = detail.shape
@@ -193,27 +273,20 @@
     total_cells = cells_x * nw * cells_y * nn
     mask_float = tile_mask.astype(jnp.float32)
 
-    panels = lax.all_gather(coarse, "narrow", axis=1, tiled=True)
-    flat_panel = panels.reshape(-1, columns)
-    parent_flat = parents.reshape(-1)
-    onehot = (
-        parent_flat[:, None] == jnp.arange(flat_panel.shape[0], dtype=jnp.int32)[None, :]
-    ).astype(jnp.bfloat16)
-    tile_values = jnp.dot(onehot, flat_panel, preferred_element_type=jnp.float32)
+    tile_values = gather_tiles(parents, coarse, nn).T
     tv = tile_values.reshape(tiles_x, tiles_y, columns)
 
     m_rows = jnp.repeat(mask_float, TS, axis=1)
     m0 = jnp.broadcast_to(m_rows[:, :, None], (tiles_x, cells_y, columns))
     cm0 = m0 * jnp.repeat(tv, TS, axis=1)
 
-    det_f = detail.astype(jnp.float32)
     h = HALO
-    c0_top = cm0[0][None] + m0[0][None] * det_f[:h]
-    c0_bot = cm0[-1][None] + m0[-1][None] * det_f[-h:]
+    c0_top = cm0[0][None] + m0[0][None] * detail[:h].astype(jnp.float32)
+    c0_bot = cm0[-1][None] + m0[-1][None] * detail[-h:].astype(jnp.float32)
     cm_rep = jnp.repeat(cm0, TS, axis=0)
     m_rep = jnp.repeat(m0, TS, axis=0)
-    c0_left = cm_rep[:, :h] + m_rep[:, :h] * det_f[:, :h]
-    c0_right = cm_rep[:, -h:] + m_rep[:, -h:] * det_f[:, -h:]
+    c0_left = cm_rep[:, :h] + m_rep[:, :h] * detail[:, :h].astype(jnp.float32)
+    c0_right = cm_rep[:, -h:] + m_rep[:, -h:] * detail[:, -h:].astype(jnp.float32)
 
     d = diagonal
     mf = mask_float

time: 189 us -> 142 us (0.75)
  waiting for transfers between devices: 47 us -> 4.26 us
  Pallas kernels: 45.7 us -> 63.6 us
  between operations: 13.8 us -> 0.44 us
  other arithmetic: 24 us -> 16.7 us
  local copies, waits for them, and re-layouts: 30.4 us -> 33.7 us
  matrix products: 2.89 us -> 0 us
    all_gather x1 -> x0, waiting for transfers between devices: 41.6 us -> none  [local(): panels = lax.all_gather(coarse, 'narrow', axis=1, tiled=True)]
    pallas_call x0 -> x1, Pallas kernels: none -> 18 us  [gather_tiles(): pl.pallas_call(functools.partial(gather_kernel, nn, ccx), in_specs=[vmem,...]
    convert_element_type x1 -> x0, other arithmetic: 6.66 us -> none  [local(): det_f = detail.astype(jnp.float32)]
    reshape x0 -> x2, local copies, waits for them, and re-layouts: none -> 3.17 us  [the longest x1 1.82 us: gather_tiles(): ct = coarse.reshape(ccx * ccy, k).T]
    dot_general x1 -> x0, matrix products: 2.89 us -> none  [local(): jnp.dot(onehot, flat_panel, preferred_element_type=jnp.float32)]
  transfers between devices with their start and end apart: 9 -> 8, of which waited for: 2 -> 1; matrix products, arithmetic and copies ran while one was open for 12% -> 8% of each run, Pallas kernels for 0% -> 0%
where the time goes in v3:
time: 142 us; the launch traced here: 141 us
  Pallas kernels  63.6 us (45%)
  local copies, waits for them, and re-layouts  33.7 us (24%)
  starting transfers between devices  22.5 us (16%)
  other arithmetic  16.7 us (12%)
  waiting for transfers between devices  4.26 us (3%)
    pallas_call x1, Pallas kernels, run_stencil(): pl.pallas_call(stencil_kernel, grid=(steps,), in_specs=[vmem] * 9, out_sp...  28.3 us
    ppermute x8, starting transfers between devices, exchange(): got = lax.ppermute(flat, ('wide', 'narrow'), shift_pairs(dw, dn, nw, nn))  22.5 us
    pallas_call x1, Pallas kernels, gather_tiles(): pl.pallas_call(functools.partial(gather_kernel, nn, ccx), in_specs=[vmem,...  18 us
    pallas_call x1, Pallas kernels, allreduce(): pl.pallas_call(functools.partial(allreduce_kernel, nw, nn), in_specs=[vme...  17.2 us
    div x1, other arithmetic, local(): return cheb_three / jnp.sqrt(squares / total_cells + EPSILON)  8.41 us
    broadcast_in_dim x1, local copies, waits for them, and re-layouts, local(): g_b = jnp.broadcast_to(g[:, :, None], (cells_x + 2 * h, width, columns))  6.89 us
    ppermute x8, waiting for transfers between devices, exchange(): got = lax.ppermute(flat, ('wide', 'narrow'), shift_pairs(dw, dn, nw, nn))  4.26 us
    concatenate x4, local copies, waits for them, and re-layouts, exchange(): flat = jnp.concatenate([p.reshape(-1) for p in pieces])  2.88 us
  transfers between devices with their start and end apart: 8, of which 1 were waited for; matrix products, arithmetic and copies ran while one was open for 8% of the time, Pallas kernels for 0%

profile of v3, /device:TPU:1, one launch (start us, length us, event | category | flops | bytes accessed | tf_op | source)
XLA Modules:
  0.0 141.2 jit_solution(968211876067420094)
XLA Ops:
  0.0 0.7 convert_element_type.15
  0.7 0.7 fusion.8
  1.4 1.4 reshape.281.par_ref
  2.9 0.1 broadcast_in_dim.78
  3.0 0.1 broadcast_in_dim.76
  3.1 0.8 fusion.7
  4.1 1.8 %copy.51 = bf16[1024,128]{0,1:T(8,128)(2,1)} copy(bf16[1024,128]{1,0:T(8,128)(2,1)} %bitcast.66) | data formatting | bytes 524288 | tf_op jit(solution)/shard_map/reshape | solution.py:249
  5.9 18.0 %shard_map.64 = f32[128,256]{1,0:T(8,128)} custom-call(s32[1,256]{1,0:T(1,128)} %reshape.281.par_ref, bf16[128,1024]{1,0:T(8,128)(2,1)} %bitcast.59), custom_call_target="tpu_custom_call" | custom-call | tf_op jit(solution)/shard_map/pallas_call | solution.py:251
  24.0 1.0 copy.52
  25.0 0.3 bitcast_multiply_fusion.cm_ref
  25.4 1.3 multiply_add_fusion
  26.7 0.7 concatenate.72
  27.4 1.3 collective-permute-start.2
  28.7 0.8 concatenate.70
  29.5 5.3 %collective-permute-start = (f32[1162]{0:T(1024)S(1)}, f32[1162]{0:T(1024)S(1)}, u32[]{:S(2)}, u32[]{:S(2)}) collective-permute-start(f32[1162]{0:T(1024)S(1)} %concatenate.70), channel_id=1, source_target_pairs={{0,9},{1,10},{2,11},{3,12},{4,13},{5,14},{6,15},{8,17},{9,18},{10,... | collective-permute-start | bytes 13952 | tf_op jit(solution)/shard_map/ppermute | solution.py:33
  34.9 0.8 concatenate.74
  35.6 4.1 %collective-permute-start.3 = (f32[1162]{0:T(1024)S(1)}, f32[1162]{0:T(1024)S(1)}, u32[]{:S(2)}, u32[]{:S(2)}) collective-permute-start(f32[1162]{0:T(1024)S(1)} %concatenate.74), channel_id=1, source_target_pairs={{8,1},{9,2},{10,3},{11,4},{12,5},{13,6},{14,7},{16,9},{17,10},{18,... | collective-permute-start | bytes 13952 | tf_op jit(solution)/shard_map/ppermute | solution.py:33
  39.8 0.7 concatenate.76
  40.5 1.3 collective-permute-start.5
  41.8 0.7 slice_bitcast_fusion.4
  42.5 1.9 %collective-permute-start.4 = (f32[49552]{0:T(1024)S(1)}, f32[49552]{0:T(1024)S(1)}, u32[]{:S(2)}, u32[]{:S(2)}) collective-permute-start(f32[49552]{0:T(1024)S(1)} %pad_maximum_fusion.1), channel_id=1, source_target_pairs={{8,0},{9,1},{10,2},{11,3},{12,4},{13,5},{14,6},{15,7},{16,8},{17,9... | collective-permute-start | bytes 594632 | tf_op jit(solution)/shard_map/ppermute | solution.py:33
  44.5 0.2 slice_reduce_fusion
  44.6 1.0 fusion.6
  45.7 0.2 reshape.313
  45.9 0.2 reshape.309
  46.1 1.1 broadcast_in_dim.79
  47.3 1.4 slice_add_fusion
  48.7 0.1 reshape.312
  48.8 0.1 reshape.308
  49.0 0.1 copy.58
  49.1 3.6 %collective-permute-start.1 = (f32[49552]{0:T(1024)S(1)}, f32[49552]{0:T(1024)S(1)}, u32[]{:S(2)}, u32[]{:S(2)}) collective-permute-start(f32[49552]{0:T(1024)S(1)} %pad_maximum_fusion), channel_id=1, source_target_pairs={{0,8},{1,9},{2,10},{3,11},{4,12},{5,13},{6,14},{7,15},{8,16},{9,17... | collective-permute-start | bytes 594632 | tf_op jit(solution)/shard_map/ppermute | solution.py:33
  52.9 3.7 %collective-permute-start.6 = (f32[49552]{0:T(1024)S(1)}, f32[49552]{0:T(1024)S(1)}, u32[]{:S(2)}, u32[]{:S(2)}) collective-permute-start(f32[49552]{0:T(1024)S(1)} %pad_maximum_fusion.2), channel_id=1, source_target_pairs={{0,1},{1,2},{2,3},{3,4},{4,5},{5,6},{6,7},{8,9},{9,10},{10,11},{11... | collective-permute-start | bytes 594632 | tf_op jit(solution)/shard_map/ppermute | solution.py:33
  56.7 1.3 collective-permute-start.7
  58.1 0.1 reshape.335
  58.2 0.6 slice.295
  58.8 0.6 slice.293
  59.3 0.6 slice.298
  60.0 0.6 slice.300
  60.6 0.1 concatenate.89
  60.7 0.1 copy.61
  60.8 0.1 concatenate.87
  60.9 0.1 copy.60
  61.0 0.1 copy.54
  61.1 0.2 reshape.331
  61.5 4.2 %collective-permute-done.7 = f32[49552]{0:T(1024)S(1)} collective-permute-done((f32[49552]{0:T(1024)S(1)}, f32[49552]{0:T(1024)S(1)}, u32[]{:S(2)}, u32[]{:S(2)}) %collective-permute-start.7) | collective-permute-done | bytes 198240 | tf_op jit(solution)/shard_map/ppermute | solution.py:33
  65.8 0.1 copy.55
  65.9 2.5 %broadcast_multiply_fusion = (f32[18,18]{1,0:T(8,128)S(1)}, f32[18,18]{1,0:T(8,128)S(1)}) fusion(f32[1,1]{1,0:T(1,128)} %bitcast.29, f32[1,16]{1,0:T(1,128)S(1)} %slice_bitcast_fusion.6, f32[1,1]{1,0:T(1,128)} %bitcast.27, f32[16,1]{1,0:T(8,128)S(1)} %copy.55, f32[16,16]{1,0:T(8,128)S(1)} %convert_element_type.15, f32[16,1]{1,0:T(8,128)S(1)} %copy.54, ...), kind=kLoop, calls=%fused_computation.23 | loop fusion | flops 2916 | bytes 3888 | tf_op jit(solution)/shard_map/div | solution.py:335
  68.4 0.1 copy.63
  68.6 0.2 reshape.332
  68.9 0.7 gather_fusion
  69.7 0.1 fusion.2
  69.8 0.1 copy.62
  70.1 0.8 concatenate.81.right_ref
  70.9 0.9 concatenate.79.left_ref
  71.8 1.9 %concatenate.77.bot_ref = f32[3,144,128]{2,1,0:T(8,128)} concatenate(f32[3,5,128]{2,1,0:T(8,128)S(1)} %broadcast_in_dim.74, f32[3,3,128]{2,1,0:T(4,128)S(1)} %reshape.299, f32[3,128,128]{2,1,0:T(8,128)S(1)} %bitcast.62, f32[3,3,128]{2,1,0:T(4,128)S(1)} %reshape.306, f32[3,5,128]{2,1,0:T(8,128)S(1)} %broadcast_in_dim.74), dimensions={1} | concatenate | bytes 442368 | tf_op jit(solution)/shard_map/concatenate | solution.py:305
  73.7 1.9 %concatenate.73.top_ref = f32[3,144,128]{2,1,0:T(8,128)} concatenate(f32[3,5,128]{2,1,0:T(8,128)S(1)} %broadcast_in_dim.74, f32[3,3,128]{2,1,0:T(4,128)S(1)} %reshape.288, f32[3,128,128]{2,1,0:T(8,128)S(1)} %bitcast.63, f32[3,3,128]{2,1,0:T(4,128)S(1)} %reshape.295, f32[3,5,128]{2,1,0:T(8,128)S(1)} %broadcast_in_dim.74), dimensions={1} | concatenate | bytes 442368 | tf_op jit(solution)/shard_map/concatenate | solution.py:304
  75.6 1.4 broadcast_in_dim.72.m_ref
  77.0 1.5 %broadcast_in_dim.89.h_ref = f32[18,144,128]{2,1,0:T(8,128)} broadcast(f32[18,144]{1,0:T(8,128)S(1)} %copy.64), dimensions={0,1} | broadcast | bytes 1337472 | tf_op jit(solution)/shard_map/broadcast_in_dim | solution.py:336
  78.5 6.9 %broadcast_in_dim.86.g_ref = f32[134,144,128]{2,1,0:T(8,128)} broadcast(f32[134,144]{1,0:T(8,128)S(1)} %copy.62), dimensions={0,1} | broadcast | bytes 9956736 | tf_op jit(solution)/shard_map/broadcast_in_dim | solution.py:334
  85.4 28.3 %shard_map.65 = (f32[128,128,128]{2,1,0:T(8,128)}, f32[8,128]{1,0:T(8,128)}) custom-call(bf16[128,128,128]{2,1,0:T(8,128)(2,1)} %det_ref.1, f32[16,128,128]{2,1,0:T(8,128)} %copy-done, f32[16,128,128]{2,1,0:T(8,128)} %broadcast_in_dim.72.m_ref, f32[3,144,128]{2,1,0:T(8,128)} %concatenate.73.top_ref, f32[3,144,128]{2,1,0:T(8,128)} %concatenate.77.bot_ref, ...), custom_call_target="tpu_custom_call" | custom-call | flops 75497472 | bytes 22462464 | tf_op jit(solution)/shard_map/pallas_call | solution.py:113
  113.6 1.3 reduce_sum.9
  114.9 17.2 %shard_map.66 = f32[1,128]{1,0:T(1,128)} custom-call(f32[1,128]{1,0:T(1,128)} %bitcast.71), custom_call_target="tpu_custom_call" | custom-call | tf_op jit(solution)/shard_map/pallas_call | solution.py:172
  132.2 0.6 sqrt_bitcast_fusion
  132.8 8.4 %broadcast_divide_fusion = f32[128,128,128]{2,1,0:T(8,128)} fusion(f32[128,128,128]{2,1,0:T(8,128)} %get-tuple-element.19, f32[128]{0:T(128)S(1)} %sqrt_bitcast_fusion), kind=kLoop, calls=%fused_computation.1 | loop fusion | flops 2097152 | bytes 16777728 | tf_op jit(solution)/shard_map/div | solution.py:341
  (70 shorter events, 1.7 us)
Async XLA Ops:
  24.0 25.0 %copy-start.2 = (s32[134]{0:T(256)S(1)}, s32[134]{0:T(256)}, u32[]{:S(2)}) copy-start(s32[134]{0:T(256)} %constant.117) | copy-start | bytes 1612
  24.0 25.0 %copy-start.1 = (f32[128,128]{1,0:T(8,128)S(1)}, f32[128,128]{1,0:T(8,128)}, u32[]{:S(2)}) copy-start(f32[128,128]{1,0:T(8,128)} %param.10) | copy-start | bytes 196612
  25.4 36.2 %copy-start = (f32[16,128,128]{2,1,0:T(8,128)}, f32[16,128,128]{2,1,0:T(8,128)S(1)}, u32[]{:S(2)}) copy-start(f32[16,128,128]{2,1,0:T(8,128)S(1)} %bitcast_multiply_fusion.cm_ref) | copy-start | bytes 3145732
  27.4 21.7 %collective-permute-start.2 = (f32[1162]{0:T(1024)S(1)}, f32[1162]{0:T(1024)S(1)}, u32[]{:S(2)}, u32[]{:S(2)}) collective-permute-start(f32[1162]{0:T(1024)S(1)} %concatenate.72), channel_id=1, source_target_pairs={{1,8},{2,9},{3,10},{4,11},{5,12},{6,13},{7,14},{9,16},{10,17},{11,... | collective-permute-start | bytes 13952 | tf_op jit(solution)/shard_map/ppermute | solution.py:33
  29.5 23.4 %collective-permute-start = (f32[1162]{0:T(1024)S(1)}, f32[1162]{0:T(1024)S(1)}, u32[]{:S(2)}, u32[]{:S(2)}) collective-permute-start(f32[1162]{0:T(1024)S(1)} %concatenate.70), channel_id=1, source_target_pairs={{0,9},{1,10},{2,11},{3,12},{4,13},{5,14},{6,15},{8,17},{9,18},{10,... | collective-permute-start | bytes 13952 | tf_op jit(solution)/shard_map/ppermute | solution.py:33
  35.6 21.1 %collective-permute-start.3 = (f32[1162]{0:T(1024)S(1)}, f32[1162]{0:T(1024)S(1)}, u32[]{:S(2)}, u32[]{:S(2)}) collective-permute-start(f32[1162]{0:T(1024)S(1)} %concatenate.74), channel_id=1, source_target_pairs={{8,1},{9,2},{10,3},{11,4},{12,5},{13,6},{14,7},{16,9},{17,10},{18,... | collective-permute-start | bytes 13952 | tf_op jit(solution)/shard_map/ppermute | solution.py:33
  40.5 17.6 %collective-permute-start.5 = (f32[1162]{0:T(1024)S(1)}, f32[1162]{0:T(1024)S(1)}, u32[]{:S(2)}, u32[]{:S(2)}) collective-permute-start(f32[1162]{0:T(1024)S(1)} %concatenate.76), channel_id=1, source_target_pairs={{9,0},{10,1},{11,2},{12,3},{13,4},{14,5},{15,6},{17,8},{18,9},{19,... | collective-permute-start | bytes 13952 | tf_op jit(solution)/shard_map/ppermute | solution.py:33
  42.5 18.0 %collective-permute-start.4 = (f32[49552]{0:T(1024)S(1)}, f32[49552]{0:T(1024)S(1)}, u32[]{:S(2)}, u32[]{:S(2)}) collective-permute-start(f32[49552]{0:T(1024)S(1)} %pad_maximum_fusion.1), channel_id=1, source_target_pairs={{8,0},{9,1},{10,2},{11,3},{12,4},{13,5},{14,6},{15,7},{16,8},{17,9... | collective-permute-start | bytes 594632 | tf_op jit(solution)/shard_map/ppermute | solution.py:33
  49.1 11.7 %collective-permute-start.1 = (f32[49552]{0:T(1024)S(1)}, f32[49552]{0:T(1024)S(1)}, u32[]{:S(2)}, u32[]{:S(2)}) collective-permute-start(f32[49552]{0:T(1024)S(1)} %pad_maximum_fusion), channel_id=1, source_target_pairs={{0,8},{1,9},{2,10},{3,11},{4,12},{5,13},{6,14},{7,15},{8,16},{9,17... | collective-permute-start | bytes 594632 | tf_op jit(solution)/shard_map/ppermute | solution.py:33
  52.9 8.2 %collective-permute-start.6 = (f32[49552]{0:T(1024)S(1)}, f32[49552]{0:T(1024)S(1)}, u32[]{:S(2)}, u32[]{:S(2)}) collective-permute-start(f32[49552]{0:T(1024)S(1)} %pad_maximum_fusion.2), channel_id=1, source_target_pairs={{0,1},{1,2},{2,3},{3,4},{4,5},{5,6},{6,7},{8,9},{9,10},{10,11},{11... | collective-permute-start | bytes 594632 | tf_op jit(solution)/shard_map/ppermute | solution.py:33
  56.7 9.1 %collective-permute-start.7 = (f32[49552]{0:T(1024)S(1)}, f32[49552]{0:T(1024)S(1)}, u32[]{:S(2)}, u32[]{:S(2)}) collective-permute-start(f32[49552]{0:T(1024)S(1)} %pad_maximum_fusion.3), channel_id=1, source_target_pairs={{1,0},{2,1},{3,2},{4,3},{5,4},{6,5},{7,6},{9,8},{10,9},{11,10},{12... | collective-permute-start | bytes 594632 | tf_op jit(solution)/shard_map/ppermute | solution.py:33

commit v4 on v3

--- a/solution.py
+++ b/solution.py
@@ -38,8 +38,8 @@
     return out
 
 
-def stencil_kernel(det_ref, cm_ref, m_ref, top_ref, bot_ref, left_ref, right_ref, g_ref, h_ref,
-                   out_ref, ss_ref, r0, r1, r2):
+def stencil_kernel(det_ref, cm_ref, m_ref, top_ref, bot_ref, left_ref, right_ref,
+                   tl_ref, tr_ref, bl_ref, br_ref, g_ref, h_ref, out_ref, ss_ref, r0, r1, r2):
     i = pl.program_id(0)
     cx = det_ref.shape[0]
     width = g_ref.shape[1]
@@ -48,22 +48,33 @@
 
     def c0_row(x):
         s = x % RING
+        zero = jnp.zeros((width, det_ref.shape[2]), jnp.float32)
 
         @pl.when(x < HALO)
         def _():
-            r0[s] = top_ref[jnp.minimum(x, HALO - 1)]
+            j = jnp.minimum(x, HALO - 1)
+            r0[s] = zero
+            r0[s, LPAD - HALO:LPAD] = tl_ref[j]
+            r0[s, LPAD:LPAD + cy] = top_ref[j]
+            r0[s, LPAD + cy:LPAD + cy + HALO] = tr_ref[j]
 
         @pl.when(x >= HALO + cx)
         def _():
-            r0[s] = bot_ref[jnp.maximum(x - HALO - cx, 0)]
+            j = jnp.clip(x - HALO - cx, 0, HALO - 1)
+            r0[s] = zero
+            r0[s, LPAD - HALO:LPAD] = bl_ref[j]
+            r0[s, LPAD:LPAD + cy] = bot_ref[j]
+            r0[s, LPAD + cy:LPAD + cy + HALO] = br_ref[j]
 
         @pl.when(jnp.logical_and(x >= HALO, x < HALO + cx))
         def _():
             b = jnp.clip(x - HALO, 0, cx - 1)
             t = b // TS
-            r0[s, 0:LPAD] = left_ref[b]
+            r0[s, 0:LPAD] = zero[0:LPAD]
+            r0[s, LPAD - HALO:LPAD] = left_ref[b]
             r0[s, LPAD:LPAD + cy] = cm_ref[t] + m_ref[t] * det_ref[b].astype(jnp.float32)
-            r0[s, LPAD + cy:width] = right_ref[b]
+            r0[s, LPAD + cy:width] = zero[0:width - LPAD - cy]
+            r0[s, LPAD + cy:LPAD + cy + HALO] = right_ref[b]
 
     def apply_b(src, x):
         v = src[x % RING]
@@ -104,7 +115,7 @@
     rows(c3_row, base + HALO, ROWS)
 
 
-def run_stencil(det, cm, m, top, bot, left, right, g, h):
+def run_stencil(det, cm, m, halos, g, h):
     cx, cy, k = det.shape
     width = g.shape[1]
     steps = cx // ROWS
@@ -113,7 +124,7 @@
     return pl.pallas_call(
         stencil_kernel,
         grid=(steps,),
-        in_specs=[vmem] * 9,
+        in_specs=[vmem] * 13,
         out_specs=[
             pl.BlockSpec((ROWS, cy, k), lambda i: (i, 0, 0)),
             pl.BlockSpec((8, k), lambda i: (0, 0)),
@@ -129,7 +140,7 @@
         cost_estimate=pl.CostEstimate(
             flops=ops, transcendentals=0, bytes_accessed=det.size * 2 + cx * cy * k * 4 + g.size * 4
         ),
-    )(det, cm, m, top, bot, left, right, g, h)
+    )(det, cm, m, *halos, g, h)
 
 
 def allreduce_kernel(nw, nn, x_ref, o_ref, r1, r2, s1, q1, s2, q2):
@@ -266,6 +277,82 @@
     )(par, ct)
 
 
+DIRS = ((1, 0), (-1, 0), (0, 1), (0, -1), (1, 1), (1, -1), (-1, 1), (-1, -1))
+
+
+def halo_kernel(nw, nn, *refs):
+    nd = len(DIRS)
+    ins, outs = refs[:2 * nd], refs[2 * nd:4 * nd]
+    send, recv = refs[4 * nd], refs[4 * nd + 1]
+    me_w = lax.axis_index("wide")
+    me_n = lax.axis_index("narrow")
+    mesh_id = pl.DeviceIdType.MESH
+
+    def inside(dw, dn, sign):
+        w, n = me_w + sign * dw, me_n + sign * dn
+        return jnp.logical_and(jnp.logical_and(w >= 0, w < nw), jnp.logical_and(n >= 0, n < nn))
+
+    def clamp(v, n):
+        return jnp.clip(v, 0, n - 1)
+
+    barrier = pltpu.get_barrier_semaphore()
+    count = 0
+    for dw, dn in DIRS:
+        ok = inside(dw, dn, 1)
+
+        @pl.when(ok)
+        def _():
+            pl.semaphore_signal(barrier, inc=1, device_id=(clamp(me_w + dw, nw), clamp(me_n + dn, nn)),
+                                device_id_type=mesh_id)
+        count = count + ok.astype(jnp.int32)
+    pl.semaphore_wait(barrier, count)
+
+    def copy(d, p, sign):
+        dw, dn = DIRS[d]
+        j = 2 * d + p
+        return pltpu.make_async_remote_copy(
+            src_ref=ins[j], dst_ref=outs[j], send_sem=send.at[j], recv_sem=recv.at[j],
+            device_id=(clamp(me_w + sign * dw, nw), clamp(me_n + sign * dn, nn)), device_id_type=mesh_id)
+
+    for d, (dw, dn) in enumerate(DIRS):
+        @pl.when(inside(dw, dn, 1))
+        def _():
+            for p in range(2):
+                copy(d, p, 1).start()
+
+    for d, (dw, dn) in enumerate(DIRS):
+        src_ok = inside(dw, dn, -1)
+
+        @pl.when(src_ok)
+        def _():
+            for p in range(2):
+                copy(d, p, -1).wait_recv()
+
+        @pl.when(jnp.logical_not(src_ok))
+        def _():
+            for p in range(2):
+                outs[2 * d + p][...] = jnp.zeros(outs[2 * d + p].shape, outs[2 * d + p].dtype)
+
+    for d, (dw, dn) in enumerate(DIRS):
+        @pl.when(inside(dw, dn, 1))
+        def _():
+            for p in range(2):
+                copy(d, p, 1).wait_send()
+
+
+def exchange_halos(pieces, nw, nn):
+    vmem = pl.BlockSpec(memory_space=pltpu.VMEM)
+    n = len(pieces)
+    return pl.pallas_call(
+        functools.partial(halo_kernel, nw, nn),
+        in_specs=[vmem] * n,
+        out_specs=[vmem] * n,
+        out_shape=[jax.ShapeDtypeStruct(p.shape, p.dtype) for p in pieces],
+        scratch_shapes=[pltpu.SemaphoreType.DMA((n,)), pltpu.SemaphoreType.DMA((n,))],
+        compiler_params=pltpu.CompilerParams(collective_id=2, has_side_effects=True),
+    )(*pieces)
+
+
 def local(detail, coarse, diagonal, parents, tile_mask):
     tiles_x, tiles_y = parents.shape
     cells_x, cells_y, columns = detail.shape
@@ -288,54 +375,54 @@
     c0_left = cm_rep[:, :h] + m_rep[:, :h] * detail[:, :h].astype(jnp.float32)
     c0_right = cm_rep[:, -h:] + m_rep[:, -h:] * detail[:, -h:].astype(jnp.float32)
 
-    d = diagonal
-    mf = mask_float
-    top_c, top_d, top_m = exchange([c0_bot, d[-h:], mf[-1:]], 1, 0, nw, nn)
-    bot_c, bot_d, bot_m = exchange([c0_top, d[:h], mf[:1]], -1, 0, nw, nn)
-    lft_c, lft_d, lft_m = exchange([c0_right, d[:, -h:], mf[:, -1:]], 0, 1, nw, nn)
-    rgt_c, rgt_d, rgt_m = exchange([c0_left, d[:, :h], mf[:, :1]], 0, -1, nw, nn)
-    tl_c, tl_d, tl_m = exchange([c0_bot[:, -h:], d[-h:, -h:], mf[-1:, -1:]], 1, 1, nw, nn)
-    tr_c, tr_d, tr_m = exchange([c0_bot[:, :h], d[-h:, :h], mf[-1:, :1]], 1, -1, nw, nn)
-    bl_c, bl_d, bl_m = exchange([c0_top[:, -h:], d[:h, -h:], mf[:1, -1:]], -1, 1, nw, nn)
-    br_c, br_d, br_m = exchange([c0_top[:, :h], d[:h, :h], mf[:1, :1]], -1, -1, nw, nn)
+    cell_mask = jnp.repeat(jnp.repeat(mask_float, TS, axis=0), TS, axis=1)
+    g_own = (cell_mask * (4.0 + diagonal) - CENTER) / HALF_WIDTH
+    h_own = cell_mask / HALF_WIDTH
+    gh = jnp.stack([g_own, h_own])
+
+    def edge(a, dw, dn, rows_axis, cols_axis):
+        idx = [slice(None)] * a.ndim
+        if dw == 1:
+            idx[rows_axis] = slice(a.shape[rows_axis] - h, None)
+        elif dw == -1:
+            idx[rows_axis] = slice(0, h)
+        if dn == 1:
+            idx[cols_axis] = slice(a.shape[cols_axis] - h, None)
+        elif dn == -1:
+            idx[cols_axis] = slice(0, h)
+        return a[tuple(idx)]
+
+    c0_pieces = {
+        (1, 0): c0_bot, (-1, 0): c0_top, (0, 1): c0_right, (0, -1): c0_left,
+        (1, 1): c0_bot[:, -h:], (1, -1): c0_bot[:, :h], (-1, 1): c0_top[:, -h:], (-1, -1): c0_top[:, :h],
+    }
+    pieces = []
+    for dw, dn in DIRS:
+        pieces.append(c0_pieces[(dw, dn)])
+        pieces.append(edge(gh, dw, dn, 1, 2))
+    got = exchange_halos(pieces, nw, nn)
+    hc = {dirn: got[2 * k] for k, dirn in enumerate(DIRS)}
+    hg = {dirn: got[2 * k + 1] for k, dirn in enumerate(DIRS)}
+    halos = [hc[(1, 0)], hc[(-1, 0)], hc[(0, 1)], hc[(0, -1)],
+             hc[(1, 1)], hc[(1, -1)], hc[(-1, 1)], hc[(-1, -1)]]
 
     rpad = LPAD - h
-    z3 = jnp.zeros((h, rpad, columns), jnp.float32)
-    top = jnp.concatenate([z3, tl_c, top_c, tr_c, z3], axis=1)
-    bot = jnp.concatenate([z3, bl_c, bot_c, br_c, z3], axis=1)
-    zc = jnp.zeros((cells_x, rpad, columns), jnp.float32)
-    left = jnp.concatenate([zc, lft_c], axis=1)
-    right = jnp.concatenate([rgt_c, zc], axis=1)
-
-    zd3 = jnp.zeros((h, rpad), jnp.float32)
-    zdc = jnp.zeros((cells_x, rpad), jnp.float32)
-    diag_ext = jnp.concatenate(
+    z3 = jnp.zeros((2, h, rpad), jnp.float32)
+    zc = jnp.zeros((2, cells_x, rpad), jnp.float32)
+    gh_ext = jnp.concatenate(
         [
-            jnp.concatenate([zd3, tl_d, top_d, tr_d, zd3], axis=1),
-            jnp.concatenate([zdc, lft_d, d, rgt_d, zdc], axis=1),
-            jnp.concatenate([zd3, bl_d, bot_d, br_d, zd3], axis=1),
+            jnp.concatenate([z3, hg[(1, 1)], hg[(1, 0)], hg[(1, -1)], z3], axis=2),
+            jnp.concatenate([zc, hg[(0, 1)], gh, hg[(0, -1)], zc], axis=2),
+            jnp.concatenate([z3, hg[(-1, 1)], hg[(-1, 0)], hg[(-1, -1)], z3], axis=2),
         ],
-        axis=0,
+        axis=1,
     )
-    mask_ext = jnp.concatenate(
-        [
-            jnp.concatenate([tl_m, top_m, tr_m], axis=1),
-            jnp.concatenate([lft_m, mf, rgt_m], axis=1),
-            jnp.concatenate([bl_m, bot_m, br_m], axis=1),
-        ],
-        axis=0,
-    )
-    reps = [h] + [TS] * tiles_x + [h]
-    cell_mask_ext = jnp.repeat(
-        jnp.repeat(mask_ext, jnp.array(reps), axis=0, total_repeat_length=cells_x + 2 * h), TS, axis=1
-    )
-    g = (cell_mask_ext * (4.0 + diag_ext) - CENTER) / HALF_WIDTH
     width = cells_y + 2 * LPAD
-    g_b = jnp.broadcast_to(g[:, :, None], (cells_x + 2 * h, width, columns))
-    h_t = jnp.repeat(mask_ext / HALF_WIDTH, TS, axis=1)
-    h_b = jnp.broadcast_to(h_t[:, :, None], (tiles_x + 2, width, columns))
-
-    cheb_three, ss = run_stencil(detail, cm0, m0, top, bot, left, right, g_b, h_b)
+    g_b = jnp.broadcast_to(gh_ext[0][:, :, None], (cells_x + 2 * h, width, columns))
+    h_rows = gh_ext[1][jnp.array([0] + [h + TS * t for t in range(tiles_x)] + [h + cells_x])]
+    h_b = jnp.broadcast_to(h_rows[:, :, None], (tiles_x + 2, width, columns))
+
+    cheb_three, ss = run_stencil(detail, cm0, m0, halos, g_b, h_b)
     local_squares = jnp.sum(ss, axis=0, keepdims=True)
     squares = allreduce(local_squares, nw, nn)[0]
     return cheb_three / jnp.sqrt(squares / total_cells + EPSILON)

time: 142 us -> 124 us (0.87)
  starting transfers between devices: 22.5 us -> 0 us
  Pallas kernels: 63.6 us -> 84.6 us
  local copies, waits for them, and re-layouts: 33.7 us -> 19.9 us
  waiting for transfers between devices: 4.26 us -> 0 us
  other arithmetic: 16.7 us -> 18.4 us
    ppermute x8 -> x0, starting transfers between devices: 22.5 us -> none  [exchange(): got = lax.ppermute(flat, ('wide', 'narrow'), shift_pairs(dw, dn, nw, nn))]
    pallas_call x1 -> x2, Pallas kernels: 28.3 us -> 50.5 us  [the longest x1 28.7 us: run_stencil(): pl.pallas_call(stencil_kernel, grid=(steps,), in_specs=[vmem] * 13, out_s...]
    concatenate x13 -> x3, local copies, waits for them, and re-layouts: 8.87 us -> 2.77 us  [the longest x1 1.2 us: local(): jnp.concatenate([zc, hg[0, 1], gh, hg[0, -1], zc], axis=2)]
    slice x18 -> x0, local copies, waits for them, and re-layouts: 5.16 us -> none  [the longest x14 2.48 us: exchange(): out.append(got[at:at + p.size].reshape(p.shape))]
    ppermute x8 -> x0, waiting for transfers between devices: 4.26 us -> none  [exchange(): got = lax.ppermute(flat, ('wide', 'narrow'), shift_pairs(dw, dn, nw, nn))]
    another operation x0 -> x5, other arithmetic: none -> 2.93 us  [local(): gh = jnp.stack([g_own, h_own])]
    reshape x35 -> x4, local copies, waits for them, and re-layouts: 2.92 us -> 0.2 us  [local(): cell_mask = jnp.repeat(jnp.repeat(mask_float, TS, axis=0), TS, axis=1)]
    div x2 -> x1, other arithmetic: 2.67 us -> 0.01 us  [local(): h_own = cell_mask / HALF_WIDTH]
  transfers between devices with their start and end apart: 8 -> 0, of which waited for: 1 -> 0; matrix products, arithmetic and copies ran while one was open for 8% -> 0% of each run, Pallas kernels for 0% -> 0%
where the time goes in v4:
time: 124 us; the launch traced here: 123 us
  Pallas kernels  84.6 us (68%)
  local copies, waits for them, and re-layouts  19.9 us (16%)
  other arithmetic  18.4 us (15%)
    pallas_call x1, Pallas kernels, run_stencil(): pl.pallas_call(stencil_kernel, grid=(steps,), in_specs=[vmem] * 13, out_s...  28.7 us
    pallas_call x1, Pallas kernels, exchange_halos(): pl.pallas_call(functools.partial(halo_kernel, nw, nn), in_specs=[vmem] *...  21.8 us
    pallas_call x1, Pallas kernels, gather_tiles(): pl.pallas_call(functools.partial(gather_kernel, nn, ccx), in_specs=[vmem,...  18 us
    pallas_call x1, Pallas kernels, allreduce(): pl.pallas_call(functools.partial(allreduce_kernel, nw, nn), in_specs=[vme...  16 us
    div x1, other arithmetic, local(): return cheb_three / jnp.sqrt(squares / total_cells + EPSILON)  8.41 us
    broadcast_in_dim x1, local copies, waits for them, and re-layouts, local(): jnp.broadcast_to(gh_ext[0][:, :, None], (cells_x + 2 * h, width, columns))  6.9 us
    another operation x5, other arithmetic, local(): gh = jnp.stack([g_own, h_own])  2.93 us

profile of v4, /device:TPU:1, one launch (start us, length us, event | category | flops | bytes accessed | tf_op | source)
XLA Modules:
  0.0 123.0 jit_solution(8731725823801773414)
XLA Ops:
  0.0 1.4 %reshape.62.par_ref = s32[1,256]{1,0:T(1,128)} reshape(s32[16,16]{1,0:T(8,128)} %param.9) | data formatting | bytes 2048 | tf_op jit(solution)/shard_map/reshape | solution.py:258
  1.4 0.7 pad_clamp_fusion
  2.0 0.7 convert_element_type.15
  2.7 0.1 broadcast_in_dim.64
  2.8 0.1 broadcast_in_dim.65
  2.9 0.1 broadcast_in_dim.59
  3.0 0.1 broadcast_in_dim.60
  3.1 0.1 copy.17
  3.1 0.1 copy.18
  3.2 0.1 copy.21
  3.3 0.1 copy.22
  3.4 0.9 multiply_bitcast_fusion
  4.3 0.1 copy.23
  4.3 0.1 copy.24
  4.5 0.6 fusion.3
  5.1 0.7 fusion.7
  5.8 0.1 fusion.10
  5.9 0.8 fusion.1
  6.6 1.8 %copy.19 = bf16[1024,128]{0,1:T(8,128)(2,1)} copy(bf16[1024,128]{1,0:T(8,128)(2,1)} %bitcast.39) | data formatting | bytes 524288 | tf_op jit(solution)/shard_map/reshape | solution.py:260
  8.4 18.0 %shard_map.64 = f32[128,256]{1,0:T(8,128)} custom-call(s32[1,256]{1,0:T(1,128)} %reshape.62.par_ref, bf16[128,1024]{1,0:T(8,128)(2,1)} %bitcast.36), custom_call_target="tpu_custom_call" | custom-call | tf_op jit(solution)/shard_map/pallas_call | solution.py:262
  26.5 1.0 copy.20
  27.5 0.3 bitcast_multiply_fusion.cm_ref
  27.8 0.0 copy-start
  27.8 1.3 %multiply_add_fusion = (f32[3,128,128]{2,1,0:T(8,128)S(1)}, f32[3,128,128]{2,1,0:T(8,128)S(1)}) fusion(bf16[128,128,128]{2,1,0:T(8,128)(2,1)} %det_ref.1, f32[128]{0:T(128)S(1)} %broadcast_in_dim.65, f32[128,128]{1,0:T(8,128)S(1)} %get-tuple-element.45, f32[128]{0:T(128)S(1)} %broadcast_in_dim.60, f32[128,128]{1,0:T(8,128)S(1)} %get-tuple-element.46), kind=kLoop, calls=%fused_computation.23 | loop fusion | flops 294912 | bytes 721920 | tf_op jit(solution)/shard_map/add | solution.py:371
  29.1 0.0 copy-start.1
  29.1 0.0 copy-start.2
  29.1 0.7 fusion.8
  29.8 1.4 %broadcast_in_dim.57.m_ref = f32[16,128,128]{2,1,0:T(8,128)} broadcast(f32[16,128]{1,0:T(8,128)S(1)} %copy.18), dimensions={0,1} | broadcast | bytes 1056768 | tf_op jit(solution)/shard_map/broadcast_in_dim | solution.py:367
  31.2 1.0 broadcast_in_dim.66
  32.2 2.2 %slice_add_fusion = (f32[128,3,128]{2,1,0:T(4,128)}, f32[128,3,128]{2,1,0:T(4,128)}) fusion(f32[128,128,128]{2,1,0:T(8,128)S(1)} %bitcast.35, bf16[128,128,128]{2,1,0:T(8,128)(2,1)} %det_ref.1, f32[128,3]{1,0:T(8,128)S(1)} %get-tuple-element.61, f32[128,3]{1,0:T(8,128)S(1)} %get-tuple-element.62), kind=kLoop, calls=%fused_computation.21 | loop fusion | flops 294912 | bytes 986112 | tf_op jit(solution)/shard_map/add | solution.py:375
  34.4 0.0 copy-done.1
  34.4 0.0 copy-done.2
  34.4 21.8 %shard_map.65 = (f32[3,128,128]{2,1,0:T(8,128)}, f32[2,3,128]{2,1,0:T(4,128)}, f32[3,128,128]{2,1,0:T(8,128)}, f32[2,3,128]{2,1,0:T(4,128)}, f32[128,3,128]{2,1,...) custom-call(f32[3,128,128]{2,1,0:T(8,128)} %copy-done.2, ...), custom_call_target="tpu_custom_call" | custom-call | tf_op jit(solution)/shard_map/pallas_call | solution.py:346
  56.3 1.2 concatenate.13
  57.5 0.8 concatenate.12
  58.3 0.8 concatenate.14
  59.1 0.6 gather_fusion
  59.7 1.5 %broadcast_in_dim.71.h_ref = f32[18,144,128]{2,1,0:T(8,128)} broadcast(f32[18,144]{1,0:T(8,128)S(1)} %gather_fusion), dimensions={0,1} | broadcast | bytes 1337472 | tf_op jit(solution)/shard_map/broadcast_in_dim | solution.py:423
  61.2 0.0 copy-done
  61.2 6.9 %broadcast_in_dim.69.g_ref = f32[134,144,128]{2,1,0:T(8,128)} broadcast(f32[134,144]{1,0:T(8,128)S(1)} %get-tuple-element.48), dimensions={0,1} | broadcast | bytes 9956736 | tf_op jit(solution)/shard_map/broadcast_in_dim | solution.py:421
  68.1 28.7 %shard_map.66 = (f32[128,128,128]{2,1,0:T(8,128)}, f32[8,128]{1,0:T(8,128)}) custom-call(bf16[128,128,128]{2,1,0:T(8,128)(2,1)} %det_ref.1, f32[16,128,128]{2,1,0:T(8,128)} %copy-done, f32[16,128,128]{2,1,0:T(8,128)} %broadcast_in_dim.57.m_ref, f32[3,128,128]{2,1,0:T(8,128)} %get-tuple-element.23.top_ref, f32[3,128,128]{2,1,0:T(8,128)} %get-tuple-element.24.bot_ref, ...), custom_call_target="tpu_custom_call" | custom-call | flops 75497472 | bytes 22462464 | tf_op jit(solution)/shard_map/pallas_call | solution.py:124
  96.8 1.2 reduce_sum.9
  98.0 16.0 %shard_map.67 = f32[1,128]{1,0:T(1,128)} custom-call(f32[1,128]{1,0:T(1,128)} %bitcast.40), custom_call_target="tpu_custom_call" | custom-call | tf_op jit(solution)/shard_map/pallas_call | solution.py:183
  114.0 0.6 sqrt_bitcast_fusion
  114.6 8.4 %broadcast_divide_fusion = f32[128,128,128]{2,1,0:T(8,128)} fusion(f32[128,128,128]{2,1,0:T(8,128)} %get-tuple-element.39, f32[128]{0:T(128)S(1)} %sqrt_bitcast_fusion), kind=kLoop, calls=%fused_computation.1 | loop fusion | flops 2097152 | bytes 16777728 | tf_op jit(solution)/shard_map/div | solution.py:428
  (13 shorter events, 0.2 us)
Async XLA Ops:
  27.8 33.4 %copy-start = (f32[16,128,128]{2,1,0:T(8,128)}, f32[16,128,128]{2,1,0:T(8,128)S(1)}, u32[]{:S(2)}) copy-start(f32[16,128,128]{2,1,0:T(8,128)S(1)} %bitcast_multiply_fusion.cm_ref) | copy-start | bytes 3145732
  29.1 5.3 %copy-start.1 = (f32[3,128,128]{2,1,0:T(8,128)}, f32[3,128,128]{2,1,0:T(8,128)S(1)}, u32[]{:S(2)}) copy-start(f32[3,128,128]{2,1,0:T(8,128)S(1)} %get-tuple-element.43.refs_2_) | copy-start | bytes 589828
  29.1 5.3 %copy-start.2 = (f32[3,128,128]{2,1,0:T(8,128)}, f32[3,128,128]{2,1,0:T(8,128)S(1)}, u32[]{:S(2)}) copy-start(f32[3,128,128]{2,1,0:T(8,128)S(1)} %get-tuple-element.44.refs_0_) | copy-start | bytes 589828

commit v5 on v4

--- a/solution.py
+++ b/solution.py
@@ -71,10 +71,12 @@
             b = jnp.clip(x - HALO, 0, cx - 1)
             t = b // TS
             r0[s, 0:LPAD] = zero[0:LPAD]
-            r0[s, LPAD - HALO:LPAD] = left_ref[b]
+            for p in range(HALO):
+                r0[s, pl.ds(LPAD - HALO + p, 1)] = left_ref[p, pl.ds(b, 1)]
             r0[s, LPAD:LPAD + cy] = cm_ref[t] + m_ref[t] * det_ref[b].astype(jnp.float32)
             r0[s, LPAD + cy:width] = zero[0:width - LPAD - cy]
-            r0[s, LPAD + cy:LPAD + cy + HALO] = right_ref[b]
+            for p in range(HALO):
+                r0[s, pl.ds(LPAD + cy + p, 1)] = right_ref[p, pl.ds(b, 1)]
 
     def apply_b(src, x):
         v = src[x % RING]
@@ -353,6 +355,23 @@
     )(*pieces)
 
 
+def scale_kernel(x_ref, s_ref, o_ref):
+    o_ref[...] = x_ref[...] * s_ref[...]
+
+
+def scale_rows(x, inv):
+    cx, cy, k = x.shape
+    return pl.pallas_call(
+        scale_kernel,
+        grid=(cx // ROWS,),
+        in_specs=[pl.BlockSpec((ROWS, cy, k), lambda i: (i, 0, 0)), pl.BlockSpec((1, k), lambda i: (0, 0))],
+        out_specs=pl.BlockSpec((ROWS, cy, k), lambda i: (i, 0, 0)),
+        out_shape=jax.ShapeDtypeStruct(x.shape, x.dtype),
+        input_output_aliases={0: 0},
+        cost_estimate=pl.CostEstimate(flops=x.size, transcendentals=0, bytes_accessed=x.size * 8),
+    )(x, inv)
+
+
 def local(detail, coarse, diagonal, parents, tile_mask):
     tiles_x, tiles_y = parents.shape
     cells_x, cells_y, columns = detail.shape
@@ -393,16 +412,20 @@
         return a[tuple(idx)]
 
     c0_pieces = {
-        (1, 0): c0_bot, (-1, 0): c0_top, (0, 1): c0_right, (0, -1): c0_left,
+        (1, 0): c0_bot, (-1, 0): c0_top,
+        (0, 1): c0_right.transpose(1, 0, 2), (0, -1): c0_left.transpose(1, 0, 2),
         (1, 1): c0_bot[:, -h:], (1, -1): c0_bot[:, :h], (-1, 1): c0_top[:, -h:], (-1, -1): c0_top[:, :h],
     }
     pieces = []
     for dw, dn in DIRS:
         pieces.append(c0_pieces[(dw, dn)])
-        pieces.append(edge(gh, dw, dn, 1, 2))
+        e = edge(gh, dw, dn, 1, 2)
+        pieces.append(e.transpose(0, 2, 1) if dw == 0 else e)
     got = exchange_halos(pieces, nw, nn)
     hc = {dirn: got[2 * k] for k, dirn in enumerate(DIRS)}
     hg = {dirn: got[2 * k + 1] for k, dirn in enumerate(DIRS)}
+    for dirn in ((0, 1), (0, -1)):
+        hg[dirn] = hg[dirn].transpose(0, 2, 1)
     halos = [hc[(1, 0)], hc[(-1, 0)], hc[(0, 1)], hc[(0, -1)],
              hc[(1, 1)], hc[(1, -1)], hc[(-1, 1)], hc[(-1, -1)]]
 
@@ -424,8 +447,9 @@
 
     cheb_three, ss = run_stencil(detail, cm0, m0, halos, g_b, h_b)
     local_squares = jnp.sum(ss, axis=0, keepdims=True)
-    squares = allreduce(local_squares, nw, nn)[0]
-    return cheb_three / jnp.sqrt(squares / total_cells + EPSILON)
+    squares = allreduce(local_squares, nw, nn)
+    inv = 1.0 / jnp.sqrt(squares / total_cells + EPSILON)
+    return scale_rows(cheb_three, inv)
 
 
 def solution(mesh):

time: 124 us -> 124 us (level)
  other arithmetic: 18.4 us -> 8.59 us
  Pallas kernels: 84.6 us -> 90.5 us
  local copies, waits for them, and re-layouts: 19.9 us -> 23.8 us
    pallas_call x0 -> x1, Pallas kernels: none -> 11.9 us  [scale_rows(): pl.pallas_call(scale_kernel, grid=(cx // ROWS,), in_specs=[pl.BlockSpec((...]
    div x1 -> x0, other arithmetic: 8.41 us -> none  [local(): return cheb_three / jnp.sqrt(squares / total_cells + EPSILON)]
    pallas_call x1, Pallas kernels: 21.8 us -> 16 us  [exchange_halos(): pl.pallas_call(functools.partial(halo_kernel, nw, nn), in_specs=[vmem] *...]
    add x1 -> x0, other arithmetic: 2.19 us -> none  [local(): c0_left = cm_rep[:, :h] + m_rep[:, :h] * detail[:, :h].astype(jnp.float32)]
    pallas_call x0 -> x2, local copies, waits for them, and re-layouts: none -> 1.61 us  [exchange_halos(): pl.pallas_call(functools.partial(halo_kernel, nw, nn), in_specs=[vmem] *...]
    transpose x0 -> x2, local copies, waits for them, and re-layouts: none -> 1.33 us  [local(): pieces.append(e.transpose(0, 2, 1) if dw == 0 else e)]
    another operation x5 -> x4, other arithmetic: 2.93 us -> 2.17 us  [local(): gh = jnp.stack([g_own, h_own])]
where the time goes in v5:
time: 124 us; the launch traced here: 123 us
  Pallas kernels  90.5 us (73%)
  local copies, waits for them, and re-layouts  23.8 us (19%)
  other arithmetic  8.59 us (7%)
    pallas_call x1, Pallas kernels, run_stencil(): pl.pallas_call(stencil_kernel, grid=(steps,), in_specs=[vmem] * 13, out_s...  28.5 us
    pallas_call x1, Pallas kernels, gather_tiles(): pl.pallas_call(functools.partial(gather_kernel, nn, ccx), in_specs=[vmem,...  18 us
    pallas_call x1, Pallas kernels, exchange_halos(): pl.pallas_call(functools.partial(halo_kernel, nw, nn), in_specs=[vmem] *...  16 us
    pallas_call x1, Pallas kernels, allreduce(): pl.pallas_call(functools.partial(allreduce_kernel, nw, nn), in_specs=[vme...  16 us
    pallas_call x1, Pallas kernels, scale_rows(): pl.pallas_call(scale_kernel, grid=(cx // ROWS,), in_specs=[pl.BlockSpec((...  11.9 us
    broadcast_in_dim x1, local copies, waits for them, and re-layouts, local(): jnp.broadcast_to(gh_ext[0][:, :, None], (cells_x + 2 * h, width, columns))  6.86 us

profile of v5, /device:TPU:1, one launch (start us, length us, event | category | flops | bytes accessed | tf_op | source)
XLA Modules:
  0.0 123.1 jit_solution(11021752483077382293)
XLA Ops:
  0.0 1.3 %reshape.50.par_ref = s32[1,256]{1,0:T(1,128)} reshape(s32[16,16]{1,0:T(8,128)} %param.9) | data formatting | bytes 2048 | tf_op jit(solution)/shard_map/reshape | solution.py:260
  1.3 0.7 pad_clamp_fusion
  2.0 0.7 convert_element_type.15
  2.7 0.1 broadcast_in_dim.63
  2.8 0.1 broadcast_in_dim.64
  2.8 0.1 broadcast_in_dim.58
  2.9 0.1 broadcast_in_dim.59
  3.0 0.1 copy.35
  3.1 0.1 copy.36
  3.2 0.1 copy.39
  3.2 0.1 copy.40
  3.4 0.9 multiply_bitcast_fusion
  4.2 0.1 copy.41
  4.3 0.1 copy.42
  4.4 0.6 fusion.7
  5.0 0.7 fusion.11
  5.7 0.1 fusion.15
  5.8 0.1 copy.47
  5.8 0.1 copy.45
  6.0 0.1 fusion.5
  6.1 0.7 copy.50.refs_7_
  6.7 0.7 copy.49.refs_5_
  7.4 1.8 %copy.37 = bf16[1024,128]{0,1:T(8,128)(2,1)} copy(bf16[1024,128]{1,0:T(8,128)(2,1)} %bitcast.49) | data formatting | bytes 524288 | tf_op jit(solution)/shard_map/reshape | solution.py:262
  9.2 18.0 %shard_map.64 = f32[128,256]{1,0:T(8,128)} custom-call(s32[1,256]{1,0:T(1,128)} %reshape.50.par_ref, bf16[128,1024]{1,0:T(8,128)(2,1)} %bitcast.44), custom_call_target="tpu_custom_call" | custom-call | tf_op jit(solution)/shard_map/pallas_call | solution.py:264
  27.2 1.0 copy.38
  28.2 1.1 fusion.12
  29.4 0.3 bitcast_multiply_fusion.cm_ref
  29.7 0.0 copy-start
  29.7 1.3 %multiply_add_fusion = (f32[3,128,128]{2,1,0:T(8,128)S(1)}, f32[3,128,128]{2,1,0:T(8,128)S(1)}) fusion(bf16[128,128,128]{2,1,0:T(8,128)(2,1)} %det_ref.1, f32[128]{0:T(128)S(1)} %broadcast_in_dim.64, f32[128,128]{1,0:T(8,128)S(1)} %get-tuple-element.47, f32[128]{0:T(128)S(1)} %broadcast_in_dim.59, f32[128,128]{1,0:T(8,128)S(1)} %get-tuple-element.48), kind=kLoop, calls=%fused_computation.25 | loop fusion | flops 294912 | bytes 721920 | tf_op jit(solution)/shard_map/add | solution.py:390
  31.0 0.0 copy-start.1
  31.0 0.0 copy-start.2
  31.1 0.7 fusion.13
  31.7 1.4 %broadcast_in_dim.56.m_ref = f32[16,128,128]{2,1,0:T(8,128)} broadcast(f32[16,128]{1,0:T(8,128)S(1)} %copy.36), dimensions={0,1} | broadcast | bytes 1056768 | tf_op jit(solution)/shard_map/broadcast_in_dim | solution.py:386
  33.1 0.6 copy.43
  33.7 1.2 broadcast_bitcast_fusion
  34.9 0.9 fusion
  35.8 0.0 copy-done.1
  35.8 0.0 copy-done.2
  35.8 16.0 %shard_map.65 = (f32[3,128,128]{2,1,0:T(8,128)}, f32[2,3,128]{2,1,0:T(4,128)}, f32[3,128,128]{2,1,0:T(8,128)}, f32[2,3,128]{2,1,0:T(4,128)}, f32[3,128,128]{2,1,...) custom-call(f32[3,128,128]{2,1,0:T(8,128)} %copy-done.2, ...), custom_call_target="tpu_custom_call" | custom-call | tf_op jit(solution)/shard_map/pallas_call | solution.py:348
  51.9 0.8 concatenate.12
  52.6 0.8 concatenate.14
  53.4 0.8 copy.51
  54.2 0.8 copy.52
  55.1 0.2 concatenate.13
  55.3 0.0 copy-done
  55.4 0.6 gather_fusion
  56.0 1.5 %broadcast_in_dim.70.h_ref = f32[18,144,128]{2,1,0:T(8,128)} broadcast(f32[18,144]{1,0:T(8,128)S(1)} %gather_fusion), dimensions={0,1} | broadcast | bytes 1337472 | tf_op jit(solution)/shard_map/broadcast_in_dim | solution.py:446
  57.4 6.9 %broadcast_in_dim.68.g_ref = f32[134,144,128]{2,1,0:T(8,128)} broadcast(f32[134,144]{1,0:T(8,128)S(1)} %get-tuple-element.50), dimensions={0,1} | broadcast | bytes 9956736 | tf_op jit(solution)/shard_map/broadcast_in_dim | solution.py:444
  64.3 28.5 %shard_map.66 = (f32[128,128,128]{2,1,0:T(8,128)}, f32[8,128]{1,0:T(8,128)}) custom-call(bf16[128,128,128]{2,1,0:T(8,128)(2,1)} %det_ref.1, f32[16,128,128]{2,1,0:T(8,128)} %copy-done, f32[16,128,128]{2,1,0:T(8,128)} %broadcast_in_dim.56.m_ref, f32[3,128,128]{2,1,0:T(8,128)} %get-tuple-element.23.top_ref, f32[3,128,128]{2,1,0:T(8,128)} %get-tuple-element.24.bot_ref, ...), custom_call_target="tpu_custom_call" | custom-call | flops 75497472 | bytes 22462464 | tf_op jit(solution)/shard_map/pallas_call | solution.py:126
  92.8 1.2 reduce_sum.9
  94.0 16.0 %shard_map.67 = f32[1,128]{1,0:T(1,128)} custom-call(f32[1,128]{1,0:T(1,128)} %bitcast.50), custom_call_target="tpu_custom_call" | custom-call | tf_op jit(solution)/shard_map/pallas_call | solution.py:185
  110.1 1.2 add_rsqrt_fusion.s_ref
  111.3 11.9 %shard_map.68 = f32[128,128,128]{2,1,0:T(8,128)} custom-call(f32[128,128,128]{2,1,0:T(8,128)} %get-tuple-element.39.x_ref, f32[1,128]{1,0:T(1,128)} %add_rsqrt_fusion.s_ref), custom_call_target="tpu_custom_call", output_to_operand_aliasing={{}: (0, {})} | custom-call | flops 2097152 | bytes 16777216 | tf_op jit(solution)/shard_map/pallas_call | solution.py:364
  (13 shorter events, 0.2 us)
Async XLA Ops:
  29.7 25.6 %copy-start = (f32[16,128,128]{2,1,0:T(8,128)}, f32[16,128,128]{2,1,0:T(8,128)S(1)}, u32[]{:S(2)}) copy-start(f32[16,128,128]{2,1,0:T(8,128)S(1)} %bitcast_multiply_fusion.cm_ref) | copy-start | bytes 3145732
  31.0 4.8 %copy-start.1 = (f32[3,128,128]{2,1,0:T(8,128)}, f32[3,128,128]{2,1,0:T(8,128)S(1)}, u32[]{:S(2)}) copy-start(f32[3,128,128]{2,1,0:T(8,128)S(1)} %get-tuple-element.45.refs_2_) | copy-start | bytes 589828
  31.0 4.8 %copy-start.2 = (f32[3,128,128]{2,1,0:T(8,128)}, f32[3,128,128]{2,1,0:T(8,128)S(1)}, u32[]{:S(2)}) copy-start(f32[3,128,128]{2,1,0:T(8,128)S(1)} %get-tuple-element.46.refs_0_) | copy-start | bytes 589828

commit v6 on v5

--- a/solution.py
+++ b/solution.py
@@ -16,6 +16,7 @@
 LPAD = 8
 RING = 16
 ROWS = 8
+SCALE_ROWS = 32
 
 
 def shift_pairs(dw, dn, nw, nn):
@@ -363,9 +364,9 @@
     cx, cy, k = x.shape
     return pl.pallas_call(
         scale_kernel,
-        grid=(cx // ROWS,),
-        in_specs=[pl.BlockSpec((ROWS, cy, k), lambda i: (i, 0, 0)), pl.BlockSpec((1, k), lambda i: (0, 0))],
-        out_specs=pl.BlockSpec((ROWS, cy, k), lambda i: (i, 0, 0)),
+        grid=(cx // SCALE_ROWS,),
+        in_specs=[pl.BlockSpec((SCALE_ROWS, cy, k), lambda i: (i, 0, 0)), pl.BlockSpec((1, k), lambda i: (0, 0))],
+        out_specs=pl.BlockSpec((SCALE_ROWS, cy, k), lambda i: (i, 0, 0)),
         out_shape=jax.ShapeDtypeStruct(x.shape, x.dtype),
         input_output_aliases={0: 0},
         cost_estimate=pl.CostEstimate(flops=x.size, transcendentals=0, bytes_accessed=x.size * 8),

time: 124 us -> 119 us (0.960)
  Pallas kernels: 90.5 us -> 85.7 us
    pallas_call x1, Pallas kernels: 11.9 us -> 7.11 us  [scale_rows(): pl.pallas_call(scale_kernel, grid=(cx // SCALE_ROWS,), in_specs=[pl.Block...]
where the time goes in v6:
time: 119 us; the launch traced here: 118 us
  Pallas kernels  85.7 us (72%)
  local copies, waits for them, and re-layouts  23.8 us (20%)
  other arithmetic  8.59 us (7%)
    pallas_call x1, Pallas kernels, run_stencil(): pl.pallas_call(stencil_kernel, grid=(steps,), in_specs=[vmem] * 13, out_s...  28.5 us
    pallas_call x1, Pallas kernels, gather_tiles(): pl.pallas_call(functools.partial(gather_kernel, nn, ccx), in_specs=[vmem,...  18 us
    pallas_call x1, Pallas kernels, exchange_halos(): pl.pallas_call(functools.partial(halo_kernel, nw, nn), in_specs=[vmem] *...  16 us
    pallas_call x1, Pallas kernels, allreduce(): pl.pallas_call(functools.partial(allreduce_kernel, nw, nn), in_specs=[vme...  16 us
    pallas_call x1, Pallas kernels, scale_rows(): pl.pallas_call(scale_kernel, grid=(cx // SCALE_ROWS,), in_specs=[pl.Block...  7.11 us
    broadcast_in_dim x1, local copies, waits for them, and re-layouts, local(): jnp.broadcast_to(gh_ext[0][:, :, None], (cells_x + 2 * h, width, columns))  6.86 us

profile of v6, /device:TPU:1, one launch (start us, length us, event | category | flops | bytes accessed | tf_op | source)
XLA Modules:
  0.0 118.4 jit_solution(269448539313247712)
XLA Ops:
  0.0 1.3 %reshape.50.par_ref = s32[1,256]{1,0:T(1,128)} reshape(s32[16,16]{1,0:T(8,128)} %param.9) | data formatting | bytes 2048 | tf_op jit(solution)/shard_map/reshape | solution.py:261
  1.3 0.7 pad_clamp_fusion
  2.0 0.7 convert_element_type.15
  2.7 0.1 broadcast_in_dim.63
  2.8 0.1 broadcast_in_dim.64
  2.8 0.1 broadcast_in_dim.58
  2.9 0.1 broadcast_in_dim.59
  3.0 0.1 copy.35
  3.1 0.1 copy.36
  3.2 0.1 copy.39
  3.2 0.1 copy.40
  3.4 0.9 multiply_bitcast_fusion
  4.2 0.1 copy.41
  4.3 0.1 copy.42
  4.4 0.6 fusion.7
  5.0 0.7 fusion.11
  5.7 0.1 fusion.15
  5.8 0.1 copy.47
  5.8 0.1 copy.45
  6.0 0.1 fusion.5
  6.1 0.7 copy.50.refs_7_
  6.7 0.7 copy.49.refs_5_
  7.4 1.8 %copy.37 = bf16[1024,128]{0,1:T(8,128)(2,1)} copy(bf16[1024,128]{1,0:T(8,128)(2,1)} %bitcast.49) | data formatting | bytes 524288 | tf_op jit(solution)/shard_map/reshape | solution.py:263
  9.2 18.0 %shard_map.64 = f32[128,256]{1,0:T(8,128)} custom-call(s32[1,256]{1,0:T(1,128)} %reshape.50.par_ref, bf16[128,1024]{1,0:T(8,128)(2,1)} %bitcast.44), custom_call_target="tpu_custom_call" | custom-call | tf_op jit(solution)/shard_map/pallas_call | solution.py:265
  27.2 1.0 copy.38
  28.2 1.1 fusion.12
  29.4 0.3 bitcast_multiply_fusion.cm_ref
  29.7 0.0 copy-start
  29.7 1.3 %multiply_add_fusion = (f32[3,128,128]{2,1,0:T(8,128)S(1)}, f32[3,128,128]{2,1,0:T(8,128)S(1)}) fusion(bf16[128,128,128]{2,1,0:T(8,128)(2,1)} %det_ref.1, f32[128]{0:T(128)S(1)} %broadcast_in_dim.64, f32[128,128]{1,0:T(8,128)S(1)} %get-tuple-element.47, f32[128]{0:T(128)S(1)} %broadcast_in_dim.59, f32[128,128]{1,0:T(8,128)S(1)} %get-tuple-element.48), kind=kLoop, calls=%fused_computation.25 | loop fusion | flops 294912 | bytes 721920 | tf_op jit(solution)/shard_map/add | solution.py:391
  31.0 0.0 copy-start.1
  31.0 0.0 copy-start.2
  31.1 0.7 fusion.13
  31.7 1.4 %broadcast_in_dim.56.m_ref = f32[16,128,128]{2,1,0:T(8,128)} broadcast(f32[16,128]{1,0:T(8,128)S(1)} %copy.36), dimensions={0,1} | broadcast | bytes 1056768 | tf_op jit(solution)/shard_map/broadcast_in_dim | solution.py:387
  33.1 0.6 copy.43
  33.7 1.2 broadcast_bitcast_fusion
  34.9 0.9 fusion
  35.8 0.0 copy-done.1
  35.8 0.0 copy-done.2
  35.8 16.0 %shard_map.65 = (f32[3,128,128]{2,1,0:T(8,128)}, f32[2,3,128]{2,1,0:T(4,128)}, f32[3,128,128]{2,1,0:T(8,128)}, f32[2,3,128]{2,1,0:T(4,128)}, f32[3,128,128]{2,1,...) custom-call(f32[3,128,128]{2,1,0:T(8,128)} %copy-done.2, ...), custom_call_target="tpu_custom_call" | custom-call | tf_op jit(solution)/shard_map/pallas_call | solution.py:349
  51.9 0.8 concatenate.12
  52.6 0.8 concatenate.14
  53.4 0.8 copy.51
  54.2 0.8 copy.52
  55.1 0.2 concatenate.13
  55.3 0.0 copy-done
  55.4 0.6 gather_fusion
  56.0 1.5 %broadcast_in_dim.70.h_ref = f32[18,144,128]{2,1,0:T(8,128)} broadcast(f32[18,144]{1,0:T(8,128)S(1)} %gather_fusion), dimensions={0,1} | broadcast | bytes 1337472 | tf_op jit(solution)/shard_map/broadcast_in_dim | solution.py:447
  57.4 6.9 %broadcast_in_dim.68.g_ref = f32[134,144,128]{2,1,0:T(8,128)} broadcast(f32[134,144]{1,0:T(8,128)S(1)} %get-tuple-element.50), dimensions={0,1} | broadcast | bytes 9956736 | tf_op jit(solution)/shard_map/broadcast_in_dim | solution.py:445
  64.3 28.5 %shard_map.66 = (f32[128,128,128]{2,1,0:T(8,128)}, f32[8,128]{1,0:T(8,128)}) custom-call(bf16[128,128,128]{2,1,0:T(8,128)(2,1)} %det_ref.1, f32[16,128,128]{2,1,0:T(8,128)} %copy-done, f32[16,128,128]{2,1,0:T(8,128)} %broadcast_in_dim.56.m_ref, f32[3,128,128]{2,1,0:T(8,128)} %get-tuple-element.23.top_ref, f32[3,128,128]{2,1,0:T(8,128)} %get-tuple-element.24.bot_ref, ...), custom_call_target="tpu_custom_call" | custom-call | flops 75497472 | bytes 22462464 | tf_op jit(solution)/shard_map/pallas_call | solution.py:127
  92.8 1.2 %reduce_sum.9 = f32[128]{0:T(128)} reduce(f32[8,128]{1,0:T(8,128)} %get-tuple-element.40, f32[]{:T(128)} %constant.5.clone.1), dimensions={0}, to_apply=%region_0.0 | reduce | flops 896 | bytes 4612 | tf_op jit(solution)/shard_map/reduce_sum | solution.py:450
  94.0 16.0 %shard_map.67 = f32[1,128]{1,0:T(1,128)} custom-call(f32[1,128]{1,0:T(1,128)} %bitcast.50), custom_call_target="tpu_custom_call" | custom-call | tf_op jit(solution)/shard_map/pallas_call | solution.py:186
  110.1 1.2 %add_rsqrt_fusion.s_ref = f32[1,128]{1,0:T(1,128)} fusion(f32[1,128]{1,0:T(1,128)} %shard_map.67), kind=kLoop, calls=%fused_computation.51 | loop fusion | flops 256 | bytes 1024 | tf_op jit(solution)/shard_map/sqrt | solution.py:452
  111.3 7.1 %shard_map.68 = f32[128,128,128]{2,1,0:T(8,128)} custom-call(f32[128,128,128]{2,1,0:T(8,128)} %get-tuple-element.39.x_ref, f32[1,128]{1,0:T(1,128)} %add_rsqrt_fusion.s_ref), custom_call_target="tpu_custom_call", output_to_operand_aliasing={{}: (0, {})} | custom-call | flops 2097152 | bytes 16777216 | tf_op jit(solution)/shard_map/pallas_call | solution.py:365
  (13 shorter events, 0.2 us)
Async XLA Ops:
  29.7 25.6 %copy-start = (f32[16,128,128]{2,1,0:T(8,128)}, f32[16,128,128]{2,1,0:T(8,128)S(1)}, u32[]{:S(2)}) copy-start(f32[16,128,128]{2,1,0:T(8,128)S(1)} %bitcast_multiply_fusion.cm_ref) | copy-start | bytes 3145732
  31.0 4.8 %copy-start.1 = (f32[3,128,128]{2,1,0:T(8,128)}, f32[3,128,128]{2,1,0:T(8,128)S(1)}, u32[]{:S(2)}) copy-start(f32[3,128,128]{2,1,0:T(8,128)S(1)} %get-tuple-element.45.refs_2_) | copy-start | bytes 589828
  31.0 4.8 %copy-start.2 = (f32[3,128,128]{2,1,0:T(8,128)}, f32[3,128,128]{2,1,0:T(8,128)S(1)}, u32[]{:S(2)}) copy-start(f32[3,128,128]{2,1,0:T(8,128)S(1)} %get-tuple-element.46.refs_0_) | copy-start | bytes 589828

commit v7 on v6

--- a/solution.py
+++ b/solution.py
@@ -39,9 +39,14 @@
     return out
 
 
-def stencil_kernel(det_ref, cm_ref, m_ref, top_ref, bot_ref, left_ref, right_ref,
-                   tl_ref, tr_ref, bl_ref, br_ref, g_ref, h_ref, out_ref, ss_ref, r0, r1, r2):
+def stencil_kernel(nw, nn, det_ref, cm_ref, m_ref, top_ref, bot_ref, left_ref, right_ref,
+                   tl_ref, tr_ref, bl_ref, br_ref, g_ref, h_ref, out_ref, sq_ref, r0, r1, r2, ss_ref,
+                   part1, part2, q1, q2, s1, p1, s2, p2):
     i = pl.program_id(0)
+    me_w = lax.axis_index("wide")
+    me_n = lax.axis_index("narrow")
+    mesh_id = pl.DeviceIdType.MESH
+    barrier = pltpu.get_barrier_semaphore()
     cx = det_ref.shape[0]
     width = g_ref.shape[1]
     ext_rows = g_ref.shape[0]
@@ -106,6 +111,10 @@
 
     @pl.when(i == 0)
     def _():
+        for k in range(1, nn):
+            pl.semaphore_signal(barrier, inc=1, device_id=(me_w, (me_n + k) % nn), device_id_type=mesh_id)
+        for k in range(1, nw):
+            pl.semaphore_signal(barrier, inc=1, device_id=((me_w + k) % nw, me_n), device_id_type=mesh_id)
         ss_ref[...] = jnp.zeros_like(ss_ref)
         rows(c0_row, 0, 2 * HALO)
         rows(c1_row, 1, 2 * HALO - 2)
@@ -117,87 +126,71 @@
     rows(c2_row, base + 2 * HALO - 2, ROWS)
     rows(c3_row, base + HALO, ROWS)
 
-
-def run_stencil(det, cm, m, halos, g, h):
+    @pl.when(i == pl.num_programs(0) - 1)
+    def _():
+        pl.semaphore_wait(barrier, nn - 1 + nw - 1)
+        part1[...] = jnp.sum(ss_ref[...], axis=0, keepdims=True)
+        part2[...] = exchange_sum(part1, q1, s1, p1, me_n, nn, lambda j: (me_w, j))
+        sq_ref[...] = exchange_sum(part2, q2, s2, p2, me_w, nw, lambda j: (j, me_n))
+
+
+def exchange_sum(src, slots, send, recv, me, n, peer_of):
+    mesh_id = pl.DeviceIdType.MESH
+    copies = []
+    for k in range(1, n):
+        c = pltpu.make_async_remote_copy(
+            src_ref=src, dst_ref=slots.at[me], send_sem=send.at[k], recv_sem=recv.at[me],
+            device_id=peer_of((me + k) % n), device_id_type=mesh_id)
+        c.start()
+        copies.append(c)
+    slots[me] = src[...]
+    for k in range(1, n):
+        other = (me + k) % n
+        pltpu.make_async_remote_copy(
+            src_ref=src, dst_ref=slots.at[other], send_sem=send.at[k], recv_sem=recv.at[other],
+            device_id=peer_of(other), device_id_type=mesh_id).wait_recv()
+    for c in copies:
+        c.wait_send()
+    return jnp.sum(slots[...], axis=0)
+
+
+def run_stencil(det, cm, m, halos, g, h, nw, nn):
     cx, cy, k = det.shape
     width = g.shape[1]
     steps = cx // ROWS
     vmem = pl.BlockSpec(memory_space=pltpu.VMEM)
     ops = cx * cy * k * 3 * 12
     return pl.pallas_call(
-        stencil_kernel,
+        functools.partial(stencil_kernel, nw, nn),
         grid=(steps,),
         in_specs=[vmem] * 13,
         out_specs=[
             pl.BlockSpec((ROWS, cy, k), lambda i: (i, 0, 0)),
-            pl.BlockSpec((8, k), lambda i: (0, 0)),
+            pl.BlockSpec((1, k), lambda i: (0, 0)),
         ],
         out_shape=[
             jax.ShapeDtypeStruct((cx, cy, k), jnp.float32),
-            jax.ShapeDtypeStruct((8, k), jnp.float32),
+            jax.ShapeDtypeStruct((1, k), jnp.float32),
         ],
-        scratch_shapes=[pltpu.VMEM((RING, width, k), jnp.float32) for _ in range(3)],
+        scratch_shapes=[pltpu.VMEM((RING, width, k), jnp.float32) for _ in range(3)] + [
+            pltpu.VMEM((8, k), jnp.float32),
+            pltpu.VMEM((1, k), jnp.float32),
+            pltpu.VMEM((1, k), jnp.float32),
+            pltpu.VMEM((nn, 1, k), jnp.float32),
+            pltpu.VMEM((nw, 1, k), jnp.float32),
+            pltpu.SemaphoreType.DMA((nn,)),
+            pltpu.SemaphoreType.DMA((nn,)),
+            pltpu.SemaphoreType.DMA((nw,)),
+            pltpu.SemaphoreType.DMA((nw,)),
+        ],
         compiler_params=pltpu.CompilerParams(
-            dimension_semantics=("arbitrary",), vmem_limit_bytes=56 * 1024 * 1024
+            dimension_semantics=("arbitrary",), vmem_limit_bytes=56 * 1024 * 1024,
+            collective_id=0, has_side_effects=True,
         ),
         cost_estimate=pl.CostEstimate(
             flops=ops, transcendentals=0, bytes_accessed=det.size * 2 + cx * cy * k * 4 + g.size * 4
         ),
     )(det, cm, m, *halos, g, h)
-
-
-def allreduce_kernel(nw, nn, x_ref, o_ref, r1, r2, s1, q1, s2, q2):
-    me_w = lax.axis_index("wide")
-    me_n = lax.axis_index("narrow")
-    mesh_id = pl.DeviceIdType.MESH
-    barrier = pltpu.get_barrier_semaphore()
-    for k in range(1, nn):
-        pl.semaphore_signal(barrier, inc=1, device_id=(me_w, (me_n + k) % nn), device_id_type=mesh_id)
-    for k in range(1, nw):
-        pl.semaphore_signal(barrier, inc=1, device_id=((me_w + k) % nw, me_n), device_id_type=mesh_id)
-    pl.semaphore_wait(barrier, nn - 1 + nw - 1)
-
-    def phase(src, slots, send, recv, me, n, peer_of):
-        copies = []
-        for k in range(1, n):
-            c = pltpu.make_async_remote_copy(
-                src_ref=src, dst_ref=slots.at[me], send_sem=send.at[k], recv_sem=recv.at[me],
-                device_id=peer_of((me + k) % n), device_id_type=mesh_id)
-            c.start()
-            copies.append(c)
-        slots[me] = src[...]
-        for k in range(1, n):
-            other = (me + k) % n
-            pltpu.make_async_remote_copy(
-                src_ref=src, dst_ref=slots.at[other], send_sem=send.at[k], recv_sem=recv.at[other],
-                device_id=peer_of(other), device_id_type=mesh_id).wait_recv()
-        for c in copies:
-            c.wait_send()
-        return jnp.sum(slots[...], axis=0)
-
-    part = phase(x_ref, r1, s1, q1, me_n, nn, lambda j: (me_w, j))
-    o_ref[...] = part
-    o_ref[...] = phase(o_ref, r2, s2, q2, me_w, nw, lambda j: (j, me_n))
-
-
-def allreduce(x, nw, nn):
-    k = x.shape[-1]
-    vmem = pl.BlockSpec(memory_space=pltpu.VMEM)
-    return pl.pallas_call(
-        functools.partial(allreduce_kernel, nw, nn),
-        in_specs=[vmem],
-        out_specs=vmem,
-        out_shape=jax.ShapeDtypeStruct((1, k), jnp.float32),
-        scratch_shapes=[
-            pltpu.VMEM((nn, 1, k), jnp.float32),
-            pltpu.VMEM((nw, 1, k), jnp.float32),
-            pltpu.SemaphoreType.DMA((nn,)),
-            pltpu.SemaphoreType.DMA((nn,)),
-            pltpu.SemaphoreType.DMA((nw,)),
-            pltpu.SemaphoreType.DMA((nw,)),
-        ],
-        compiler_params=pltpu.CompilerParams(collective_id=0, has_side_effects=True),
-    )(x)
 
 
 def gather_kernel(nn, cols, par_ref, ct_ref, o_ref, pslots, stage, tslots, ps, pq, ts, tq):
@@ -368,7 +361,6 @@
         in_specs=[pl.BlockSpec((SCALE_ROWS, cy, k), lambda i: (i, 0, 0)), pl.BlockSpec((1, k), lambda i: (0, 0))],
         out_specs=pl.BlockSpec((SCALE_ROWS, cy, k), lambda i: (i, 0, 0)),
         out_shape=jax.ShapeDtypeStruct(x.shape, x.dtype),
-        input_output_aliases={0: 0},
         cost_estimate=pl.CostEstimate(flops=x.size, transcendentals=0, bytes_accessed=x.size * 8),
     )(x, inv)
 
@@ -446,9 +438,7 @@
     h_rows = gh_ext[1][jnp.array([0] + [h + TS * t for t in range(tiles_x)] + [h + cells_x])]
     h_b = jnp.broadcast_to(h_rows[:, :, None], (tiles_x + 2, width, columns))
 
-    cheb_three, ss = run_stencil(detail, cm0, m0, halos, g_b, h_b)
-    local_squares = jnp.sum(ss, axis=0, keepdims=True)
-    squares = allreduce(local_squares, nw, nn)
+    cheb_three, squares = run_stencil(detail, cm0, m0, halos, g_b, h_b, nw, nn)
     inv = 1.0 / jnp.sqrt(squares / total_cells + EPSILON)
     return scale_rows(cheb_three, inv)
 

time: 119 us -> 116 us (0.975)
  Pallas kernels: 85.7 us -> 83.5 us
    pallas_call x2 -> x1, Pallas kernels: 44.6 us -> 42.3 us  [run_stencil(): pl.pallas_call(functools.partial(stencil_kernel, nw, nn), grid=(steps,),...]
    reduce_sum x1 -> x0, other arithmetic: 1.21 us -> none  [local(): local_squares = jnp.sum(ss, axis=0, keepdims=True)]
where the time goes in v7:
time: 116 us; the launch traced here: 115 us
  Pallas kernels  83.5 us (72%)
  local copies, waits for them, and re-layouts  23.9 us (21%)
  other arithmetic  7.45 us (6%)
    pallas_call x1, Pallas kernels, run_stencil(): pl.pallas_call(functools.partial(stencil_kernel, nw, nn), grid=(steps,),...  42.3 us
    pallas_call x1, Pallas kernels, gather_tiles(): pl.pallas_call(functools.partial(gather_kernel, nn, ccx), in_specs=[vmem,...  18 us
    pallas_call x1, Pallas kernels, exchange_halos(): pl.pallas_call(functools.partial(halo_kernel, nw, nn), in_specs=[vmem] *...  16 us
    pallas_call x1, Pallas kernels, scale_rows(): pl.pallas_call(scale_kernel, grid=(cx // SCALE_ROWS,), in_specs=[pl.Block...  7.11 us
    broadcast_in_dim x1, local copies, waits for them, and re-layouts, local(): jnp.broadcast_to(gh_ext[0][:, :, None], (cells_x + 2 * h, width, columns))  6.89 us

profile of v7, /device:TPU:1, one launch (start us, length us, event | category | flops | bytes accessed | tf_op | source)
XLA Modules:
  0.0 115.0 jit_solution(14015482939968930601)
XLA Ops:
  0.0 1.4 %reshape.50.par_ref = s32[1,256]{1,0:T(1,128)} reshape(s32[16,16]{1,0:T(8,128)} %param.9) | data formatting | bytes 2048 | tf_op jit(solution)/shard_map/reshape | solution.py:254
  1.4 0.7 pad_clamp_fusion
  2.0 0.7 convert_element_type.15
  2.7 0.1 broadcast_in_dim.60
  2.8 0.1 broadcast_in_dim.61
  2.9 0.1 broadcast_in_dim.55
  3.0 0.1 broadcast_in_dim.56
  3.0 0.1 copy.34
  3.1 0.1 copy.35
  3.2 0.1 copy.38
  3.3 0.1 copy.39
  3.4 0.9 multiply_bitcast_fusion
  4.3 0.1 copy.40
  4.3 0.1 copy.41
  4.5 0.6 fusion.7
  5.1 0.7 fusion.11
  5.7 0.1 fusion.15
  5.8 0.1 copy.46
  5.9 0.1 copy.44
  6.0 0.1 fusion.5
  6.1 0.7 copy.49.refs_7_
  6.8 0.7 copy.48.refs_5_
  7.4 1.8 %copy.36 = bf16[1024,128]{0,1:T(8,128)(2,1)} copy(bf16[1024,128]{1,0:T(8,128)(2,1)} %bitcast.48) | data formatting | bytes 524288 | tf_op jit(solution)/shard_map/reshape | solution.py:256
  9.2 18.0 %shard_map.64 = f32[128,256]{1,0:T(8,128)} custom-call(s32[1,256]{1,0:T(1,128)} %reshape.50.par_ref, bf16[128,1024]{1,0:T(8,128)(2,1)} %bitcast.43), custom_call_target="tpu_custom_call" | custom-call | tf_op jit(solution)/shard_map/pallas_call | solution.py:258
  27.3 1.0 copy.37
  28.3 1.1 fusion.12
  29.4 0.3 bitcast_multiply_fusion.cm_ref
  29.8 0.0 copy-start
  29.8 1.3 %multiply_add_fusion = (f32[3,128,128]{2,1,0:T(8,128)S(1)}, f32[3,128,128]{2,1,0:T(8,128)S(1)}) fusion(bf16[128,128,128]{2,1,0:T(8,128)(2,1)} %det_ref.1, f32[128]{0:T(128)S(1)} %broadcast_in_dim.61, f32[128,128]{1,0:T(8,128)S(1)} %get-tuple-element.47, f32[128]{0:T(128)S(1)} %broadcast_in_dim.56, f32[128,128]{1,0:T(8,128)S(1)} %get-tuple-element.48), kind=kLoop, calls=%fused_computation.25 | loop fusion | flops 294912 | bytes 721920 | tf_op jit(solution)/shard_map/add | solution.py:383
  31.1 0.0 copy-start.1
  31.1 0.0 copy-start.2
  31.1 0.7 fusion.13
  31.8 1.3 %broadcast_in_dim.53.m_ref = f32[16,128,128]{2,1,0:T(8,128)} broadcast(f32[16,128]{1,0:T(8,128)S(1)} %copy.35), dimensions={0,1} | broadcast | bytes 1056768 | tf_op jit(solution)/shard_map/broadcast_in_dim | solution.py:379
  33.1 0.6 copy.42
  33.7 1.2 %broadcast_bitcast_fusion = f32[128,128,128]{2,0,1:T(8,128)S(1)} fusion(f32[16,128,128]{2,0,1:T(8,128)S(1)} %copy.42), kind=kLoop, calls=%fused_computation.1 | loop fusion | bytes 9437184 | tf_op jit(solution)/shard_map/reshape | solution.py:385
  34.9 0.9 fusion
  35.8 0.0 copy-done.1
  35.8 0.0 copy-done.2
  35.8 16.0 %shard_map.65 = (f32[3,128,128]{2,1,0:T(8,128)}, f32[2,3,128]{2,1,0:T(4,128)}, f32[3,128,128]{2,1,0:T(8,128)}, f32[2,3,128]{2,1,0:T(4,128)}, f32[3,128,128]{2,1,...) custom-call(f32[3,128,128]{2,1,0:T(8,128)} %copy-done.2, ...), custom_call_target="tpu_custom_call" | custom-call | tf_op jit(solution)/shard_map/pallas_call | solution.py:342
  51.9 0.8 concatenate.12
  52.7 0.8 concatenate.14
  53.4 0.8 copy.50
  54.2 0.8 copy.51
  55.1 0.2 concatenate.13
  55.3 0.0 copy-done
  55.4 0.6 gather_fusion
  56.0 1.5 %broadcast_in_dim.67.h_ref = f32[18,144,128]{2,1,0:T(8,128)} broadcast(f32[18,144]{1,0:T(8,128)S(1)} %gather_fusion), dimensions={0,1} | broadcast | bytes 1337472 | tf_op jit(solution)/shard_map/broadcast_in_dim | solution.py:439
  57.5 6.9 %broadcast_in_dim.65.g_ref = f32[134,144,128]{2,1,0:T(8,128)} broadcast(f32[134,144]{1,0:T(8,128)S(1)} %get-tuple-element.50), dimensions={0,1} | broadcast | bytes 9956736 | tf_op jit(solution)/shard_map/broadcast_in_dim | solution.py:437
  64.3 42.3 %shard_map.66 = (f32[128,128,128]{2,1,0:T(8,128)}, f32[1,128]{1,0:T(1,128)}) custom-call(bf16[128,128,128]{2,1,0:T(8,128)(2,1)} %det_ref.1, f32[16,128,128]{2,1,0:T(8,128)} %copy-done, f32[16,128,128]{2,1,0:T(8,128)} %broadcast_in_dim.53.m_ref, f32[3,128,128]{2,1,0:T(8,128)} %get-tuple-element.23.top_ref, f32[3,128,128]{2,1,0:T(8,128)} %get-tuple-element.24.bot_ref, ...), custom_call_target="tpu_custom_call" | custom-call | flops 75497472 | bytes 22462464 | tf_op jit(solution)/shard_map/pallas_call | solution.py:163
  106.7 1.3 %add_rsqrt_fusion.s_ref = f32[1,128]{1,0:T(1,128)} fusion(f32[1,128]{1,0:T(1,128)} %get-tuple-element.40), kind=kLoop, calls=%fused_computation.51 | loop fusion | flops 256 | bytes 1024 | tf_op jit(solution)/shard_map/sqrt | solution.py:442
  107.9 7.1 %shard_map.67 = f32[128,128,128]{2,1,0:T(8,128)} custom-call(f32[128,128,128]{2,1,0:T(8,128)} %get-tuple-element.39.x_ref, f32[1,128]{1,0:T(1,128)} %add_rsqrt_fusion.s_ref), custom_call_target="tpu_custom_call" | custom-call | flops 2097152 | bytes 16777216 | tf_op jit(solution)/shard_map/pallas_call | solution.py:358
  (13 shorter events, 0.2 us)
Async XLA Ops:
  29.8 25.5 %copy-start = (f32[16,128,128]{2,1,0:T(8,128)}, f32[16,128,128]{2,1,0:T(8,128)S(1)}, u32[]{:S(2)}) copy-start(f32[16,128,128]{2,1,0:T(8,128)S(1)} %bitcast_multiply_fusion.cm_ref) | copy-start | bytes 3145732
  31.1 4.7 %copy-start.1 = (f32[3,128,128]{2,1,0:T(8,128)}, f32[3,128,128]{2,1,0:T(8,128)S(1)}, u32[]{:S(2)}) copy-start(f32[3,128,128]{2,1,0:T(8,128)S(1)} %get-tuple-element.45.refs_2_) | copy-start | bytes 589828
  31.1 4.7 %copy-start.2 = (f32[3,128,128]{2,1,0:T(8,128)}, f32[3,128,128]{2,1,0:T(8,128)S(1)}, u32[]{:S(2)}) copy-start(f32[3,128,128]{2,1,0:T(8,128)S(1)} %get-tuple-element.46.refs_0_) | copy-start | bytes 589828

commit v8 on v7

--- a/solution.py
+++ b/solution.py
@@ -213,7 +213,7 @@
         c.start()
         sent.append(c)
 
-    local_cells = ct_ref.shape[1]
+    local_cells = ct_ref.shape[0]
     ncols = local_cells // cols
 
     def contribution(par):
@@ -222,7 +222,8 @@
         idx = jnp.where(col // ncols == me_n, idx, -1)
         rows = lax.broadcasted_iota(jnp.int32, (local_cells, par.shape[-1]), 0)
         onehot = (rows == idx).astype(jnp.bfloat16)
-        got = jnp.dot(ct_ref[...], onehot, preferred_element_type=jnp.float32)
+        got = lax.dot_general(ct_ref[...], onehot, (((0,), (0,)), ((), ())),
+                              preferred_element_type=jnp.float32)
         return got.astype(jnp.bfloat16)
 
     tslots[me_n] = contribution(par_ref[...])
@@ -253,7 +254,7 @@
     ccx, ccy, k = coarse.shape
     par = parents.reshape(1, -1)
     n_t = par.shape[-1]
-    ct = coarse.reshape(ccx * ccy, k).T
+    ct = coarse.reshape(ccx * ccy, k)
     vmem = pl.BlockSpec(memory_space=pltpu.VMEM)
     return pl.pallas_call(
         functools.partial(gather_kernel, nn, ccx),
@@ -412,13 +413,10 @@
     pieces = []
     for dw, dn in DIRS:
         pieces.append(c0_pieces[(dw, dn)])
-        e = edge(gh, dw, dn, 1, 2)
-        pieces.append(e.transpose(0, 2, 1) if dw == 0 else e)
+        pieces.append(edge(gh, dw, dn, 1, 2))
     got = exchange_halos(pieces, nw, nn)
     hc = {dirn: got[2 * k] for k, dirn in enumerate(DIRS)}
     hg = {dirn: got[2 * k + 1] for k, dirn in enumerate(DIRS)}
-    for dirn in ((0, 1), (0, -1)):
-        hg[dirn] = hg[dirn].transpose(0, 2, 1)
     halos = [hc[(1, 0)], hc[(-1, 0)], hc[(0, 1)], hc[(0, -1)],
              hc[(1, 1)], hc[(1, -1)], hc[(-1, 1)], hc[(-1, -1)]]
 

time: 116 us -> 118 us (1.017)
  Pallas kernels: 83.5 us -> 89.2 us
  local copies, waits for them, and re-layouts: 23.9 us -> 20.1 us
    pallas_call x1, Pallas kernels: 16 us -> 21.6 us  [exchange_halos(): pl.pallas_call(functools.partial(halo_kernel, nw, nn), in_specs=[vmem] *...]
    reshape x1 -> x0, local copies, waits for them, and re-layouts: 1.79 us -> none  [gather_tiles(): ct = coarse.reshape(ccx * ccy, k).T]
    pallas_call x2 -> x0, local copies, waits for them, and re-layouts: 1.61 us -> none  [exchange_halos(): pl.pallas_call(functools.partial(halo_kernel, nw, nn), in_specs=[vmem] *...]
    transpose x2 -> x0, local copies, waits for them, and re-layouts: 1.34 us -> none  [local(): pieces.append(e.transpose(0, 2, 1) if dw == 0 else e)]
    another operation x4 -> x5, other arithmetic: 2.17 us -> 2.91 us  [local(): gh = jnp.stack([g_own, h_own])]
where the time goes in v8:
time: 118 us
  Pallas kernels  89.2 us (76%)
  local copies, waits for them, and re-layouts  20.1 us (17%)
  other arithmetic  8.1 us (7%)
    pallas_call x1, Pallas kernels, run_stencil(): pl.pallas_call(functools.partial(stencil_kernel, nw, nn), grid=(steps,),...  42.3 us
    pallas_call x1, Pallas kernels, exchange_halos(): pl.pallas_call(functools.partial(halo_kernel, nw, nn), in_specs=[vmem] *...  21.6 us
    pallas_call x1, Pallas kernels, gather_tiles(): pl.pallas_call(functools.partial(gather_kernel, nn, ccx), in_specs=[vmem,...  18.2 us
    pallas_call x1, Pallas kernels, scale_rows(): pl.pallas_call(scale_kernel, grid=(cx // SCALE_ROWS,), in_specs=[pl.Block...  7.11 us
    broadcast_in_dim x1, local copies, waits for them, and re-layouts, local(): jnp.broadcast_to(gh_ext[0][:, :, None], (cells_x + 2 * h, width, columns))  6.89 us
    another operation x5, other arithmetic, local(): gh = jnp.stack([g_own, h_own])  2.91 us

profile of v8, /device:TPU:1, one launch (start us, length us, event | category | flops | bytes accessed | tf_op | source)
XLA Modules:
  0.0 117.6 jit_solution(15093645535744662439)
XLA Ops:
  0.0 1.3 %reshape.50.par_ref = s32[1,256]{1,0:T(1,128)} reshape(s32[16,16]{1,0:T(8,128)} %param.9) | data formatting | bytes 2048 | tf_op jit(solution)/shard_map/reshape | solution.py:255
  1.3 0.7 pad_clamp_fusion
  2.0 0.7 convert_element_type.15
  2.7 0.1 broadcast_in_dim.60
  2.8 0.1 broadcast_in_dim.61
  2.9 0.1 broadcast_in_dim.55
  2.9 0.1 broadcast_in_dim.56
  3.0 0.1 copy.24
  3.1 0.1 copy.25
  3.2 0.1 copy.27
  3.3 0.1 copy.28
  3.4 0.9 multiply_bitcast_fusion
  4.3 0.1 copy.29
  4.3 0.1 copy.30
  4.4 0.6 fusion.5
  5.0 0.7 fusion.9
  5.7 0.1 fusion.13
  5.8 0.1 copy.35
  5.9 0.1 copy.33
  5.9 18.2 %shard_map.64 = f32[128,256]{1,0:T(8,128)} custom-call(s32[1,256]{1,0:T(1,128)} %reshape.50.par_ref, bf16[1024,128]{1,0:T(8,128)(2,1)} %bitcast.38), custom_call_target="tpu_custom_call" | custom-call | tf_op jit(solution)/shard_map/pallas_call | solution.py:259
  24.1 1.0 copy.26
  25.1 0.8 fusion.3
  25.9 1.1 fusion.10
  27.0 0.3 bitcast_multiply_fusion.cm_ref
  27.4 0.0 copy-start
  27.4 1.3 %multiply_add_fusion = (f32[3,128,128]{2,1,0:T(8,128)S(1)}, f32[3,128,128]{2,1,0:T(8,128)S(1)}) fusion(bf16[128,128,128]{2,1,0:T(8,128)(2,1)} %det_ref.1, f32[128]{0:T(128)S(1)} %broadcast_in_dim.61, f32[128,128]{1,0:T(8,128)S(1)} %get-tuple-element.47, f32[128]{0:T(128)S(1)} %broadcast_in_dim.56, f32[128,128]{1,0:T(8,128)S(1)} %get-tuple-element.48), kind=kLoop, calls=%fused_computation.25 | loop fusion | flops 294912 | bytes 721920 | tf_op jit(solution)/shard_map/add | solution.py:384
  28.7 0.0 copy-start.1
  28.7 0.0 copy-start.2
  28.7 0.7 fusion.11
  29.4 1.3 %broadcast_in_dim.53.m_ref = f32[16,128,128]{2,1,0:T(8,128)} broadcast(f32[16,128]{1,0:T(8,128)S(1)} %copy.25), dimensions={0,1} | broadcast | bytes 1056768 | tf_op jit(solution)/shard_map/broadcast_in_dim | solution.py:380
  30.7 0.6 copy.31
  31.3 1.2 broadcast_bitcast_fusion
  32.5 0.9 fusion
  33.4 0.0 copy-done.1
  33.4 0.0 copy-done.2
  33.4 21.6 %shard_map.65 = (f32[3,128,128]{2,1,0:T(8,128)}, f32[2,3,128]{2,1,0:T(4,128)}, f32[3,128,128]{2,1,0:T(8,128)}, f32[2,3,128]{2,1,0:T(4,128)}, f32[3,128,128]{2,1,...) custom-call(f32[3,128,128]{2,1,0:T(8,128)} %copy-done.2, ...), custom_call_target="tpu_custom_call" | custom-call | tf_op jit(solution)/shard_map/pallas_call | solution.py:343
  55.1 1.2 %concatenate.13 = f32[2,128,144]{2,1,0:T(8,128)S(1)} concatenate(f32[2,128,5]{2,1,0:T(8,128)S(1)} %broadcast_in_dim.63, f32[2,128,3]{2,1,0:T(8,128)} %get-tuple-element.34, f32[2,128,128]{2,1,0:T(8,128)S(1)} %pad_maximum_fusion, f32[2,128,3]{2,1,0:T(8,128)} %get-tuple-element.35, f32[2,128,5]{2,1,0:T(8,128)S(1)} %broadcast_in_dim.63), dimensions={2} | concatenate | bytes 294912 | tf_op jit(solution)/shard_map/concatenate | solution.py:429
  56.3 0.0 copy-done
  56.3 0.8 concatenate.12
  57.1 0.8 concatenate.14
  57.9 0.6 gather_fusion
  58.5 1.5 %broadcast_in_dim.67.h_ref = f32[18,144,128]{2,1,0:T(8,128)} broadcast(f32[18,144]{1,0:T(8,128)S(1)} %gather_fusion), dimensions={0,1} | broadcast | bytes 1337472 | tf_op jit(solution)/shard_map/broadcast_in_dim | solution.py:437
  60.0 6.9 %broadcast_in_dim.65.g_ref = f32[134,144,128]{2,1,0:T(8,128)} broadcast(f32[134,144]{1,0:T(8,128)S(1)} %get-tuple-element.50), dimensions={0,1} | broadcast | bytes 9956736 | tf_op jit(solution)/shard_map/broadcast_in_dim | solution.py:435
  66.9 42.3 %shard_map.66 = (f32[128,128,128]{2,1,0:T(8,128)}, f32[1,128]{1,0:T(1,128)}) custom-call(bf16[128,128,128]{2,1,0:T(8,128)(2,1)} %det_ref.1, f32[16,128,128]{2,1,0:T(8,128)} %copy-done, f32[16,128,128]{2,1,0:T(8,128)} %broadcast_in_dim.53.m_ref, f32[3,128,128]{2,1,0:T(8,128)} %get-tuple-element.23.top_ref, f32[3,128,128]{2,1,0:T(8,128)} %get-tuple-element.24.bot_ref, ...), custom_call_target="tpu_custom_call" | custom-call | flops 75497472 | bytes 22462464 | tf_op jit(solution)/shard_map/pallas_call | solution.py:163
  109.2 1.3 %add_rsqrt_fusion.s_ref = f32[1,128]{1,0:T(1,128)} fusion(f32[1,128]{1,0:T(1,128)} %get-tuple-element.40), kind=kLoop, calls=%fused_computation.49 | loop fusion | flops 256 | bytes 1024 | tf_op jit(solution)/shard_map/sqrt | solution.py:440
  110.5 7.1 %shard_map.67 = f32[128,128,128]{2,1,0:T(8,128)} custom-call(f32[128,128,128]{2,1,0:T(8,128)} %get-tuple-element.39.x_ref, f32[1,128]{1,0:T(1,128)} %add_rsqrt_fusion.s_ref), custom_call_target="tpu_custom_call" | custom-call | flops 2097152 | bytes 16777216 | tf_op jit(solution)/shard_map/pallas_call | solution.py:359
  (13 shorter events, 0.2 us)
Async XLA Ops:
  27.4 28.9 %copy-start = (f32[16,128,128]{2,1,0:T(8,128)}, f32[16,128,128]{2,1,0:T(8,128)S(1)}, u32[]{:S(2)}) copy-start(f32[16,128,128]{2,1,0:T(8,128)S(1)} %bitcast_multiply_fusion.cm_ref) | copy-start | bytes 3145732
  28.7 4.7 %copy-start.1 = (f32[3,128,128]{2,1,0:T(8,128)}, f32[3,128,128]{2,1,0:T(8,128)S(1)}, u32[]{:S(2)}) copy-start(f32[3,128,128]{2,1,0:T(8,128)S(1)} %get-tuple-element.45.refs_2_) | copy-start | bytes 589828
  28.7 4.7 %copy-start.2 = (f32[3,128,128]{2,1,0:T(8,128)}, f32[3,128,128]{2,1,0:T(8,128)S(1)}, u32[]{:S(2)}) copy-start(f32[3,128,128]{2,1,0:T(8,128)S(1)} %get-tuple-element.46.refs_0_) | copy-start | bytes 589828

commit v9 on v8

--- a/solution.py
+++ b/solution.py
@@ -413,10 +413,13 @@
     pieces = []
     for dw, dn in DIRS:
         pieces.append(c0_pieces[(dw, dn)])
-        pieces.append(edge(gh, dw, dn, 1, 2))
+        e = edge(gh, dw, dn, 1, 2)
+        pieces.append(e.transpose(0, 2, 1) if dw == 0 else e)
     got = exchange_halos(pieces, nw, nn)
     hc = {dirn: got[2 * k] for k, dirn in enumerate(DIRS)}
     hg = {dirn: got[2 * k + 1] for k, dirn in enumerate(DIRS)}
+    for dirn in ((0, 1), (0, -1)):
+        hg[dirn] = hg[dirn].transpose(0, 2, 1)
     halos = [hc[(1, 0)], hc[(-1, 0)], hc[(0, 1)], hc[(0, -1)],
              hc[(1, 1)], hc[(1, -1)], hc[(-1, 1)], hc[(-1, -1)]]
 

time: 118 us -> 114 us (0.966)
  Pallas kernels: 89.2 us -> 83.6 us
  local copies, waits for them, and re-layouts: 20.1 us -> 22.1 us
    pallas_call x1, Pallas kernels: 21.6 us -> 16 us  [exchange_halos(): pl.pallas_call(functools.partial(halo_kernel, nw, nn), in_specs=[vmem] *...]
    pallas_call x0 -> x2, local copies, waits for them, and re-layouts: none -> 1.61 us  [exchange_halos(): pl.pallas_call(functools.partial(halo_kernel, nw, nn), in_specs=[vmem] *...]
    transpose x0 -> x2, local copies, waits for them, and re-layouts: none -> 1.35 us  [local(): pieces.append(e.transpose(0, 2, 1) if dw == 0 else e)]
    another operation x5 -> x4, other arithmetic: 2.91 us -> 2.14 us  [local(): gh = jnp.stack([g_own, h_own])]
where the time goes in v9:
time: 114 us; the launch traced here: 113 us
  Pallas kernels  83.6 us (73%)
  local copies, waits for them, and re-layouts  22.1 us (19%)
  other arithmetic  7.42 us (7%)
    pallas_call x1, Pallas kernels, run_stencil(): pl.pallas_call(functools.partial(stencil_kernel, nw, nn), grid=(steps,),...  42.3 us
    pallas_call x1, Pallas kernels, gather_tiles(): pl.pallas_call(functools.partial(gather_kernel, nn, ccx), in_specs=[vmem,...  18.2 us
    pallas_call x1, Pallas kernels, exchange_halos(): pl.pallas_call(functools.partial(halo_kernel, nw, nn), in_specs=[vmem] *...  16 us
    pallas_call x1, Pallas kernels, scale_rows(): pl.pallas_call(scale_kernel, grid=(cx // SCALE_ROWS,), in_specs=[pl.Block...  7.11 us
    broadcast_in_dim x1, local copies, waits for them, and re-layouts, local(): jnp.broadcast_to(gh_ext[0][:, :, None], (cells_x + 2 * h, width, columns))  6.89 us

profile of v9, /device:TPU:1, one launch (start us, length us, event | category | flops | bytes accessed | tf_op | source)
XLA Modules:
  0.0 113.3 jit_solution(12000745005173362483)
XLA Ops:
  0.0 1.3 %reshape.50.par_ref = s32[1,256]{1,0:T(1,128)} reshape(s32[16,16]{1,0:T(8,128)} %param.9) | data formatting | bytes 2048 | tf_op jit(solution)/shard_map/reshape | solution.py:255
  1.3 0.7 pad_clamp_fusion
  2.0 0.7 convert_element_type.15
  2.7 0.1 broadcast_in_dim.60
  2.8 0.1 broadcast_in_dim.61
  2.9 0.1 broadcast_in_dim.55
  2.9 0.1 broadcast_in_dim.56
  3.0 0.1 copy.32
  3.1 0.1 copy.33
  3.2 0.1 copy.35
  3.3 0.1 copy.36
  3.4 0.9 multiply_bitcast_fusion
  4.3 0.1 copy.37
  4.3 0.1 copy.38
  4.4 0.6 fusion.7
  5.0 0.7 fusion.11
  5.7 0.1 fusion.15
  5.8 0.1 copy.43
  5.9 0.1 copy.41
  5.9 18.2 %shard_map.64 = f32[128,256]{1,0:T(8,128)} custom-call(s32[1,256]{1,0:T(1,128)} %reshape.50.par_ref, bf16[1024,128]{1,0:T(8,128)(2,1)} %bitcast.46), custom_call_target="tpu_custom_call" | custom-call | tf_op jit(solution)/shard_map/pallas_call | solution.py:259
  24.1 1.0 copy.34
  25.1 0.1 fusion.5
  25.2 0.7 copy.46.refs_7_
  25.9 0.7 copy.45.refs_5_
  26.6 1.1 %fusion.12 = (bf16[128,3,128]{2,1,0:T(4,128)(2,1)S(1)}, bf16[128,3,128]{2,1,0:T(4,128)(2,1)S(1)}) fusion(bf16[128,128,128]{2,1,0:T(8,128)(2,1)} %det_ref.1), kind=kLoop, calls=%fused_computation.52 | loop fusion | bytes 393216 | tf_op jit(solution)/shard_map/slice | solution.py:388
  27.7 0.3 bitcast_multiply_fusion.cm_ref
  28.1 0.0 copy-start
  28.1 1.3 %multiply_add_fusion = (f32[3,128,128]{2,1,0:T(8,128)S(1)}, f32[3,128,128]{2,1,0:T(8,128)S(1)}) fusion(bf16[128,128,128]{2,1,0:T(8,128)(2,1)} %det_ref.1, f32[128]{0:T(128)S(1)} %broadcast_in_dim.61, f32[128,128]{1,0:T(8,128)S(1)} %get-tuple-element.47, f32[128]{0:T(128)S(1)} %broadcast_in_dim.56, f32[128,128]{1,0:T(8,128)S(1)} %get-tuple-element.48), kind=kLoop, calls=%fused_computation.25 | loop fusion | flops 294912 | bytes 721920 | tf_op jit(solution)/shard_map/add | solution.py:384
  29.4 0.0 copy-start.1
  29.4 0.0 copy-start.2
  29.4 0.7 fusion.13
  30.1 1.3 %broadcast_in_dim.53.m_ref = f32[16,128,128]{2,1,0:T(8,128)} broadcast(f32[16,128]{1,0:T(8,128)S(1)} %copy.33), dimensions={0,1} | broadcast | bytes 1056768 | tf_op jit(solution)/shard_map/broadcast_in_dim | solution.py:380
  31.4 0.6 copy.39
  32.0 1.2 %broadcast_bitcast_fusion = f32[128,128,128]{2,0,1:T(8,128)S(1)} fusion(f32[16,128,128]{2,0,1:T(8,128)S(1)} %copy.39), kind=kLoop, calls=%fused_computation.1 | loop fusion | bytes 9437184 | tf_op jit(solution)/shard_map/reshape | solution.py:386
  33.2 0.9 fusion
  34.1 0.0 copy-done.1
  34.1 0.0 copy-done.2
  34.1 16.0 %shard_map.65 = (f32[3,128,128]{2,1,0:T(8,128)}, f32[2,3,128]{2,1,0:T(4,128)}, f32[3,128,128]{2,1,0:T(8,128)}, f32[2,3,128]{2,1,0:T(4,128)}, f32[3,128,128]{2,1,...) custom-call(f32[3,128,128]{2,1,0:T(8,128)} %copy-done.2, ...), custom_call_target="tpu_custom_call" | custom-call | tf_op jit(solution)/shard_map/pallas_call | solution.py:343
  50.1 0.8 concatenate.12
  50.9 0.8 concatenate.14
  51.7 0.8 copy.47
  52.5 0.8 copy.48
  53.3 0.2 concatenate.13
  53.6 0.0 copy-done
  53.6 0.6 gather_fusion
  54.2 1.5 %broadcast_in_dim.67.h_ref = f32[18,144,128]{2,1,0:T(8,128)} broadcast(f32[18,144]{1,0:T(8,128)S(1)} %gather_fusion), dimensions={0,1} | broadcast | bytes 1337472 | tf_op jit(solution)/shard_map/broadcast_in_dim | solution.py:440
  55.7 6.9 %broadcast_in_dim.65.g_ref = f32[134,144,128]{2,1,0:T(8,128)} broadcast(f32[134,144]{1,0:T(8,128)S(1)} %get-tuple-element.50), dimensions={0,1} | broadcast | bytes 9956736 | tf_op jit(solution)/shard_map/broadcast_in_dim | solution.py:438
  62.6 42.3 %shard_map.66 = (f32[128,128,128]{2,1,0:T(8,128)}, f32[1,128]{1,0:T(1,128)}) custom-call(bf16[128,128,128]{2,1,0:T(8,128)(2,1)} %det_ref.1, f32[16,128,128]{2,1,0:T(8,128)} %copy-done, f32[16,128,128]{2,1,0:T(8,128)} %broadcast_in_dim.53.m_ref, f32[3,128,128]{2,1,0:T(8,128)} %get-tuple-element.23.top_ref, f32[3,128,128]{2,1,0:T(8,128)} %get-tuple-element.24.bot_ref, ...), custom_call_target="tpu_custom_call" | custom-call | flops 75497472 | bytes 22462464 | tf_op jit(solution)/shard_map/pallas_call | solution.py:163
  104.9 1.3 %add_rsqrt_fusion.s_ref = f32[1,128]{1,0:T(1,128)} fusion(f32[1,128]{1,0:T(1,128)} %get-tuple-element.40), kind=kLoop, calls=%fused_computation.51 | loop fusion | flops 256 | bytes 1024 | tf_op jit(solution)/shard_map/sqrt | solution.py:443
  106.2 7.1 %shard_map.67 = f32[128,128,128]{2,1,0:T(8,128)} custom-call(f32[128,128,128]{2,1,0:T(8,128)} %get-tuple-element.39.x_ref, f32[1,128]{1,0:T(1,128)} %add_rsqrt_fusion.s_ref), custom_call_target="tpu_custom_call" | custom-call | flops 2097152 | bytes 16777216 | tf_op jit(solution)/shard_map/pallas_call | solution.py:359
  (13 shorter events, 0.2 us)
Async XLA Ops:
  28.1 25.5 %copy-start = (f32[16,128,128]{2,1,0:T(8,128)}, f32[16,128,128]{2,1,0:T(8,128)S(1)}, u32[]{:S(2)}) copy-start(f32[16,128,128]{2,1,0:T(8,128)S(1)} %bitcast_multiply_fusion.cm_ref) | copy-start | bytes 3145732
  29.4 4.7 %copy-start.1 = (f32[3,128,128]{2,1,0:T(8,128)}, f32[3,128,128]{2,1,0:T(8,128)S(1)}, u32[]{:S(2)}) copy-start(f32[3,128,128]{2,1,0:T(8,128)S(1)} %get-tuple-element.45.refs_2_) | copy-start | bytes 589828
  29.4 4.7 %copy-start.2 = (f32[3,128,128]{2,1,0:T(8,128)}, f32[3,128,128]{2,1,0:T(8,128)S(1)}, u32[]{:S(2)}) copy-start(f32[3,128,128]{2,1,0:T(8,128)S(1)} %get-tuple-element.46.refs_0_) | copy-start | bytes 589828

commit v10 on v8

--- a/solution.py
+++ b/solution.py
@@ -17,6 +17,60 @@
 RING = 16
 ROWS = 8
 SCALE_ROWS = 32
+DIRS = ((1, 0), (-1, 0), (0, 1), (0, -1), (1, 1), (1, -1), (-1, 1), (-1, -1))
+DIAGONALS = DIRS[4:]
+VERTICAL = ((1, 0), (-1, 0)) + DIAGONALS
+
+
+def inside(me_w, me_n, dw, dn, nw, nn):
+    w, n = me_w + dw, me_n + dn
+    return jnp.logical_and(jnp.logical_and(w >= 0, w < nw), jnp.logical_and(n >= 0, n < nn))
+
+
+def signal_others(barrier, me_w, me_n, nw, nn, dirs):
+    count = 0
+    for dw, dn in dirs:
+        ok = inside(me_w, me_n, dw, dn, nw, nn)
+
+        @pl.when(ok)
+        def _():
+            pl.semaphore_signal(barrier, inc=1, device_id=(jnp.clip(me_w + dw, 0, nw - 1),
+                                jnp.clip(me_n + dn, 0, nn - 1)), device_id_type=pl.DeviceIdType.MESH)
+        count = count + ok.astype(jnp.int32)
+    return count
+
+
+def halo_copy(ins, outs, send, recv, d, sign, me_w, me_n, nw, nn):
+    dw, dn = DIRS[d]
+    return pltpu.make_async_remote_copy(
+        src_ref=ins[d], dst_ref=outs[d], send_sem=send.at[d], recv_sem=recv.at[d],
+        device_id=(jnp.clip(me_w + sign * dw, 0, nw - 1), jnp.clip(me_n + sign * dn, 0, nn - 1)),
+        device_id_type=pl.DeviceIdType.MESH)
+
+
+def halo_start(ins, outs, send, recv, me_w, me_n, nw, nn):
+    for d, (dw, dn) in enumerate(DIRS):
+        @pl.when(inside(me_w, me_n, dw, dn, nw, nn))
+        def _():
+            halo_copy(ins, outs, send, recv, d, 1, me_w, me_n, nw, nn).start()
+
+
+def halo_finish(ins, outs, send, recv, me_w, me_n, nw, nn):
+    for d, (dw, dn) in enumerate(DIRS):
+        src_ok = inside(me_w, me_n, -dw, -dn, nw, nn)
+
+        @pl.when(src_ok)
+        def _():
+            halo_copy(ins, outs, send, recv, d, -1, me_w, me_n, nw, nn).wait_recv()
+
+        @pl.when(jnp.logical_not(src_ok))
+        def _():
+            outs[d][...] = jnp.zeros(outs[d].shape, outs[d].dtype)
+
+    for d, (dw, dn) in enumerate(DIRS):
+        @pl.when(inside(me_w, me_n, dw, dn, nw, nn))
+        def _():
+            halo_copy(ins, outs, send, recv, d, 1, me_w, me_n, nw, nn).wait_send()
 
 
 def shift_pairs(dw, dn, nw, nn):
@@ -39,9 +93,15 @@
     return out
 
 
-def stencil_kernel(nw, nn, det_ref, cm_ref, m_ref, top_ref, bot_ref, left_ref, right_ref,
-                   tl_ref, tr_ref, bl_ref, br_ref, g_ref, h_ref, out_ref, sq_ref, r0, r1, r2, ss_ref,
-                   part1, part2, q1, q2, s1, p1, s2, p2):
+def stencil_kernel(nw, nn, *refs):
+    nd = len(DIRS)
+    det_ref, cm_ref, m_ref = refs[:3]
+    sends = refs[3:3 + nd]
+    g_ref, h_ref, out_ref, sq_ref, r0, r1, r2, ss_ref, part1, part2, q1, q2, s1, p1, s2, p2 = \
+        refs[3 + nd:19 + nd]
+    halos = refs[19 + nd:19 + 2 * nd]
+    hs, hr = refs[19 + 2 * nd:]
+    top_ref, bot_ref, left_ref, right_ref, tl_ref, tr_ref, bl_ref, br_ref = halos
     i = pl.program_id(0)
     me_w = lax.axis_index("wide")
     me_n = lax.axis_index("narrow")
@@ -115,6 +175,10 @@
             pl.semaphore_signal(barrier, inc=1, device_id=(me_w, (me_n + k) % nn), device_id_type=mesh_id)
         for k in range(1, nw):
             pl.semaphore_signal(barrier, inc=1, device_id=((me_w + k) % nw, me_n), device_id_type=mesh_id)
+        diag = signal_others(barrier, me_w, me_n, nw, nn, DIAGONALS)
+        pl.semaphore_wait(barrier, nn - 1 + nw - 1 + diag)
+        halo_start(sends, halos, hs, hr, me_w, me_n, nw, nn)
+        halo_finish(sends, halos, hs, hr, me_w, me_n, nw, nn)
         ss_ref[...] = jnp.zeros_like(ss_ref)
         rows(c0_row, 0, 2 * HALO)
         rows(c1_row, 1, 2 * HALO - 2)
@@ -128,7 +192,6 @@
 
     @pl.when(i == pl.num_programs(0) - 1)
     def _():
-        pl.semaphore_wait(barrier, nn - 1 + nw - 1)
         part1[...] = jnp.sum(ss_ref[...], axis=0, keepdims=True)
         part2[...] = exchange_sum(part1, q1, s1, p1, me_n, nn, lambda j: (me_w, j))
         sq_ref[...] = exchange_sum(part2, q2, s2, p2, me_w, nw, lambda j: (j, me_n))
@@ -154,7 +217,7 @@
     return jnp.sum(slots[...], axis=0)
 
 
-def run_stencil(det, cm, m, halos, g, h, nw, nn):
+def run_stencil(det, cm, m, sends, g, h, nw, nn):
     cx, cy, k = det.shape
     width = g.shape[1]
     steps = cx // ROWS
@@ -163,7 +226,7 @@
     return pl.pallas_call(
         functools.partial(stencil_kernel, nw, nn),
         grid=(steps,),
-        in_specs=[vmem] * 13,
+        in_specs=[vmem] * (5 + len(sends)),
         out_specs=[
             pl.BlockSpec((ROWS, cy, k), lambda i: (i, 0, 0)),
             pl.BlockSpec((1, k), lambda i: (0, 0)),
@@ -182,6 +245,9 @@
             pltpu.SemaphoreType.DMA((nn,)),
             pltpu.SemaphoreType.DMA((nw,)),
             pltpu.SemaphoreType.DMA((nw,)),
+        ] + [pltpu.VMEM(p.shape, p.dtype) for p in sends] + [
+            pltpu.SemaphoreType.DMA((len(sends),)),
+            pltpu.SemaphoreType.DMA((len(sends),)),
         ],
         compiler_params=pltpu.CompilerParams(
             dimension_semantics=("arbitrary",), vmem_limit_bytes=56 * 1024 * 1024,
@@ -190,17 +256,25 @@
         cost_estimate=pl.CostEstimate(
             flops=ops, transcendentals=0, bytes_accessed=det.size * 2 + cx * cy * k * 4 + g.size * 4
         ),
-    )(det, cm, m, *halos, g, h)
-
-
-def gather_kernel(nn, cols, par_ref, ct_ref, o_ref, pslots, stage, tslots, ps, pq, ts, tq):
+    )(det, cm, m, *sends, g, h)
+
+
+def gather_kernel(nw, nn, cols, *refs):
+    nd = len(DIRS)
+    par_ref, ct_ref = refs[:2]
+    gh_in = refs[2:2 + nd]
+    o_ref = refs[2 + nd]
+    gh_out = refs[3 + nd:3 + 2 * nd]
+    pslots, stage, tslots, ps, pq, ts, tq, hs, hr = refs[3 + 2 * nd:]
     me_w = lax.axis_index("wide")
     me_n = lax.axis_index("narrow")
     mesh_id = pl.DeviceIdType.MESH
     barrier = pltpu.get_barrier_semaphore()
     for k in range(1, nn):
         pl.semaphore_signal(barrier, inc=1, device_id=(me_w, (me_n + k) % nn), device_id_type=mesh_id)
-    pl.semaphore_wait(barrier, nn - 1)
+    extra = signal_others(barrier, me_w, me_n, nw, nn, VERTICAL)
+    pl.semaphore_wait(barrier, nn - 1 + extra)
+    halo_start(gh_in, gh_out, hs, hr, me_w, me_n, nw, nn)
 
     def par_copy(k, other, slot):
         return pltpu.make_async_remote_copy(
@@ -244,23 +318,25 @@
             device_id=(me_w, other), device_id_type=mesh_id).wait_recv()
     for c in sent + out_copies:
         c.wait_send()
+    halo_finish(gh_in, gh_out, hs, hr, me_w, me_n, nw, nn)
     total = tslots[0].astype(jnp.float32)
     for j in range(1, nn):
         total = total + tslots[j].astype(jnp.float32)
     o_ref[...] = total
 
 
-def gather_tiles(parents, coarse, nn):
+def gather_tiles(parents, coarse, gh_pieces, nw, nn):
     ccx, ccy, k = coarse.shape
     par = parents.reshape(1, -1)
     n_t = par.shape[-1]
     ct = coarse.reshape(ccx * ccy, k)
     vmem = pl.BlockSpec(memory_space=pltpu.VMEM)
     return pl.pallas_call(
-        functools.partial(gather_kernel, nn, ccx),
-        in_specs=[vmem, vmem],
-        out_specs=vmem,
-        out_shape=jax.ShapeDtypeStruct((k, n_t), jnp.float32),
+        functools.partial(gather_kernel, nw, nn, ccx),
+        in_specs=[vmem] * (2 + len(gh_pieces)),
+        out_specs=[vmem] * (1 + len(gh_pieces)),
+        out_shape=[jax.ShapeDtypeStruct((k, n_t), jnp.float32)]
+        + [jax.ShapeDtypeStruct(p.shape, p.dtype) for p in gh_pieces],
         scratch_shapes=[
             pltpu.VMEM((nn, 1, n_t), jnp.int32),
             pltpu.VMEM((nn, k, n_t), jnp.bfloat16),
@@ -269,85 +345,11 @@
             pltpu.SemaphoreType.DMA((nn,)),
             pltpu.SemaphoreType.DMA((nn,)),
             pltpu.SemaphoreType.DMA((nn,)),
+            pltpu.SemaphoreType.DMA((len(gh_pieces),)),
+            pltpu.SemaphoreType.DMA((len(gh_pieces),)),
         ],
         compiler_params=pltpu.CompilerParams(collective_id=1, has_side_effects=True),
-    )(par, ct)
-
-
-DIRS = ((1, 0), (-1, 0), (0, 1), (0, -1), (1, 1), (1, -1), (-1, 1), (-1, -1))
-
-
-def halo_kernel(nw, nn, *refs):
-    nd = len(DIRS)
-    ins, outs = refs[:2 * nd], refs[2 * nd:4 * nd]
-    send, recv = refs[4 * nd], refs[4 * nd + 1]
-    me_w = lax.axis_index("wide")
-    me_n = lax.axis_index("narrow")
-    mesh_id = pl.DeviceIdType.MESH
-
-    def inside(dw, dn, sign):
-        w, n = me_w + sign * dw, me_n + sign * dn
-        return jnp.logical_and(jnp.logical_and(w >= 0, w < nw), jnp.logical_and(n >= 0, n < nn))
-
-    def clamp(v, n):
-        return jnp.clip(v, 0, n - 1)
-
-    barrier = pltpu.get_barrier_semaphore()
-    count = 0
-    for dw, dn in DIRS:
-        ok = inside(dw, dn, 1)
-
-        @pl.when(ok)
-        def _():
-            pl.semaphore_signal(barrier, inc=1, device_id=(clamp(me_w + dw, nw), clamp(me_n + dn, nn)),
-                                device_id_type=mesh_id)
-        count = count + ok.astype(jnp.int32)
-    pl.semaphore_wait(barrier, count)
-
-    def copy(d, p, sign):
-        dw, dn = DIRS[d]
-        j = 2 * d + p
-        return pltpu.make_async_remote_copy(
-            src_ref=ins[j], dst_ref=outs[j], send_sem=send.at[j], recv_sem=recv.at[j],
-            device_id=(clamp(me_w + sign * dw, nw), clamp(me_n + sign * dn, nn)), device_id_type=mesh_id)
-
-    for d, (dw, dn) in enumerate(DIRS):
-        @pl.when(inside(dw, dn, 1))
-        def _():
-            for p in range(2):
-                copy(d, p, 1).start()
-
-    for d, (dw, dn) in enumerate(DIRS):
-        src_ok = inside(dw, dn, -1)
-
-        @pl.when(src_ok)
-        def _():
-            for p in range(2):
-                copy(d, p, -1).wait_recv()
-
-        @pl.when(jnp.logical_not(src_ok))
-        def _():
-            for p in range(2):
-                outs[2 * d + p][...] = jnp.zeros(outs[2 * d + p].shape, outs[2 * d + p].dtype)
-
-    for d, (dw, dn) in enumerate(DIRS):
-        @pl.when(inside(dw, dn, 1))
-        def _():
-            for p in range(2):
-                copy(d, p, 1).wait_send()
-
-
-def exchange_halos(pieces, nw, nn):
-    vmem = pl.BlockSpec(memory_space=pltpu.VMEM)
-    n = len(pieces)
-    return pl.pallas_call(
-        functools.partial(halo_kernel, nw, nn),
-        in_specs=[vmem] * n,
-        out_specs=[vmem] * n,
-        out_shape=[jax.ShapeDtypeStruct(p.shape, p.dtype) for p in pieces],
-        scratch_shapes=[pltpu.SemaphoreType.DMA((n,)), pltpu.SemaphoreType.DMA((n,))],
-        compiler_params=pltpu.CompilerParams(collective_id=2, has_side_effects=True),
-    )(*pieces)
+    )(par, ct, *gh_pieces)
 
 
 def scale_kernel(x_ref, s_ref, o_ref):
@@ -373,21 +375,7 @@
     total_cells = cells_x * nw * cells_y * nn
     mask_float = tile_mask.astype(jnp.float32)
 
-    tile_values = gather_tiles(parents, coarse, nn).T
-    tv = tile_values.reshape(tiles_x, tiles_y, columns)
-
-    m_rows = jnp.repeat(mask_float, TS, axis=1)
-    m0 = jnp.broadcast_to(m_rows[:, :, None], (tiles_x, cells_y, columns))
-    cm0 = m0 * jnp.repeat(tv, TS, axis=1)
-
     h = HALO
-    c0_top = cm0[0][None] + m0[0][None] * detail[:h].astype(jnp.float32)
-    c0_bot = cm0[-1][None] + m0[-1][None] * detail[-h:].astype(jnp.float32)
-    cm_rep = jnp.repeat(cm0, TS, axis=0)
-    m_rep = jnp.repeat(m0, TS, axis=0)
-    c0_left = cm_rep[:, :h] + m_rep[:, :h] * detail[:, :h].astype(jnp.float32)
-    c0_right = cm_rep[:, -h:] + m_rep[:, -h:] * detail[:, -h:].astype(jnp.float32)
-
     cell_mask = jnp.repeat(jnp.repeat(mask_float, TS, axis=0), TS, axis=1)
     g_own = (cell_mask * (4.0 + diagonal) - CENTER) / HALF_WIDTH
     h_own = cell_mask / HALF_WIDTH
@@ -405,20 +393,33 @@
             idx[cols_axis] = slice(0, h)
         return a[tuple(idx)]
 
+    gh_pieces = []
+    for dw, dn in DIRS:
+        e = edge(gh, dw, dn, 1, 2)
+        gh_pieces.append(e.transpose(0, 2, 1) if dw == 0 else e)
+    got = gather_tiles(parents, coarse, gh_pieces, nw, nn)
+    tile_values = got[0].T
+    hg = {dirn: got[1 + k] for k, dirn in enumerate(DIRS)}
+    for dirn in ((0, 1), (0, -1)):
+        hg[dirn] = hg[dirn].transpose(0, 2, 1)
+    tv = tile_values.reshape(tiles_x, tiles_y, columns)
+
+    m_rows = jnp.repeat(mask_float, TS, axis=1)
+    m0 = jnp.broadcast_to(m_rows[:, :, None], (tiles_x, cells_y, columns))
+    cm0 = m0 * jnp.repeat(tv, TS, axis=1)
+
+    c0_top = cm0[0][None] + m0[0][None] * detail[:h].astype(jnp.float32)
+    c0_bot = cm0[-1][None] + m0[-1][None] * detail[-h:].astype(jnp.float32)
+    cm_rep = jnp.repeat(cm0, TS, axis=0)
+    m_rep = jnp.repeat(m0, TS, axis=0)
+    c0_left = cm_rep[:, :h] + m_rep[:, :h] * detail[:, :h].astype(jnp.float32)
+    c0_right = cm_rep[:, -h:] + m_rep[:, -h:] * detail[:, -h:].astype(jnp.float32)
     c0_pieces = {
         (1, 0): c0_bot, (-1, 0): c0_top,
         (0, 1): c0_right.transpose(1, 0, 2), (0, -1): c0_left.transpose(1, 0, 2),
         (1, 1): c0_bot[:, -h:], (1, -1): c0_bot[:, :h], (-1, 1): c0_top[:, -h:], (-1, -1): c0_top[:, :h],
     }
-    pieces = []
-    for dw, dn in DIRS:
-        pieces.append(c0_pieces[(dw, dn)])
-        pieces.append(edge(gh, dw, dn, 1, 2))
-    got = exchange_halos(pieces, nw, nn)
-    hc = {dirn: got[2 * k] for k, dirn in enumerate(DIRS)}
-    hg = {dirn: got[2 * k + 1] for k, dirn in enumerate(DIRS)}
-    halos = [hc[(1, 0)], hc[(-1, 0)], hc[(0, 1)], hc[(0, -1)],
-             hc[(1, 1)], hc[(1, -1)], hc[(-1, 1)], hc[(-1, -1)]]
+    sends = [c0_pieces[dirn] for dirn in DIRS]
 
     rpad = LPAD - h
     z3 = jnp.zeros((2, h, rpad), jnp.float32)
@@ -436,7 +437,7 @@
     h_rows = gh_ext[1][jnp.array([0] + [h + TS * t for t in range(tiles_x)] + [h + cells_x])]
     h_b = jnp.broadcast_to(h_rows[:, :, None], (tiles_x + 2, width, columns))
 
-    cheb_three, squares = run_stencil(detail, cm0, m0, halos, g_b, h_b, nw, nn)
+    cheb_three, squares = run_stencil(detail, cm0, m0, sends, g_b, h_b, nw, nn)
     inv = 1.0 / jnp.sqrt(squares / total_cells + EPSILON)
     return scale_rows(cheb_three, inv)
 

time: 118 us -> 112 us (0.949)
  Pallas kernels: 89.2 us -> 81.5 us
  local copies, waits for them, and re-layouts: 20.1 us -> 22.1 us
    pallas_call x2 -> x1, Pallas kernels: 39.8 us -> 17.6 us  [gather_tiles(): pl.pallas_call(functools.partial(gather_kernel, nw, nn, ccx), in_specs=[v...]
    pallas_call x1, Pallas kernels: 42.3 us -> 56.8 us  [run_stencil(): pl.pallas_call(functools.partial(stencil_kernel, nw, nn), grid=(steps,),...]
    pallas_call x0 -> x2, local copies, waits for them, and re-layouts: none -> 1.62 us  [gather_tiles(): pl.pallas_call(functools.partial(gather_kernel, nw, nn, ccx), in_specs=[v...]
    transpose x1 -> x3, local copies, waits for them, and re-layouts: 0.99 us -> 2.34 us  [the longest x2 1.34 us: local(): gh_pieces.append(e.transpose(0, 2, 1) if dw == 0 else e)]
    another operation x5 -> x4, other arithmetic: 2.91 us -> 2.16 us  [local(): gh = jnp.stack([g_own, h_own])]
where the time goes in v10:
time: 112 us; the launch traced here: 111 us
  Pallas kernels  81.5 us (73%)
  local copies, waits for them, and re-layouts  22.1 us (20%)
  other arithmetic  7.45 us (7%)
    pallas_call x1, Pallas kernels, run_stencil(): pl.pallas_call(functools.partial(stencil_kernel, nw, nn), grid=(steps,),...  56.8 us
    pallas_call x1, Pallas kernels, gather_tiles(): pl.pallas_call(functools.partial(gather_kernel, nw, nn, ccx), in_specs=[v...  17.6 us
    pallas_call x1, Pallas kernels, scale_rows(): pl.pallas_call(scale_kernel, grid=(cx // SCALE_ROWS,), in_specs=[pl.Block...  7.11 us
    broadcast_in_dim x1, local copies, waits for them, and re-layouts, local(): jnp.broadcast_to(gh_ext[0][:, :, None], (cells_x + 2 * h, width, columns))  6.89 us

profile of v10, /device:TPU:1, one launch (start us, length us, event | category | flops | bytes accessed | tf_op | source)
XLA Modules:
  0.0 111.2 jit_solution(5628487211262433310)
XLA Ops:
  0.0 1.4 %reshape.50.refs_0_ = s32[1,256]{1,0:T(1,128)} reshape(s32[16,16]{1,0:T(8,128)} %param.9) | data formatting | bytes 2048 | tf_op jit(solution)/shard_map/reshape | solution.py:330
  1.4 0.7 pad_clamp_fusion
  2.0 0.7 convert_element_type.15
  2.7 0.1 broadcast_in_dim.60
  2.8 0.1 broadcast_in_dim.61
  2.9 0.1 broadcast_in_dim.58
  3.0 0.1 broadcast_in_dim.59
  3.1 0.1 copy.32
  3.1 0.1 copy.33
  3.2 0.1 copy.36
  3.3 0.1 copy.37
  3.4 0.1 copy.34
  3.5 0.1 copy.35
  3.6 0.9 multiply_bitcast_fusion
  4.5 0.6 fusion.7
  5.1 0.7 fusion.11
  5.7 0.1 fusion.15
  5.8 0.1 copy.45
  5.9 0.1 copy.43
  6.0 0.1 fusion.5
  6.1 0.7 copy.39.refs_5_
  6.8 0.7 copy.38.refs_4_
  7.4 17.6 %shard_map.64 = (f32[128,256]{1,0:T(8,128)}, f32[2,3,128]{2,1,0:T(4,128)}, f32[2,3,128]{2,1,0:T(4,128)}, f32[2,3,128]{2,1,0:T(4,128)}, f32[2,3,128]{2,1,0:T(4,12...) custom-call(s32[1,256]{1,0:T(1,128)} %reshape.50.refs_0_, ...), custom_call_target="tpu_custom_call" | custom-call | tf_op jit(solution)/shard_map/pallas_call | solution.py:334
  25.1 1.0 copy.40
  26.1 0.8 concatenate.12
  26.9 0.8 concatenate.14
  27.6 0.8 copy.47
  28.4 0.8 copy.48
  29.3 0.2 concatenate.13
  29.6 0.6 gather_fusion
  30.2 1.1 %fusion.12 = (bf16[128,3,128]{2,1,0:T(4,128)(2,1)S(1)}, bf16[128,3,128]{2,1,0:T(4,128)(2,1)S(1)}) fusion(bf16[128,128,128]{2,1,0:T(8,128)(2,1)} %refs_0_.1), kind=kLoop, calls=%fused_computation.52 | loop fusion | bytes 393216 | tf_op jit(solution)/shard_map/slice | solution.py:415
  31.3 0.3 bitcast_multiply_fusion.refs_1_
  31.7 0.0 copy-start
  31.7 1.3 %multiply_add_fusion = (f32[3,128,128]{2,1,0:T(8,128)S(1)}, f32[3,128,128]{2,1,0:T(8,128)S(1)}) fusion(bf16[128,128,128]{2,1,0:T(8,128)(2,1)} %refs_0_.1, f32[128]{0:T(128)S(1)} %broadcast_in_dim.61, f32[128,128]{1,0:T(8,128)S(1)} %get-tuple-element.33, f32[128]{0:T(128)S(1)} %broadcast_in_dim.59, f32[128,128]{1,0:T(8,128)S(1)} %get-tuple-element.34), kind=kLoop, calls=%fused_computation.25 | loop fusion | flops 294912 | bytes 721920 | tf_op jit(solution)/shard_map/add | solution.py:411
  33.0 0.0 copy-start.1
  33.0 0.0 copy-start.2
  33.0 0.7 fusion.13
  33.7 1.3 %broadcast_in_dim.53.refs_2_ = f32[16,128,128]{2,1,0:T(8,128)} broadcast(f32[16,128]{1,0:T(8,128)S(1)} %copy.33), dimensions={0,1} | broadcast | bytes 1056768 | tf_op jit(solution)/shard_map/broadcast_in_dim | solution.py:408
  35.0 0.6 copy.41
  35.6 1.5 %broadcast_in_dim.67.refs_12_ = f32[18,144,128]{2,1,0:T(8,128)} broadcast(f32[18,144]{1,0:T(8,128)S(1)} %gather_fusion), dimensions={0,1} | broadcast | bytes 1337472 | tf_op jit(solution)/shard_map/broadcast_in_dim | solution.py:438
  37.1 1.1 %broadcast_bitcast_fusion = f32[128,128,128]{2,0,1:T(8,128)S(1)} fusion(f32[16,128,128]{2,0,1:T(8,128)S(1)} %copy.41), kind=kLoop, calls=%fused_computation.1 | loop fusion | bytes 9437184 | tf_op jit(solution)/shard_map/reshape | solution.py:413
  38.3 0.9 fusion
  39.2 6.9 %broadcast_in_dim.65.refs_11_ = f32[134,144,128]{2,1,0:T(8,128)} broadcast(f32[134,144]{1,0:T(8,128)S(1)} %get-tuple-element.36), dimensions={0,1} | broadcast | bytes 9956736 | tf_op jit(solution)/shard_map/broadcast_in_dim | solution.py:436
  46.1 0.0 copy-done
  46.1 0.0 copy-done.1
  46.1 0.0 copy-done.2
  46.1 56.8 %shard_map.65 = (f32[128,128,128]{2,1,0:T(8,128)}, f32[1,128]{1,0:T(1,128)}) custom-call(bf16[128,128,128]{2,1,0:T(8,128)(2,1)} %refs_0_.1, f32[16,128,128]{2,1,0:T(8,128)} %copy-done, f32[16,128,128]{2,1,0:T(8,128)} %broadcast_in_dim.53.refs_2_, f32[3,128,128]{2,1,0:T(8,128)} %copy-done.2, f32[3,128,128]{2,1,0:T(8,128)} %copy-done.1, ...), custom_call_target="tpu_custom_call" | custom-call | flops 75497472 | bytes 22462464 | tf_op jit(solution)/shard_map/pallas_call | solution.py:226
  102.9 1.3 %add_rsqrt_fusion.s_ref = f32[1,128]{1,0:T(1,128)} fusion(f32[1,128]{1,0:T(1,128)} %get-tuple-element.26), kind=kLoop, calls=%fused_computation.51 | loop fusion | flops 256 | bytes 1024 | tf_op jit(solution)/shard_map/sqrt | solution.py:441
  104.1 7.1 %shard_map.66 = f32[128,128,128]{2,1,0:T(8,128)} custom-call(f32[128,128,128]{2,1,0:T(8,128)} %get-tuple-element.25.x_ref, f32[1,128]{1,0:T(1,128)} %add_rsqrt_fusion.s_ref), custom_call_target="tpu_custom_call" | custom-call | flops 2097152 | bytes 16777216 | tf_op jit(solution)/shard_map/pallas_call | solution.py:361
  (13 shorter events, 0.2 us)
Async XLA Ops:
  31.7 14.4 %copy-start = (f32[16,128,128]{2,1,0:T(8,128)}, f32[16,128,128]{2,1,0:T(8,128)S(1)}, u32[]{:S(2)}) copy-start(f32[16,128,128]{2,1,0:T(8,128)S(1)} %bitcast_multiply_fusion.refs_1_) | copy-start | bytes 3145732
  33.0 13.1 %copy-start.1 = (f32[3,128,128]{2,1,0:T(8,128)}, f32[3,128,128]{2,1,0:T(8,128)S(1)}, u32[]{:S(2)}) copy-start(f32[3,128,128]{2,1,0:T(8,128)S(1)} %get-tuple-element.31.refs_4_) | copy-start | bytes 589828
  33.0 13.1 %copy-start.2 = (f32[3,128,128]{2,1,0:T(8,128)}, f32[3,128,128]{2,1,0:T(8,128)S(1)}, u32[]{:S(2)}) copy-start(f32[3,128,128]{2,1,0:T(8,128)S(1)} %get-tuple-element.32.refs_3_) | copy-start | bytes 589828

commit v11 on v10

--- a/solution.py
+++ b/solution.py
@@ -16,7 +16,7 @@
 LPAD = 8
 RING = 16
 ROWS = 8
-SCALE_ROWS = 32
+SCALE_ROWS = 64
 DIRS = ((1, 0), (-1, 0), (0, 1), (0, -1), (1, 1), (1, -1), (-1, 1), (-1, -1))
 DIAGONALS = DIRS[4:]
 VERTICAL = ((1, 0), (-1, 0)) + DIAGONALS
@@ -393,15 +393,13 @@
             idx[cols_axis] = slice(0, h)
         return a[tuple(idx)]
 
+    gh_t = gh.transpose(0, 2, 1)
     gh_pieces = []
     for dw, dn in DIRS:
-        e = edge(gh, dw, dn, 1, 2)
-        gh_pieces.append(e.transpose(0, 2, 1) if dw == 0 else e)
+        gh_pieces.append(edge(gh_t, dn, dw, 1, 2) if dw == 0 else edge(gh, dw, dn, 1, 2))
     got = gather_tiles(parents, coarse, gh_pieces, nw, nn)
     tile_values = got[0].T
     hg = {dirn: got[1 + k] for k, dirn in enumerate(DIRS)}
-    for dirn in ((0, 1), (0, -1)):
-        hg[dirn] = hg[dirn].transpose(0, 2, 1)
     tv = tile_values.reshape(tiles_x, tiles_y, columns)
 
     m_rows = jnp.repeat(mask_float, TS, axis=1)
@@ -427,7 +425,8 @@
     gh_ext = jnp.concatenate(
         [
             jnp.concatenate([z3, hg[(1, 1)], hg[(1, 0)], hg[(1, -1)], z3], axis=2),
-            jnp.concatenate([zc, hg[(0, 1)], gh, hg[(0, -1)], zc], axis=2),
+            jnp.concatenate([zc.transpose(0, 2, 1), hg[(0, 1)], gh_t, hg[(0, -1)], zc.transpose(0, 2, 1)],
+                            axis=1).transpose(0, 2, 1),
             jnp.concatenate([z3, hg[(-1, 1)], hg[(-1, 0)], hg[(-1, -1)], z3], axis=2),
         ],
         axis=1,

time: 112 us -> 110 us (0.982)
  Pallas kernels: 81.5 us -> 80.2 us
    slice x0 -> x3, local copies, waits for them, and re-layouts: none -> 1.46 us  [edge(): return a[tuple(idx)]]
    transpose x2 -> x0, local copies, waits for them, and re-layouts: 1.34 us -> none  [local(): gh_pieces.append(e.transpose(0, 2, 1) if dw == 0 else e)]
    pallas_call x1, Pallas kernels: 7.11 us -> 5.86 us  [scale_rows(): pl.pallas_call(scale_kernel, grid=(cx // SCALE_ROWS,), in_specs=[pl.Block...]
where the time goes in v11:
time: 110 us
  Pallas kernels  80.2 us (73%)
  local copies, waits for them, and re-layouts  22.2 us (20%)
  other arithmetic  7.34 us (7%)
    pallas_call x1, Pallas kernels, run_stencil(): pl.pallas_call(functools.partial(stencil_kernel, nw, nn), grid=(steps,),...  56.8 us
    pallas_call x1, Pallas kernels, gather_tiles(): pl.pallas_call(functools.partial(gather_kernel, nw, nn, ccx), in_specs=[v...  17.6 us
    broadcast_in_dim x1, local copies, waits for them, and re-layouts, local(): jnp.broadcast_to(gh_ext[0][:, :, None], (cells_x + 2 * h, width, columns))  6.89 us
    pallas_call x1, Pallas kernels, scale_rows(): pl.pallas_call(scale_kernel, grid=(cx // SCALE_ROWS,), in_specs=[pl.Block...  5.86 us

profile of v11, /device:TPU:1, one launch (start us, length us, event | category | flops | bytes accessed | tf_op | source)
XLA Modules:
  0.0 110.0 jit_solution(7014585052155190132)
XLA Ops:
  0.0 1.4 %reshape.50.refs_0_ = s32[1,256]{1,0:T(1,128)} reshape(s32[16,16]{1,0:T(8,128)} %param.9) | data formatting | bytes 2048 | tf_op jit(solution)/shard_map/reshape | solution.py:330
  1.4 0.7 pad_clamp_fusion
  2.0 0.7 convert_element_type.15
  2.7 0.1 broadcast_in_dim.57
  2.8 0.1 broadcast_in_dim.58
  2.9 0.1 broadcast_in_dim.55
  3.0 0.1 broadcast_in_dim.56
  3.1 0.1 copy.32
  3.1 0.1 copy.33
  3.2 0.1 copy.36
  3.3 0.1 copy.37
  3.4 0.1 copy.34
  3.5 0.1 copy.35
  3.6 0.9 multiply_bitcast_fusion
  4.5 0.6 fusion.4
  5.1 0.7 fusion.8
  5.8 0.1 fusion.13
  5.8 0.1 copy.45
  5.9 0.1 copy.43
  6.0 0.1 fusion.12
  6.1 0.7 copy.39.refs_5_
  6.8 0.7 copy.38.refs_4_
  7.4 17.6 %shard_map.64 = (f32[128,256]{1,0:T(8,128)}, f32[2,3,128]{2,1,0:T(4,128)}, f32[2,3,128]{2,1,0:T(4,128)}, f32[2,3,128]{2,1,0:T(4,128)}, f32[2,3,128]{2,1,0:T(4,12...) custom-call(s32[1,256]{1,0:T(1,128)} %reshape.50.refs_0_, ...), custom_call_target="tpu_custom_call" | custom-call | tf_op jit(solution)/shard_map/pallas_call | solution.py:334
  25.1 1.0 copy.40
  26.1 0.8 concatenate.12
  26.9 0.8 concatenate.14
  27.6 0.8 copy.47
  28.4 0.8 copy.48
  29.3 0.2 concatenate.13
  29.6 0.6 gather_fusion
  30.2 1.1 %fusion.9 = (bf16[128,3,128]{2,1,0:T(4,128)(2,1)S(1)}, bf16[128,3,128]{2,1,0:T(4,128)(2,1)S(1)}) fusion(bf16[128,128,128]{2,1,0:T(8,128)(2,1)} %refs_0_.1), kind=kLoop, calls=%fused_computation.45 | loop fusion | bytes 393216 | tf_op jit(solution)/shard_map/slice | solution.py:413
  31.3 0.3 bitcast_multiply_fusion.refs_1_
  31.7 0.0 copy-start
  31.7 1.3 %multiply_add_fusion = (f32[3,128,128]{2,1,0:T(8,128)S(1)}, f32[3,128,128]{2,1,0:T(8,128)S(1)}) fusion(bf16[128,128,128]{2,1,0:T(8,128)(2,1)} %refs_0_.1, f32[128]{0:T(128)S(1)} %broadcast_in_dim.58, f32[128,128]{1,0:T(8,128)S(1)} %get-tuple-element.33, f32[128]{0:T(128)S(1)} %broadcast_in_dim.56, f32[128,128]{1,0:T(8,128)S(1)} %get-tuple-element.34), kind=kLoop, calls=%fused_computation.21 | loop fusion | flops 294912 | bytes 721920 | tf_op jit(solution)/shard_map/add | solution.py:409
  33.0 0.0 copy-start.1
  33.0 0.0 copy-start.2
  33.0 0.7 fusion.10
  33.7 1.3 %broadcast_in_dim.50.refs_2_ = f32[16,128,128]{2,1,0:T(8,128)} broadcast(f32[16,128]{1,0:T(8,128)S(1)} %copy.33), dimensions={0,1} | broadcast | bytes 1056768 | tf_op jit(solution)/shard_map/broadcast_in_dim | solution.py:406
  35.0 0.6 copy.41
  35.6 1.5 %broadcast_in_dim.63.refs_12_ = f32[18,144,128]{2,1,0:T(8,128)} broadcast(f32[18,144]{1,0:T(8,128)S(1)} %gather_fusion), dimensions={0,1} | broadcast | bytes 1337472 | tf_op jit(solution)/shard_map/broadcast_in_dim | solution.py:437
  37.1 1.1 %broadcast_bitcast_fusion = f32[128,128,128]{2,0,1:T(8,128)S(1)} fusion(f32[16,128,128]{2,0,1:T(8,128)S(1)} %copy.41), kind=kLoop, calls=%fused_computation.1 | loop fusion | bytes 9437184 | tf_op jit(solution)/shard_map/reshape | solution.py:411
  38.3 0.9 fusion
  39.2 6.9 %broadcast_in_dim.61.refs_11_ = f32[134,144,128]{2,1,0:T(8,128)} broadcast(f32[134,144]{1,0:T(8,128)S(1)} %get-tuple-element.36), dimensions={0,1} | broadcast | bytes 9956736 | tf_op jit(solution)/shard_map/broadcast_in_dim | solution.py:435
  46.1 0.0 copy-done
  46.1 0.0 copy-done.1
  46.1 0.0 copy-done.2
  46.1 56.8 %shard_map.65 = (f32[128,128,128]{2,1,0:T(8,128)}, f32[1,128]{1,0:T(1,128)}) custom-call(bf16[128,128,128]{2,1,0:T(8,128)(2,1)} %refs_0_.1, f32[16,128,128]{2,1,0:T(8,128)} %copy-done, f32[16,128,128]{2,1,0:T(8,128)} %broadcast_in_dim.50.refs_2_, f32[3,128,128]{2,1,0:T(8,128)} %copy-done.2, f32[3,128,128]{2,1,0:T(8,128)} %copy-done.1, ...), custom_call_target="tpu_custom_call" | custom-call | flops 75497472 | bytes 22462464 | tf_op jit(solution)/shard_map/pallas_call | solution.py:226
  102.9 1.3 %add_rsqrt_fusion.s_ref = f32[1,128]{1,0:T(1,128)} fusion(f32[1,128]{1,0:T(1,128)} %get-tuple-element.26), kind=kLoop, calls=%fused_computation.44 | loop fusion | flops 256 | bytes 1024 | tf_op jit(solution)/shard_map/sqrt | solution.py:440
  104.1 5.9 %shard_map.66 = f32[128,128,128]{2,1,0:T(8,128)} custom-call(f32[128,128,128]{2,1,0:T(8,128)} %get-tuple-element.25.x_ref, f32[1,128]{1,0:T(1,128)} %add_rsqrt_fusion.s_ref), custom_call_target="tpu_custom_call" | custom-call | flops 2097152 | bytes 16777216 | tf_op jit(solution)/shard_map/pallas_call | solution.py:361
  (13 shorter events, 0.2 us)
Async XLA Ops:
  31.7 14.4 %copy-start = (f32[16,128,128]{2,1,0:T(8,128)}, f32[16,128,128]{2,1,0:T(8,128)S(1)}, u32[]{:S(2)}) copy-start(f32[16,128,128]{2,1,0:T(8,128)S(1)} %bitcast_multiply_fusion.refs_1_) | copy-start | bytes 3145732
  33.0 13.1 %copy-start.1 = (f32[3,128,128]{2,1,0:T(8,128)}, f32[3,128,128]{2,1,0:T(8,128)S(1)}, u32[]{:S(2)}) copy-start(f32[3,128,128]{2,1,0:T(8,128)S(1)} %get-tuple-element.31.refs_4_) | copy-start | bytes 589828
  33.0 13.1 %copy-start.2 = (f32[3,128,128]{2,1,0:T(8,128)}, f32[3,128,128]{2,1,0:T(8,128)S(1)}, u32[]{:S(2)}) copy-start(f32[3,128,128]{2,1,0:T(8,128)S(1)} %get-tuple-element.32.refs_3_) | copy-start | bytes 589828

commit v12 on v11

--- a/solution.py
+++ b/solution.py
@@ -93,7 +93,7 @@
     return out
 
 
-def stencil_kernel(nw, nn, *refs):
+def stencil_kernel(nw, nn, total_cells, *refs):
     nd = len(DIRS)
     det_ref, cm_ref, m_ref = refs[:3]
     sends = refs[3:3 + nd]
@@ -194,7 +194,8 @@
     def _():
         part1[...] = jnp.sum(ss_ref[...], axis=0, keepdims=True)
         part2[...] = exchange_sum(part1, q1, s1, p1, me_n, nn, lambda j: (me_w, j))
-        sq_ref[...] = exchange_sum(part2, q2, s2, p2, me_w, nw, lambda j: (j, me_n))
+        squares = exchange_sum(part2, q2, s2, p2, me_w, nw, lambda j: (j, me_n))
+        sq_ref[...] = 1.0 / jnp.sqrt(squares / total_cells + EPSILON)
 
 
 def exchange_sum(src, slots, send, recv, me, n, peer_of):
@@ -217,14 +218,14 @@
     return jnp.sum(slots[...], axis=0)
 
 
-def run_stencil(det, cm, m, sends, g, h, nw, nn):
+def run_stencil(det, cm, m, sends, g, h, nw, nn, total_cells):
     cx, cy, k = det.shape
     width = g.shape[1]
     steps = cx // ROWS
     vmem = pl.BlockSpec(memory_space=pltpu.VMEM)
     ops = cx * cy * k * 3 * 12
     return pl.pallas_call(
-        functools.partial(stencil_kernel, nw, nn),
+        functools.partial(stencil_kernel, nw, nn, float(total_cells)),
         grid=(steps,),
         in_specs=[vmem] * (5 + len(sends)),
         out_specs=[
@@ -436,8 +437,7 @@
     h_rows = gh_ext[1][jnp.array([0] + [h + TS * t for t in range(tiles_x)] + [h + cells_x])]
     h_b = jnp.broadcast_to(h_rows[:, :, None], (tiles_x + 2, width, columns))
 
-    cheb_three, squares = run_stencil(detail, cm0, m0, sends, g_b, h_b, nw, nn)
-    inv = 1.0 / jnp.sqrt(squares / total_cells + EPSILON)
+    cheb_three, inv = run_stencil(detail, cm0, m0, sends, g_b, h_b, nw, nn, total_cells)
     return scale_rows(cheb_three, inv)
 
 

time: 110 us -> 109 us (level)
  other arithmetic: 7.34 us -> 6.09 us
    sqrt x1 -> x0, other arithmetic: 1.25 us -> none  [local(): inv = 1.0 / jnp.sqrt(squares / total_cells + EPSILON)]
where the time goes in v12:
time: 109 us
  Pallas kernels  80.3 us (74%)
  local copies, waits for them, and re-layouts  22.2 us (20%)
  other arithmetic  6.09 us (6%)
    pallas_call x1, Pallas kernels, run_stencil(): pl.pallas_call(functools.partial(stencil_kernel, nw, nn, float(total_cell...  56.8 us
    pallas_call x1, Pallas kernels, gather_tiles(): pl.pallas_call(functools.partial(gather_kernel, nw, nn, ccx), in_specs=[v...  17.6 us
    broadcast_in_dim x1, local copies, waits for them, and re-layouts, local(): jnp.broadcast_to(gh_ext[0][:, :, None], (cells_x + 2 * h, width, columns))  6.89 us
    pallas_call x1, Pallas kernels, scale_rows(): pl.pallas_call(scale_kernel, grid=(cx // SCALE_ROWS,), in_specs=[pl.Block...  5.87 us

profile of v12, /device:TPU:1, one launch (start us, length us, event | category | flops | bytes accessed | tf_op | source)
XLA Modules:
  0.0 108.8 jit_solution(12302394430742983095)
XLA Ops:
  0.0 1.4 %reshape.50.refs_0_ = s32[1,256]{1,0:T(1,128)} reshape(s32[16,16]{1,0:T(8,128)} %param.9) | data formatting | bytes 2048 | tf_op jit(solution)/shard_map/reshape | solution.py:331
  1.4 0.7 pad_clamp_fusion
  2.0 0.7 convert_element_type.15
  2.7 0.1 broadcast_in_dim.57
  2.8 0.1 broadcast_in_dim.58
  2.9 0.1 broadcast_in_dim.55
  3.0 0.1 broadcast_in_dim.56
  3.1 0.1 copy.32
  3.1 0.1 copy.33
  3.2 0.1 copy.36
  3.3 0.1 copy.37
  3.4 0.1 copy.34
  3.5 0.1 copy.35
  3.6 0.9 multiply_bitcast_fusion
  4.5 0.6 fusion.4
  5.1 0.7 fusion.8
  5.8 0.1 fusion.13
  5.8 0.1 copy.45
  5.9 0.1 copy.43
  6.0 0.1 fusion.12
  6.1 0.7 copy.39.refs_5_
  6.8 0.7 copy.38.refs_4_
  7.4 17.6 %shard_map.64 = (f32[128,256]{1,0:T(8,128)}, f32[2,3,128]{2,1,0:T(4,128)}, f32[2,3,128]{2,1,0:T(4,128)}, f32[2,3,128]{2,1,0:T(4,128)}, f32[2,3,128]{2,1,0:T(4,12...) custom-call(s32[1,256]{1,0:T(1,128)} %reshape.50.refs_0_, ...), custom_call_target="tpu_custom_call" | custom-call | tf_op jit(solution)/shard_map/pallas_call | solution.py:335
  25.1 1.0 copy.40
  26.1 0.8 concatenate.12
  26.9 0.8 concatenate.14
  27.6 0.8 copy.47
  28.4 0.8 copy.48
  29.3 0.2 concatenate.13
  29.6 0.6 gather_fusion
  30.2 1.1 %fusion.9 = (bf16[128,3,128]{2,1,0:T(4,128)(2,1)S(1)}, bf16[128,3,128]{2,1,0:T(4,128)(2,1)S(1)}) fusion(bf16[128,128,128]{2,1,0:T(8,128)(2,1)} %refs_0_.1), kind=kLoop, calls=%fused_computation.44 | loop fusion | bytes 393216 | tf_op jit(solution)/shard_map/slice | solution.py:414
  31.3 0.3 bitcast_multiply_fusion.refs_1_
  31.7 0.0 copy-start
  31.7 1.3 %multiply_add_fusion = (f32[3,128,128]{2,1,0:T(8,128)S(1)}, f32[3,128,128]{2,1,0:T(8,128)S(1)}) fusion(bf16[128,128,128]{2,1,0:T(8,128)(2,1)} %refs_0_.1, f32[128]{0:T(128)S(1)} %broadcast_in_dim.58, f32[128,128]{1,0:T(8,128)S(1)} %get-tuple-element.33, f32[128]{0:T(128)S(1)} %broadcast_in_dim.56, f32[128,128]{1,0:T(8,128)S(1)} %get-tuple-element.34), kind=kLoop, calls=%fused_computation.21 | loop fusion | flops 294912 | bytes 721920 | tf_op jit(solution)/shard_map/add | solution.py:410
  33.0 0.0 copy-start.1
  33.0 0.0 copy-start.2
  33.0 0.7 fusion.10
  33.7 1.3 %broadcast_in_dim.50.refs_2_ = f32[16,128,128]{2,1,0:T(8,128)} broadcast(f32[16,128]{1,0:T(8,128)S(1)} %copy.33), dimensions={0,1} | broadcast | bytes 1056768 | tf_op jit(solution)/shard_map/broadcast_in_dim | solution.py:407
  35.0 0.6 copy.41
  35.6 1.5 %broadcast_in_dim.63.refs_12_ = f32[18,144,128]{2,1,0:T(8,128)} broadcast(f32[18,144]{1,0:T(8,128)S(1)} %gather_fusion), dimensions={0,1} | broadcast | bytes 1337472 | tf_op jit(solution)/shard_map/broadcast_in_dim | solution.py:438
  37.1 1.1 %broadcast_bitcast_fusion = f32[128,128,128]{2,0,1:T(8,128)S(1)} fusion(f32[16,128,128]{2,0,1:T(8,128)S(1)} %copy.41), kind=kLoop, calls=%fused_computation.1 | loop fusion | bytes 9437184 | tf_op jit(solution)/shard_map/reshape | solution.py:412
  38.3 0.9 fusion
  39.2 6.9 %broadcast_in_dim.61.refs_11_ = f32[134,144,128]{2,1,0:T(8,128)} broadcast(f32[134,144]{1,0:T(8,128)S(1)} %get-tuple-element.36), dimensions={0,1} | broadcast | bytes 9956736 | tf_op jit(solution)/shard_map/broadcast_in_dim | solution.py:436
  46.1 0.0 copy-done
  46.1 0.0 copy-done.1
  46.1 0.0 copy-done.2
  46.1 56.8 %shard_map.65 = (f32[128,128,128]{2,1,0:T(8,128)}, f32[1,128]{1,0:T(1,128)}) custom-call(bf16[128,128,128]{2,1,0:T(8,128)(2,1)} %refs_0_.1, f32[16,128,128]{2,1,0:T(8,128)} %copy-done, f32[16,128,128]{2,1,0:T(8,128)} %broadcast_in_dim.50.refs_2_, f32[3,128,128]{2,1,0:T(8,128)} %copy-done.2, f32[3,128,128]{2,1,0:T(8,128)} %copy-done.1, ...), custom_call_target="tpu_custom_call" | custom-call | flops 75497472 | bytes 22462464 | tf_op jit(solution)/shard_map/pallas_call | solution.py:227
  102.9 5.9 %shard_map.66 = f32[128,128,128]{2,1,0:T(8,128)} custom-call(f32[128,128,128]{2,1,0:T(8,128)} %get-tuple-element.25.x_ref, f32[1,128]{1,0:T(1,128)} %get-tuple-element.26.s_ref), custom_call_target="tpu_custom_call" | custom-call | flops 2097152 | bytes 16777216 | tf_op jit(solution)/shard_map/pallas_call | solution.py:362
  (13 shorter events, 0.2 us)
Async XLA Ops:
  31.7 14.4 %copy-start = (f32[16,128,128]{2,1,0:T(8,128)}, f32[16,128,128]{2,1,0:T(8,128)S(1)}, u32[]{:S(2)}) copy-start(f32[16,128,128]{2,1,0:T(8,128)S(1)} %bitcast_multiply_fusion.refs_1_) | copy-start | bytes 3145732
  33.0 13.1 %copy-start.1 = (f32[3,128,128]{2,1,0:T(8,128)}, f32[3,128,128]{2,1,0:T(8,128)S(1)}, u32[]{:S(2)}) copy-start(f32[3,128,128]{2,1,0:T(8,128)S(1)} %get-tuple-element.31.refs_4_) | copy-start | bytes 589828
  33.0 13.1 %copy-start.2 = (f32[3,128,128]{2,1,0:T(8,128)}, f32[3,128,128]{2,1,0:T(8,128)S(1)}, u32[]{:S(2)}) copy-start(f32[3,128,128]{2,1,0:T(8,128)S(1)} %get-tuple-element.32.refs_3_) | copy-start | bytes 589828

commit v13 on v12

--- a/solution.py
+++ b/solution.py
@@ -95,12 +95,12 @@
 
 def stencil_kernel(nw, nn, total_cells, *refs):
     nd = len(DIRS)
-    det_ref, cm_ref, m_ref = refs[:3]
-    sends = refs[3:3 + nd]
+    det_ref, cm_ref = refs[:2]
+    sends = refs[2:2 + nd]
     g_ref, h_ref, out_ref, sq_ref, r0, r1, r2, ss_ref, part1, part2, q1, q2, s1, p1, s2, p2 = \
-        refs[3 + nd:19 + nd]
-    halos = refs[19 + nd:19 + 2 * nd]
-    hs, hr = refs[19 + 2 * nd:]
+        refs[2 + nd:18 + nd]
+    halos = refs[18 + nd:18 + 2 * nd]
+    hs, hr = refs[18 + 2 * nd:]
     top_ref, bot_ref, left_ref, right_ref, tl_ref, tr_ref, bl_ref, br_ref = halos
     i = pl.program_id(0)
     me_w = lax.axis_index("wide")
@@ -139,7 +139,8 @@
             r0[s, 0:LPAD] = zero[0:LPAD]
             for p in range(HALO):
                 r0[s, pl.ds(LPAD - HALO + p, 1)] = left_ref[p, pl.ds(b, 1)]
-            r0[s, LPAD:LPAD + cy] = cm_ref[t] + m_ref[t] * det_ref[b].astype(jnp.float32)
+            own = h_ref[t + 1, LPAD:LPAD + cy] > 0
+            r0[s, LPAD:LPAD + cy] = cm_ref[t] + jnp.where(own, det_ref[b].astype(jnp.float32), 0.0)
             r0[s, LPAD + cy:width] = zero[0:width - LPAD - cy]
             for p in range(HALO):
                 r0[s, pl.ds(LPAD + cy + p, 1)] = right_ref[p, pl.ds(b, 1)]
@@ -218,7 +219,7 @@
     return jnp.sum(slots[...], axis=0)
 
 
-def run_stencil(det, cm, m, sends, g, h, nw, nn, total_cells):
+def run_stencil(det, cm, sends, g, h, nw, nn, total_cells):
     cx, cy, k = det.shape
     width = g.shape[1]
     steps = cx // ROWS
@@ -227,7 +228,7 @@
     return pl.pallas_call(
         functools.partial(stencil_kernel, nw, nn, float(total_cells)),
         grid=(steps,),
-        in_specs=[vmem] * (5 + len(sends)),
+        in_specs=[vmem] * (4 + len(sends)),
         out_specs=[
             pl.BlockSpec((ROWS, cy, k), lambda i: (i, 0, 0)),
             pl.BlockSpec((1, k), lambda i: (0, 0)),
@@ -257,7 +258,7 @@
         cost_estimate=pl.CostEstimate(
             flops=ops, transcendentals=0, bytes_accessed=det.size * 2 + cx * cy * k * 4 + g.size * 4
         ),
-    )(det, cm, m, *sends, g, h)
+    )(det, cm, *sends, g, h)
 
 
 def gather_kernel(nw, nn, cols, *refs):
@@ -437,7 +438,7 @@
     h_rows = gh_ext[1][jnp.array([0] + [h + TS * t for t in range(tiles_x)] + [h + cells_x])]
     h_b = jnp.broadcast_to(h_rows[:, :, None], (tiles_x + 2, width, columns))
 
-    cheb_three, inv = run_stencil(detail, cm0, m0, sends, g_b, h_b, nw, nn, total_cells)
+    cheb_three, inv = run_stencil(detail, cm0, sends, g_b, h_b, nw, nn, total_cells)
     return scale_rows(cheb_three, inv)
 
 

time: 109 us -> 108 us (level)
  local copies, waits for them, and re-layouts: 22.2 us -> 20.9 us
    broadcast_in_dim x3 -> x2, local copies, waits for them, and re-layouts: 1.39 us -> 0.06 us  [local(): m0 = jnp.broadcast_to(m_rows[:, :, None], (tiles_x, cells_y, columns))]
where the time goes in v13:
time: 108 us; the launch traced here: 107 us
  Pallas kernels  80.1 us (74%)
  local copies, waits for them, and re-layouts  20.9 us (19%)
  other arithmetic  6.09 us (6%)
    pallas_call x1, Pallas kernels, run_stencil(): pl.pallas_call(functools.partial(stencil_kernel, nw, nn, float(total_cell...  56.6 us
    pallas_call x1, Pallas kernels, gather_tiles(): pl.pallas_call(functools.partial(gather_kernel, nw, nn, ccx), in_specs=[v...  17.6 us
    broadcast_in_dim x1, local copies, waits for them, and re-layouts, local(): jnp.broadcast_to(gh_ext[0][:, :, None], (cells_x + 2 * h, width, columns))  6.89 us
    pallas_call x1, Pallas kernels, scale_rows(): pl.pallas_call(scale_kernel, grid=(cx // SCALE_ROWS,), in_specs=[pl.Block...  5.87 us

profile of v13, /device:TPU:1, one launch (start us, length us, event | category | flops | bytes accessed | tf_op | source)
XLA Modules:
  0.0 107.2 jit_solution(13287345079928075716)
XLA Ops:
  0.0 1.4 %reshape.50.refs_0_ = s32[1,256]{1,0:T(1,128)} reshape(s32[16,16]{1,0:T(8,128)} %param.9) | data formatting | bytes 2048 | tf_op jit(solution)/shard_map/reshape | solution.py:332
  1.4 0.7 pad_clamp_fusion
  2.0 0.7 convert_element_type.15
  2.7 0.1 broadcast_in_dim.57
  2.8 0.1 broadcast_in_dim.58
  2.9 0.1 broadcast_in_dim.55
  3.0 0.1 broadcast_in_dim.56
  3.1 0.1 copy.32
  3.1 0.1 copy.33
  3.2 0.1 copy.36
  3.3 0.1 copy.37
  3.4 0.1 copy.34
  3.5 0.1 copy.35
  3.6 0.9 multiply_bitcast_fusion
  4.5 0.6 fusion.4
  5.1 0.7 fusion.8
  5.8 0.1 fusion.13
  5.8 0.1 copy.45
  5.9 0.1 copy.43
  6.0 0.1 fusion.12
  6.1 0.7 copy.39.refs_5_
  6.8 0.7 copy.38.refs_4_
  7.4 17.6 %shard_map.64 = (f32[128,256]{1,0:T(8,128)}, f32[2,3,128]{2,1,0:T(4,128)}, f32[2,3,128]{2,1,0:T(4,128)}, f32[2,3,128]{2,1,0:T(4,128)}, f32[2,3,128]{2,1,0:T(4,12...) custom-call(s32[1,256]{1,0:T(1,128)} %reshape.50.refs_0_, ...), custom_call_target="tpu_custom_call" | custom-call | tf_op jit(solution)/shard_map/pallas_call | solution.py:336
  25.1 1.0 copy.40
  26.1 0.8 concatenate.12
  26.9 0.8 concatenate.14
  27.6 0.8 copy.47
  28.4 0.8 copy.48
  29.3 0.2 concatenate.13
  29.6 0.6 gather_fusion
  30.2 1.1 %fusion.9 = (bf16[128,3,128]{2,1,0:T(4,128)(2,1)S(1)}, bf16[128,3,128]{2,1,0:T(4,128)(2,1)S(1)}) fusion(bf16[128,128,128]{2,1,0:T(8,128)(2,1)} %refs_0_.1), kind=kLoop, calls=%fused_computation.44 | loop fusion | bytes 393216 | tf_op jit(solution)/shard_map/slice | solution.py:415
  31.3 0.3 bitcast_multiply_fusion.refs_1_
  31.7 0.0 copy-start
  31.7 1.3 %multiply_add_fusion = (f32[3,128,128]{2,1,0:T(8,128)S(1)}, f32[3,128,128]{2,1,0:T(8,128)S(1)}) fusion(bf16[128,128,128]{2,1,0:T(8,128)(2,1)} %refs_0_.1, f32[128]{0:T(128)S(1)} %broadcast_in_dim.58, f32[128,128]{1,0:T(8,128)S(1)} %get-tuple-element.33, f32[128]{0:T(128)S(1)} %broadcast_in_dim.56, f32[128,128]{1,0:T(8,128)S(1)} %get-tuple-element.34), kind=kLoop, calls=%fused_computation.21 | loop fusion | flops 294912 | bytes 721920 | tf_op jit(solution)/shard_map/add | solution.py:411
  33.0 0.0 copy-start.1
  33.0 0.0 copy-start.2
  33.0 0.7 fusion.10
  33.7 0.6 copy.41
  34.3 1.5 %broadcast_in_dim.63.refs_11_ = f32[18,144,128]{2,1,0:T(8,128)} broadcast(f32[18,144]{1,0:T(8,128)S(1)} %gather_fusion), dimensions={0,1} | broadcast | bytes 1337472 | tf_op jit(solution)/shard_map/broadcast_in_dim | solution.py:439
  35.8 1.1 %broadcast_bitcast_fusion = f32[128,128,128]{2,0,1:T(8,128)S(1)} fusion(f32[16,128,128]{2,0,1:T(8,128)S(1)} %copy.41), kind=kLoop, calls=%fused_computation.1 | loop fusion | bytes 9437184 | tf_op jit(solution)/shard_map/reshape | solution.py:413
  36.9 0.9 fusion
  37.8 6.9 %broadcast_in_dim.61.refs_10_ = f32[134,144,128]{2,1,0:T(8,128)} broadcast(f32[134,144]{1,0:T(8,128)S(1)} %get-tuple-element.36), dimensions={0,1} | broadcast | bytes 9956736 | tf_op jit(solution)/shard_map/broadcast_in_dim | solution.py:437
  44.7 0.0 copy-done
  44.7 0.0 copy-done.1
  44.7 0.0 copy-done.2
  44.7 56.6 %shard_map.65 = (f32[128,128,128]{2,1,0:T(8,128)}, f32[1,128]{1,0:T(1,128)}) custom-call(bf16[128,128,128]{2,1,0:T(8,128)(2,1)} %refs_0_.1, f32[16,128,128]{2,1,0:T(8,128)} %copy-done, f32[3,128,128]{2,1,0:T(8,128)} %copy-done.2, f32[3,128,128]{2,1,0:T(8,128)} %copy-done.1, f32[3,128,128]{2,1,0:T(8,128)} %get-tuple-element.28.refs_4_, ...), custom_call_target="tpu_custom_call" | custom-call | flops 75497472 | bytes 22462464 | tf_op jit(solution)/shard_map/pallas_call | solution.py:228
  101.4 5.9 %shard_map.66 = f32[128,128,128]{2,1,0:T(8,128)} custom-call(f32[128,128,128]{2,1,0:T(8,128)} %get-tuple-element.25.x_ref, f32[1,128]{1,0:T(1,128)} %get-tuple-element.26.s_ref), custom_call_target="tpu_custom_call" | custom-call | flops 2097152 | bytes 16777216 | tf_op jit(solution)/shard_map/pallas_call | solution.py:363
  (13 shorter events, 0.2 us)
Async XLA Ops:
  31.7 13.1 %copy-start = (f32[16,128,128]{2,1,0:T(8,128)}, f32[16,128,128]{2,1,0:T(8,128)S(1)}, u32[]{:S(2)}) copy-start(f32[16,128,128]{2,1,0:T(8,128)S(1)} %bitcast_multiply_fusion.refs_1_) | copy-start | bytes 3145732
  33.0 11.8 %copy-start.1 = (f32[3,128,128]{2,1,0:T(8,128)}, f32[3,128,128]{2,1,0:T(8,128)S(1)}, u32[]{:S(2)}) copy-start(f32[3,128,128]{2,1,0:T(8,128)S(1)} %get-tuple-element.31.refs_3_) | copy-start | bytes 589828
  33.0 11.8 %copy-start.2 = (f32[3,128,128]{2,1,0:T(8,128)}, f32[3,128,128]{2,1,0:T(8,128)S(1)}, u32[]{:S(2)}) copy-start(f32[3,128,128]{2,1,0:T(8,128)S(1)} %get-tuple-element.32.refs_2_) | copy-start | bytes 589828

commit v14 on v13

--- a/solution.py
+++ b/solution.py
@@ -14,8 +14,8 @@
 
 HALO = 3
 LPAD = 8
-RING = 16
-ROWS = 8
+RING = 32
+ROWS = 16
 SCALE_ROWS = 64
 DIRS = ((1, 0), (-1, 0), (0, 1), (0, -1), (1, 1), (1, -1), (-1, 1), (-1, -1))
 DIAGONALS = DIRS[4:]

time: 108 us -> 107 us (level)
  no operation moved by 1% of the time
where the time goes in v14:
time: 107 us
  Pallas kernels  79.6 us (74%)
  local copies, waits for them, and re-layouts  20.9 us (20%)
  other arithmetic  6.09 us (6%)
    pallas_call x1, Pallas kernels, run_stencil(): pl.pallas_call(functools.partial(stencil_kernel, nw, nn, float(total_cell...  56.1 us
    pallas_call x1, Pallas kernels, gather_tiles(): pl.pallas_call(functools.partial(gather_kernel, nw, nn, ccx), in_specs=[v...  17.6 us
    broadcast_in_dim x1, local copies, waits for them, and re-layouts, local(): jnp.broadcast_to(gh_ext[0][:, :, None], (cells_x + 2 * h, width, columns))  6.89 us
    pallas_call x1, Pallas kernels, scale_rows(): pl.pallas_call(scale_kernel, grid=(cx // SCALE_ROWS,), in_specs=[pl.Block...  5.87 us

profile of v14, /device:TPU:1, one launch (start us, length us, event | category | flops | bytes accessed | tf_op | source)
XLA Modules:
  0.0 106.8 jit_solution(10084332661737447977)
XLA Ops:
  0.0 1.4 %reshape.50.refs_0_ = s32[1,256]{1,0:T(1,128)} reshape(s32[16,16]{1,0:T(8,128)} %param.9) | data formatting | bytes 2048 | tf_op jit(solution)/shard_map/reshape | solution.py:332
  1.4 0.7 pad_clamp_fusion
  2.0 0.7 convert_element_type.15
  2.7 0.1 broadcast_in_dim.57
  2.8 0.1 broadcast_in_dim.58
  2.9 0.1 broadcast_in_dim.55
  3.0 0.1 broadcast_in_dim.56
  3.1 0.1 copy.32
  3.1 0.1 copy.33
  3.2 0.1 copy.36
  3.3 0.1 copy.37
  3.4 0.1 copy.34
  3.5 0.1 copy.35
  3.6 0.9 multiply_bitcast_fusion
  4.5 0.6 fusion.4
  5.1 0.7 fusion.8
  5.8 0.1 fusion.13
  5.8 0.1 copy.45
  5.9 0.1 copy.43
  6.0 0.1 fusion.12
  6.1 0.7 copy.39.refs_5_
  6.8 0.7 copy.38.refs_4_
  7.4 17.6 %shard_map.64 = (f32[128,256]{1,0:T(8,128)}, f32[2,3,128]{2,1,0:T(4,128)}, f32[2,3,128]{2,1,0:T(4,128)}, f32[2,3,128]{2,1,0:T(4,128)}, f32[2,3,128]{2,1,0:T(4,12...) custom-call(s32[1,256]{1,0:T(1,128)} %reshape.50.refs_0_, ...), custom_call_target="tpu_custom_call" | custom-call | tf_op jit(solution)/shard_map/pallas_call | solution.py:336
  25.1 1.0 copy.40
  26.1 0.8 concatenate.12
  26.9 0.8 concatenate.14
  27.6 0.8 copy.47
  28.4 0.8 copy.48
  29.3 0.2 concatenate.13
  29.6 0.6 gather_fusion
  30.2 1.1 %fusion.9 = (bf16[128,3,128]{2,1,0:T(4,128)(2,1)S(1)}, bf16[128,3,128]{2,1,0:T(4,128)(2,1)S(1)}) fusion(bf16[128,128,128]{2,1,0:T(8,128)(2,1)} %refs_0_.1), kind=kLoop, calls=%fused_computation.44 | loop fusion | bytes 393216 | tf_op jit(solution)/shard_map/slice | solution.py:415
  31.3 0.3 bitcast_multiply_fusion.refs_1_
  31.7 0.0 copy-start
  31.7 1.3 %multiply_add_fusion = (f32[3,128,128]{2,1,0:T(8,128)S(1)}, f32[3,128,128]{2,1,0:T(8,128)S(1)}) fusion(bf16[128,128,128]{2,1,0:T(8,128)(2,1)} %refs_0_.1, f32[128]{0:T(128)S(1)} %broadcast_in_dim.58, f32[128,128]{1,0:T(8,128)S(1)} %get-tuple-element.33, f32[128]{0:T(128)S(1)} %broadcast_in_dim.56, f32[128,128]{1,0:T(8,128)S(1)} %get-tuple-element.34), kind=kLoop, calls=%fused_computation.21 | loop fusion | flops 294912 | bytes 721920 | tf_op jit(solution)/shard_map/add | solution.py:411
  33.0 0.0 copy-start.1
  33.0 0.0 copy-start.2
  33.0 0.7 fusion.10
  33.7 0.6 copy.41
  34.3 1.5 %broadcast_in_dim.63.refs_11_ = f32[18,144,128]{2,1,0:T(8,128)} broadcast(f32[18,144]{1,0:T(8,128)S(1)} %gather_fusion), dimensions={0,1} | broadcast | bytes 1337472 | tf_op jit(solution)/shard_map/broadcast_in_dim | solution.py:439
  35.8 1.1 %broadcast_bitcast_fusion = f32[128,128,128]{2,0,1:T(8,128)S(1)} fusion(f32[16,128,128]{2,0,1:T(8,128)S(1)} %copy.41), kind=kLoop, calls=%fused_computation.1 | loop fusion | bytes 9437184 | tf_op jit(solution)/shard_map/reshape | solution.py:413
  36.9 0.9 fusion
  37.8 6.9 %broadcast_in_dim.61.refs_10_ = f32[134,144,128]{2,1,0:T(8,128)} broadcast(f32[134,144]{1,0:T(8,128)S(1)} %get-tuple-element.36), dimensions={0,1} | broadcast | bytes 9956736 | tf_op jit(solution)/shard_map/broadcast_in_dim | solution.py:437
  44.7 0.0 copy-done
  44.7 0.0 copy-done.1
  44.7 0.0 copy-done.2
  44.7 56.1 %shard_map.65 = (f32[128,128,128]{2,1,0:T(8,128)}, f32[1,128]{1,0:T(1,128)}) custom-call(bf16[128,128,128]{2,1,0:T(8,128)(2,1)} %refs_0_.1, f32[16,128,128]{2,1,0:T(8,128)} %copy-done, f32[3,128,128]{2,1,0:T(8,128)} %copy-done.2, f32[3,128,128]{2,1,0:T(8,128)} %copy-done.1, f32[3,128,128]{2,1,0:T(8,128)} %get-tuple-element.28.refs_4_, ...), custom_call_target="tpu_custom_call" | custom-call | flops 75497472 | bytes 22462464 | tf_op jit(solution)/shard_map/pallas_call | solution.py:228
  100.9 5.9 %shard_map.66 = f32[128,128,128]{2,1,0:T(8,128)} custom-call(f32[128,128,128]{2,1,0:T(8,128)} %get-tuple-element.25.x_ref, f32[1,128]{1,0:T(1,128)} %get-tuple-element.26.s_ref), custom_call_target="tpu_custom_call" | custom-call | flops 2097152 | bytes 16777216 | tf_op jit(solution)/shard_map/pallas_call | solution.py:363
  (13 shorter events, 0.2 us)
Async XLA Ops:
  31.7 13.1 %copy-start = (f32[16,128,128]{2,1,0:T(8,128)}, f32[16,128,128]{2,1,0:T(8,128)S(1)}, u32[]{:S(2)}) copy-start(f32[16,128,128]{2,1,0:T(8,128)S(1)} %bitcast_multiply_fusion.refs_1_) | copy-start | bytes 3145732
  33.0 11.8 %copy-start.1 = (f32[3,128,128]{2,1,0:T(8,128)}, f32[3,128,128]{2,1,0:T(8,128)S(1)}, u32[]{:S(2)}) copy-start(f32[3,128,128]{2,1,0:T(8,128)S(1)} %get-tuple-element.31.refs_3_) | copy-start | bytes 589828
  33.0 11.8 %copy-start.2 = (f32[3,128,128]{2,1,0:T(8,128)}, f32[3,128,128]{2,1,0:T(8,128)S(1)}, u32[]{:S(2)}) copy-start(f32[3,128,128]{2,1,0:T(8,128)S(1)} %get-tuple-element.32.refs_2_) | copy-start | bytes 589828

commit v15 on v14

--- a/solution.py
+++ b/solution.py
@@ -422,20 +422,20 @@
     sends = [c0_pieces[dirn] for dirn in DIRS]
 
     rpad = LPAD - h
-    z3 = jnp.zeros((2, h, rpad), jnp.float32)
+    width = cells_y + 2 * LPAD
     zc = jnp.zeros((2, cells_x, rpad), jnp.float32)
     gh_ext = jnp.concatenate(
         [
-            jnp.concatenate([z3, hg[(1, 1)], hg[(1, 0)], hg[(1, -1)], z3], axis=2),
+            (jnp.pad(hg[(1, 1)], ((0, 0), (0, 0), (rpad, width - LPAD))) + jnp.pad(hg[(1, 0)], ((0, 0), (0, 0), (LPAD, LPAD))) + jnp.pad(hg[(1, -1)], ((0, 0), (0, 0), (LPAD + cells_y, rpad)))),
             jnp.concatenate([zc.transpose(0, 2, 1), hg[(0, 1)], gh_t, hg[(0, -1)], zc.transpose(0, 2, 1)],
                             axis=1).transpose(0, 2, 1),
-            jnp.concatenate([z3, hg[(-1, 1)], hg[(-1, 0)], hg[(-1, -1)], z3], axis=2),
+            (jnp.pad(hg[(-1, 1)], ((0, 0), (0, 0), (rpad, width - LPAD))) + jnp.pad(hg[(-1, 0)], ((0, 0), (0, 0), (LPAD, LPAD))) + jnp.pad(hg[(-1, -1)], ((0, 0), (0, 0), (LPAD + cells_y, rpad)))),
         ],
         axis=1,
     )
-    width = cells_y + 2 * LPAD
     g_b = jnp.broadcast_to(gh_ext[0][:, :, None], (cells_x + 2 * h, width, columns))
-    h_rows = gh_ext[1][jnp.array([0] + [h + TS * t for t in range(tiles_x)] + [h + cells_x])]
+    h_rows = jnp.concatenate(
+        [gh_ext[1][0:1], gh_ext[1][h:h + cells_x:TS], gh_ext[1][h + cells_x:h + cells_x + 1]], axis=0)
     h_b = jnp.broadcast_to(h_rows[:, :, None], (tiles_x + 2, width, columns))
 
     cheb_three, inv = run_stencil(detail, cm0, sends, g_b, h_b, nw, nn, total_cells)

time: 107 us -> 105 us (0.981)
  local copies, waits for them, and re-layouts: 20.9 us -> 18.7 us
    concatenate x2 -> x0, local copies, waits for them, and re-layouts: 1.57 us -> none  [the longest x1 0.79 us: local(): jnp.concatenate([z3, hg[1, 1], hg[1, 0], hg[1, -1], z3], axis=2)]
where the time goes in v15:
time: 105 us
  Pallas kernels  79.6 us (76%)
  local copies, waits for them, and re-layouts  18.7 us (18%)
  other arithmetic  6.24 us (6%)
    pallas_call x1, Pallas kernels, run_stencil(): pl.pallas_call(functools.partial(stencil_kernel, nw, nn, float(total_cell...  56.1 us
    pallas_call x1, Pallas kernels, gather_tiles(): pl.pallas_call(functools.partial(gather_kernel, nw, nn, ccx), in_specs=[v...  17.6 us
    broadcast_in_dim x1, local copies, waits for them, and re-layouts, local(): jnp.broadcast_to(gh_ext[0][:, :, None], (cells_x + 2 * h, width, columns))  6.9 us
    pallas_call x1, Pallas kernels, scale_rows(): pl.pallas_call(scale_kernel, grid=(cx // SCALE_ROWS,), in_specs=[pl.Block...  5.87 us
    another operation x3, other arithmetic, local(): gh = jnp.stack([g_own, h_own])  2.13 us

profile of v15, /device:TPU:1, one launch (start us, length us, event | category | flops | bytes accessed | tf_op | source)
XLA Modules:
  0.0 104.8 jit_solution(3866394328538922690)
XLA Ops:
  0.0 1.3 %reshape.52.refs_0_ = s32[1,256]{1,0:T(1,128)} reshape(s32[16,16]{1,0:T(8,128)} %param.8) | data formatting | bytes 2048 | tf_op jit(solution)/shard_map/reshape | solution.py:332
  1.3 0.7 convert_element_type.24
  2.0 0.1 broadcast_in_dim.54
  2.1 0.1 broadcast_in_dim.55
  2.2 0.1 broadcast_in_dim.52
  2.3 0.1 broadcast_in_dim.53
  2.3 0.1 copy.31
  2.4 0.1 copy.32
  2.5 0.1 copy.35
  2.6 0.1 copy.36
  2.7 0.1 copy.33
  2.8 0.1 copy.34
  2.9 0.9 multiply_bitcast_fusion
  3.8 0.6 fusion.4
  4.4 0.7 fusion.8
  5.0 0.1 fusion.13
  5.1 0.1 copy.44
  5.2 0.1 copy.42
  5.3 0.1 fusion.12
  5.4 0.7 copy.38.refs_5_
  6.1 0.7 copy.37.refs_4_
  6.7 17.6 %shard_map.55 = (f32[128,256]{1,0:T(8,128)}, f32[2,3,128]{2,1,0:T(4,128)}, f32[2,3,128]{2,1,0:T(4,128)}, f32[2,3,128]{2,1,0:T(4,128)}, f32[2,3,128]{2,1,0:T(4,12...) custom-call(s32[1,256]{1,0:T(1,128)} %reshape.52.refs_0_, ...), custom_call_target="tpu_custom_call" | custom-call | tf_op jit(solution)/shard_map/pallas_call | solution.py:336
  24.3 1.0 copy.39
  25.3 0.8 pad_add_fusion
  26.2 0.8 copy.46
  27.0 0.8 copy.47
  27.8 0.2 concatenate.9
  28.2 1.1 %fusion.9 = (bf16[128,3,128]{2,1,0:T(4,128)(2,1)S(1)}, bf16[128,3,128]{2,1,0:T(4,128)(2,1)S(1)}) fusion(bf16[128,128,128]{2,1,0:T(8,128)(2,1)} %refs_0_.1), kind=kLoop, calls=%fused_computation.47 | loop fusion | bytes 393216 | tf_op jit(solution)/shard_map/slice | solution.py:415
  29.3 0.3 bitcast_multiply_fusion.refs_1_
  29.7 0.0 copy-start
  29.7 1.3 %multiply_add_fusion = (f32[3,128,128]{2,1,0:T(8,128)S(1)}, f32[3,128,128]{2,1,0:T(8,128)S(1)}) fusion(bf16[128,128,128]{2,1,0:T(8,128)(2,1)} %refs_0_.1, f32[128]{0:T(128)S(1)} %broadcast_in_dim.55, f32[128,128]{1,0:T(8,128)S(1)} %get-tuple-element.33, f32[128]{0:T(128)S(1)} %broadcast_in_dim.53, f32[128,128]{1,0:T(8,128)S(1)} %get-tuple-element.34), kind=kLoop, calls=%fused_computation.20 | loop fusion | flops 294912 | bytes 721920 | tf_op jit(solution)/shard_map/add | solution.py:411
  31.0 0.0 copy-start.1
  31.0 0.0 copy-start.2
  31.0 0.7 fusion.10
  31.7 0.6 copy.40
  32.3 1.5 %broadcast_in_dim.59.refs_11_ = f32[18,144,128]{2,1,0:T(8,128)} broadcast(f32[18,144]{1,0:T(8,128)S(1)} %pad_maximum_fusion.2), dimensions={0,1} | broadcast | bytes 1337472 | tf_op jit(solution)/shard_map/broadcast_in_dim | solution.py:439
  33.8 1.1 %broadcast_bitcast_fusion = f32[128,128,128]{2,0,1:T(8,128)S(1)} fusion(f32[16,128,128]{2,0,1:T(8,128)S(1)} %copy.40), kind=kLoop, calls=%fused_computation | loop fusion | bytes 9437184 | tf_op jit(solution)/shard_map/reshape | solution.py:413
  34.9 0.9 fusion
  35.9 6.9 %broadcast_in_dim.58.refs_10_ = f32[134,144,128]{2,1,0:T(8,128)} broadcast(f32[134,144]{1,0:T(8,128)S(1)} %get-tuple-element.36), dimensions={0,1} | broadcast | bytes 9956736 | tf_op jit(solution)/shard_map/broadcast_in_dim | solution.py:436
  42.8 0.0 copy-done
  42.8 0.0 copy-done.1
  42.8 0.0 copy-done.2
  42.8 56.1 %shard_map.56 = (f32[128,128,128]{2,1,0:T(8,128)}, f32[1,128]{1,0:T(1,128)}) custom-call(bf16[128,128,128]{2,1,0:T(8,128)(2,1)} %refs_0_.1, f32[16,128,128]{2,1,0:T(8,128)} %copy-done, f32[3,128,128]{2,1,0:T(8,128)} %copy-done.2, f32[3,128,128]{2,1,0:T(8,128)} %copy-done.1, f32[3,128,128]{2,1,0:T(8,128)} %get-tuple-element.28.refs_4_, ...), custom_call_target="tpu_custom_call" | custom-call | flops 75497472 | bytes 22462464 | tf_op jit(solution)/shard_map/pallas_call | solution.py:228
  98.9 5.9 %shard_map.57 = f32[128,128,128]{2,1,0:T(8,128)} custom-call(f32[128,128,128]{2,1,0:T(8,128)} %get-tuple-element.25.x_ref, f32[1,128]{1,0:T(1,128)} %get-tuple-element.26.s_ref), custom_call_target="tpu_custom_call" | custom-call | flops 2097152 | bytes 16777216 | tf_op jit(solution)/shard_map/pallas_call | solution.py:363
  (16 shorter events, 0.2 us)
Async XLA Ops:
  29.7 13.1 %copy-start = (f32[16,128,128]{2,1,0:T(8,128)}, f32[16,128,128]{2,1,0:T(8,128)S(1)}, u32[]{:S(2)}) copy-start(f32[16,128,128]{2,1,0:T(8,128)S(1)} %bitcast_multiply_fusion.refs_1_) | copy-start | bytes 3145732
  31.0 11.8 %copy-start.1 = (f32[3,128,128]{2,1,0:T(8,128)}, f32[3,128,128]{2,1,0:T(8,128)S(1)}, u32[]{:S(2)}) copy-start(f32[3,128,128]{2,1,0:T(8,128)S(1)} %get-tuple-element.31.refs_3_) | copy-start | bytes 589828
  31.0 11.8 %copy-start.2 = (f32[3,128,128]{2,1,0:T(8,128)}, f32[3,128,128]{2,1,0:T(8,128)S(1)}, u32[]{:S(2)}) copy-start(f32[3,128,128]{2,1,0:T(8,128)S(1)} %get-tuple-element.32.refs_2_) | copy-start | bytes 589828

commit v16 on v15

--- a/solution.py
+++ b/solution.py
@@ -424,15 +424,17 @@
     rpad = LPAD - h
     width = cells_y + 2 * LPAD
     zc = jnp.zeros((2, cells_x, rpad), jnp.float32)
-    gh_ext = jnp.concatenate(
-        [
-            (jnp.pad(hg[(1, 1)], ((0, 0), (0, 0), (rpad, width - LPAD))) + jnp.pad(hg[(1, 0)], ((0, 0), (0, 0), (LPAD, LPAD))) + jnp.pad(hg[(1, -1)], ((0, 0), (0, 0), (LPAD + cells_y, rpad)))),
-            jnp.concatenate([zc.transpose(0, 2, 1), hg[(0, 1)], gh_t, hg[(0, -1)], zc.transpose(0, 2, 1)],
-                            axis=1).transpose(0, 2, 1),
-            (jnp.pad(hg[(-1, 1)], ((0, 0), (0, 0), (rpad, width - LPAD))) + jnp.pad(hg[(-1, 0)], ((0, 0), (0, 0), (LPAD, LPAD))) + jnp.pad(hg[(-1, -1)], ((0, 0), (0, 0), (LPAD + cells_y, rpad)))),
-        ],
-        axis=1,
-    )
+    def cols(x, lo, hi):
+        return jnp.pad(x, ((0, 0), (0, 0), (lo, hi)))
+
+    def rows_of(x, lo, hi):
+        return jnp.pad(x, ((0, 0), (lo, hi), (0, 0)))
+
+    top = cols(hg[(1, 1)], rpad, width - LPAD) + cols(hg[(1, 0)], LPAD, LPAD) + cols(hg[(1, -1)], LPAD + cells_y, rpad)
+    bot = cols(hg[(-1, 1)], rpad, width - LPAD) + cols(hg[(-1, 0)], LPAD, LPAD) + cols(hg[(-1, -1)], LPAD + cells_y, rpad)
+    mid_t = rows_of(hg[(0, 1)], rpad, width - LPAD) + rows_of(gh_t, LPAD, LPAD) + rows_of(hg[(0, -1)], LPAD + cells_y, rpad)
+    mid = mid_t.transpose(0, 2, 1)
+    gh_ext = rows_of(top, 0, cells_x + h) + rows_of(mid, h, h) + rows_of(bot, cells_x + h, 0)
     g_b = jnp.broadcast_to(gh_ext[0][:, :, None], (cells_x + 2 * h, width, columns))
     h_rows = jnp.concatenate(
         [gh_ext[1][0:1], gh_ext[1][h:h + cells_x:TS], gh_ext[1][h + cells_x:h + cells_x + 1]], axis=0)

time: 105 us -> 105 us (level)
  no operation moved by 1% of the time
where the time goes in v16:
time: 105 us
  Pallas kernels  79.6 us (76%)
  local copies, waits for them, and re-layouts  18.4 us (18%)
  other arithmetic  6.48 us (6%)
    pallas_call x1, Pallas kernels, run_stencil(): pl.pallas_call(functools.partial(stencil_kernel, nw, nn, float(total_cell...  56.1 us
    pallas_call x1, Pallas kernels, gather_tiles(): pl.pallas_call(functools.partial(gather_kernel, nw, nn, ccx), in_specs=[v...  17.6 us
    broadcast_in_dim x1, local copies, waits for them, and re-layouts, local(): jnp.broadcast_to(gh_ext[0][:, :, None], (cells_x + 2 * h, width, columns))  6.86 us
    pallas_call x1, Pallas kernels, scale_rows(): pl.pallas_call(scale_kernel, grid=(cx // SCALE_ROWS,), in_specs=[pl.Block...  5.87 us
    another operation x3, other arithmetic, local(): gh = jnp.stack([g_own, h_own])  2.13 us

profile of v16, /device:TPU:1, one launch (start us, length us, event | category | flops | bytes accessed | tf_op | source)
XLA Modules:
  0.0 104.7 jit_solution(10095915468306632218)
XLA Ops:
  0.0 1.3 %reshape.52.refs_0_ = s32[1,256]{1,0:T(1,128)} reshape(s32[16,16]{1,0:T(8,128)} %param.8) | data formatting | bytes 2048 | tf_op jit(solution)/shard_map/reshape | solution.py:332
  1.3 0.7 convert_element_type.36
  2.0 0.1 broadcast_in_dim.54
  2.1 0.1 broadcast_in_dim.55
  2.2 0.1 broadcast_in_dim.52
  2.3 0.1 broadcast_in_dim.53
  2.4 0.1 copy.31
  2.5 0.1 copy.32
  2.6 0.1 copy.35
  2.6 0.1 copy.36
  2.7 0.1 copy.33
  2.8 0.1 copy.34
  2.9 0.9 multiply_bitcast_fusion
  3.8 0.6 fusion.4
  4.4 0.7 fusion.8
  5.1 0.1 fusion.13
  5.2 0.1 copy.44
  5.2 0.1 copy.42
  5.3 0.1 fusion.12
  5.4 0.7 copy.38.refs_5_
  6.1 0.7 copy.37.refs_4_
  6.8 17.6 %shard_map.55 = (f32[128,256]{1,0:T(8,128)}, f32[2,3,128]{2,1,0:T(4,128)}, f32[2,3,128]{2,1,0:T(4,128)}, f32[2,3,128]{2,1,0:T(4,128)}, f32[2,3,128]{2,1,0:T(4,12...) custom-call(s32[1,256]{1,0:T(1,128)} %reshape.52.refs_0_, ...), custom_call_target="tpu_custom_call" | custom-call | tf_op jit(solution)/shard_map/pallas_call | solution.py:336
  24.4 1.0 copy.39
  25.4 0.8 pad_add_fusion.1
  26.2 0.8 copy.46
  27.0 0.8 copy.47
  27.8 0.2 add_bitcast_fusion
  28.2 1.1 %fusion.9 = (bf16[128,3,128]{2,1,0:T(4,128)(2,1)S(1)}, bf16[128,3,128]{2,1,0:T(4,128)(2,1)S(1)}) fusion(bf16[128,128,128]{2,1,0:T(8,128)(2,1)} %refs_0_.1), kind=kLoop, calls=%fused_computation.48 | loop fusion | bytes 393216 | tf_op jit(solution)/shard_map/slice | solution.py:415
  29.3 0.3 bitcast_multiply_fusion.refs_1_
  29.6 0.0 copy-start
  29.7 1.3 %multiply_add_fusion = (f32[3,128,128]{2,1,0:T(8,128)S(1)}, f32[3,128,128]{2,1,0:T(8,128)S(1)}) fusion(bf16[128,128,128]{2,1,0:T(8,128)(2,1)} %refs_0_.1, f32[128]{0:T(128)S(1)} %broadcast_in_dim.55, f32[128,128]{1,0:T(8,128)S(1)} %get-tuple-element.33, f32[128]{0:T(128)S(1)} %broadcast_in_dim.53, f32[128,128]{1,0:T(8,128)S(1)} %get-tuple-element.34), kind=kLoop, calls=%fused_computation.21 | loop fusion | flops 294912 | bytes 721920 | tf_op jit(solution)/shard_map/add | solution.py:411
  31.0 0.0 copy-start.1
  31.0 0.0 copy-start.2
  31.0 0.7 fusion.10
  31.7 0.6 copy.40
  32.3 1.5 %broadcast_in_dim.59.refs_11_ = f32[18,144,128]{2,1,0:T(8,128)} broadcast(f32[18,144]{1,0:T(8,128)S(1)} %pad_maximum_fusion.1), dimensions={0,1} | broadcast | bytes 1337472 | tf_op jit(solution)/shard_map/broadcast_in_dim | solution.py:441
  33.8 1.1 %broadcast_bitcast_fusion = f32[128,128,128]{2,0,1:T(8,128)S(1)} fusion(f32[16,128,128]{2,0,1:T(8,128)S(1)} %copy.40), kind=kLoop, calls=%fused_computation | loop fusion | bytes 9437184 | tf_op jit(solution)/shard_map/reshape | solution.py:413
  34.9 0.9 fusion
  35.8 6.9 %broadcast_in_dim.58.refs_10_ = f32[134,144,128]{2,1,0:T(8,128)} broadcast(f32[134,144]{1,0:T(8,128)S(1)} %get-tuple-element.38), dimensions={0,1} | broadcast | bytes 9956736 | tf_op jit(solution)/shard_map/broadcast_in_dim | solution.py:438
  42.7 0.0 copy-done
  42.7 0.0 copy-done.1
  42.7 0.0 copy-done.2
  42.7 56.1 %shard_map.56 = (f32[128,128,128]{2,1,0:T(8,128)}, f32[1,128]{1,0:T(1,128)}) custom-call(bf16[128,128,128]{2,1,0:T(8,128)(2,1)} %refs_0_.1, f32[16,128,128]{2,1,0:T(8,128)} %copy-done, f32[3,128,128]{2,1,0:T(8,128)} %copy-done.2, f32[3,128,128]{2,1,0:T(8,128)} %copy-done.1, f32[3,128,128]{2,1,0:T(8,128)} %get-tuple-element.28.refs_4_, ...), custom_call_target="tpu_custom_call" | custom-call | flops 75497472 | bytes 22462464 | tf_op jit(solution)/shard_map/pallas_call | solution.py:228
  98.8 5.9 %shard_map.57 = f32[128,128,128]{2,1,0:T(8,128)} custom-call(f32[128,128,128]{2,1,0:T(8,128)} %get-tuple-element.25.x_ref, f32[1,128]{1,0:T(1,128)} %get-tuple-element.26.s_ref), custom_call_target="tpu_custom_call" | custom-call | flops 2097152 | bytes 16777216 | tf_op jit(solution)/shard_map/pallas_call | solution.py:363
  (14 shorter events, 0.2 us)
Async XLA Ops:
  29.6 13.1 %copy-start = (f32[16,128,128]{2,1,0:T(8,128)}, f32[16,128,128]{2,1,0:T(8,128)S(1)}, u32[]{:S(2)}) copy-start(f32[16,128,128]{2,1,0:T(8,128)S(1)} %bitcast_multiply_fusion.refs_1_) | copy-start | bytes 3145732
  31.0 11.7 %copy-start.1 = (f32[3,128,128]{2,1,0:T(8,128)}, f32[3,128,128]{2,1,0:T(8,128)S(1)}, u32[]{:S(2)}) copy-start(f32[3,128,128]{2,1,0:T(8,128)S(1)} %get-tuple-element.31.refs_3_) | copy-start | bytes 589828
  31.0 11.7 %copy-start.2 = (f32[3,128,128]{2,1,0:T(8,128)}, f32[3,128,128]{2,1,0:T(8,128)S(1)}, u32[]{:S(2)}) copy-start(f32[3,128,128]{2,1,0:T(8,128)S(1)} %get-tuple-element.32.refs_2_) | copy-start | bytes 589828

commit v17 on v16

--- a/solution.py
+++ b/solution.py
@@ -410,13 +410,20 @@
 
     c0_top = cm0[0][None] + m0[0][None] * detail[:h].astype(jnp.float32)
     c0_bot = cm0[-1][None] + m0[-1][None] * detail[-h:].astype(jnp.float32)
-    cm_rep = jnp.repeat(cm0, TS, axis=0)
-    m_rep = jnp.repeat(m0, TS, axis=0)
-    c0_left = cm_rep[:, :h] + m_rep[:, :h] * detail[:, :h].astype(jnp.float32)
-    c0_right = cm_rep[:, -h:] + m_rep[:, -h:] * detail[:, -h:].astype(jnp.float32)
+
+    def side_planes(cols_):
+        planes = []
+        for c in cols_:
+            cm_c = jnp.repeat(cm0[:, c], TS, axis=0)
+            m_c = jnp.repeat(m0[:, c], TS, axis=0)
+            planes.append(cm_c + m_c * detail[:, c].astype(jnp.float32))
+        return jnp.stack(planes)
+
+    c0_left = side_planes(range(h))
+    c0_right = side_planes(range(cells_y - h, cells_y))
     c0_pieces = {
         (1, 0): c0_bot, (-1, 0): c0_top,
-        (0, 1): c0_right.transpose(1, 0, 2), (0, -1): c0_left.transpose(1, 0, 2),
+        (0, 1): c0_right, (0, -1): c0_left,
         (1, 1): c0_bot[:, -h:], (1, -1): c0_bot[:, :h], (-1, 1): c0_top[:, -h:], (-1, -1): c0_top[:, :h],
     }
     sends = [c0_pieces[dirn] for dirn in DIRS]

time: 105 us -> 106 us (level)
    another operation x0 -> x2, other arithmetic: none -> 1.37 us  [side_planes(): return jnp.stack(planes)]
    reshape x1 -> x0, local copies, waits for them, and re-layouts: 1.15 us -> none  [local(): cm_rep = jnp.repeat(cm0, TS, axis=0)]
    slice x4 -> x2, local copies, waits for them, and re-layouts: 1.37 us -> 2.18 us  [the longest x1 2.14 us: side_planes(): planes.append(cm_c + m_c * detail[:, c].astype(jnp.float32))]
where the time goes in v17:
time: 106 us; the launch traced here: 105 us
  Pallas kernels  79.6 us (75%)
  local copies, waits for them, and re-layouts  18.5 us (17%)
  other arithmetic  6.98 us (7%)
    pallas_call x1, Pallas kernels, run_stencil(): pl.pallas_call(functools.partial(stencil_kernel, nw, nn, float(total_cell...  56.1 us
    pallas_call x1, Pallas kernels, gather_tiles(): pl.pallas_call(functools.partial(gather_kernel, nw, nn, ccx), in_specs=[v...  17.6 us
    broadcast_in_dim x1, local copies, waits for them, and re-layouts, local(): jnp.broadcast_to(gh_ext[0][:, :, None], (cells_x + 2 * h, width, columns))  6.89 us
    pallas_call x1, Pallas kernels, scale_rows(): pl.pallas_call(scale_kernel, grid=(cx // SCALE_ROWS,), in_specs=[pl.Block...  5.87 us
    slice x1, local copies, waits for them, and re-layouts, side_planes(): planes.append(cm_c + m_c * detail[:, c].astype(jnp.float32))  2.14 us
    another operation x3, other arithmetic, local(): gh = jnp.stack([g_own, h_own])  2.13 us

profile of v17, /device:TPU:1, one launch (start us, length us, event | category | flops | bytes accessed | tf_op | source)
XLA Modules:
  0.0 105.3 jit_solution(14651961512982351601)
XLA Ops:
  0.0 1.3 %reshape.333.refs_0_ = s32[1,256]{1,0:T(1,128)} reshape(s32[16,16]{1,0:T(8,128)} %param.8) | data formatting | bytes 2048 | tf_op jit(solution)/shard_map/reshape | solution.py:332
  1.3 0.7 convert_element_type.108
  2.0 0.1 broadcast_in_dim.123
  2.1 0.1 broadcast_in_dim.124
  2.2 0.1 broadcast_in_dim.121
  2.3 0.1 broadcast_in_dim.122
  2.4 0.1 copy.35
  2.4 0.1 copy.36
  2.5 0.1 broadcast_in_dim.142
  2.6 0.1 broadcast_in_dim.143
  2.7 0.1 broadcast_in_dim.152
  2.8 0.1 broadcast_in_dim.153
  2.8 0.1 broadcast_in_dim.147
  2.9 0.1 broadcast_in_dim.148
  3.0 0.1 broadcast_in_dim.137
  3.1 0.1 broadcast_in_dim.138
  3.2 0.1 broadcast_in_dim.132
  3.2 0.1 broadcast_in_dim.133
  3.3 0.1 broadcast_in_dim.127
  3.4 0.1 broadcast_in_dim.128
  3.5 0.1 copy.39
  3.6 0.1 copy.40
  3.7 0.1 copy.37
  3.8 0.1 copy.38
  3.9 0.9 multiply_bitcast_fusion
  4.8 0.6 fusion.8
  5.4 0.7 fusion.12
  6.0 0.1 fusion.17
  6.1 0.7 copy.42.refs_5_
  6.8 0.7 copy.41.refs_4_
  7.5 17.6 %shard_map.55 = (f32[128,256]{1,0:T(8,128)}, f32[2,3,128]{2,1,0:T(4,128)}, f32[2,3,128]{2,1,0:T(4,128)}, f32[2,3,128]{2,1,0:T(4,128)}, f32[2,3,128]{2,1,0:T(4,12...) custom-call(s32[1,256]{1,0:T(1,128)} %reshape.333.refs_0_, ...), custom_call_target="tpu_custom_call" | custom-call | tf_op jit(solution)/shard_map/pallas_call | solution.py:336
  25.1 1.0 copy.43
  26.1 0.8 pad_add_fusion.1
  26.9 0.8 copy.50
  27.7 0.8 copy.51
  28.5 0.2 add_bitcast_fusion
  28.9 2.1 %fusion.13 = (bf16[128,1,128]{2,1,0:T(2,128)(2,1)S(1)}, bf16[128,1,128]{2,1,0:T(2,128)(2,1)S(1)}, bf16[128,1,128]{2,1,0:T(2,128)(2,1)S(1)}, bf16[128,1,128]{2,1,...) fusion(bf16[128,128,128]{2,1,0:T(8,128)(2,1)} %refs_0_.1), kind=kLoop, calls=%fused_computation.68 | loop fusion | bytes 393216 | tf_op jit(solution)/shard_map/slice | solution.py:419
  31.0 0.3 bitcast_multiply_fusion.refs_1_
  31.4 0.0 copy-start
  31.4 0.1 fusion.5
  31.5 0.1 fusion.3
  31.6 0.1 fusion.1
  31.7 0.7 pad_maximum_fusion.2.refs_5_
  32.4 0.7 pad_maximum_fusion.1.refs_4_
  33.1 1.0 multiply_add_fusion
  34.2 0.0 copy-start.1
  34.2 0.0 copy-start.2
  34.2 0.7 fusion.15
  34.9 1.5 %broadcast_in_dim.157.refs_11_ = f32[18,144,128]{2,1,0:T(8,128)} broadcast(f32[18,144]{1,0:T(8,128)S(1)} %pad_maximum_fusion.3), dimensions={0,1} | broadcast | bytes 1337472 | tf_op jit(solution)/shard_map/broadcast_in_dim | solution.py:448
  36.4 6.9 %broadcast_in_dim.156.refs_10_ = f32[134,144,128]{2,1,0:T(8,128)} broadcast(f32[134,144]{1,0:T(8,128)S(1)} %get-tuple-element.46), dimensions={0,1} | broadcast | bytes 9956736 | tf_op jit(solution)/shard_map/broadcast_in_dim | solution.py:445
  43.3 0.0 copy-done
  43.3 0.0 copy-done.1
  43.3 0.0 copy-done.2
  43.3 56.1 %shard_map.56 = (f32[128,128,128]{2,1,0:T(8,128)}, f32[1,128]{1,0:T(1,128)}) custom-call(bf16[128,128,128]{2,1,0:T(8,128)(2,1)} %refs_0_.1, f32[16,128,128]{2,1,0:T(8,128)} %copy-done, f32[3,128,128]{2,1,0:T(8,128)} %copy-done.2, f32[3,128,128]{2,1,0:T(8,128)} %copy-done.1, f32[3,128,128]{2,1,0:T(8,128)} %pad_maximum_fusion.1.refs_4_, ...), custom_call_target="tpu_custom_call" | custom-call | flops 75497472 | bytes 22462464 | tf_op jit(solution)/shard_map/pallas_call | solution.py:228
  99.4 5.9 %shard_map.57 = f32[128,128,128]{2,1,0:T(8,128)} custom-call(f32[128,128,128]{2,1,0:T(8,128)} %get-tuple-element.25.x_ref, f32[1,128]{1,0:T(1,128)} %get-tuple-element.26.s_ref), custom_call_target="tpu_custom_call" | custom-call | flops 2097152 | bytes 16777216 | tf_op jit(solution)/shard_map/pallas_call | solution.py:363
  (15 shorter events, 0.2 us)
Async XLA Ops:
  31.4 11.9 %copy-start = (f32[16,128,128]{2,1,0:T(8,128)}, f32[16,128,128]{2,1,0:T(8,128)S(1)}, u32[]{:S(2)}) copy-start(f32[16,128,128]{2,1,0:T(8,128)S(1)} %bitcast_multiply_fusion.refs_1_) | copy-start | bytes 3145732
  34.2 9.1 %copy-start.1 = (f32[3,128,128]{2,1,0:T(8,128)}, f32[3,128,128]{2,1,0:T(8,128)S(1)}, u32[]{:S(2)}) copy-start(f32[3,128,128]{2,1,0:T(8,128)S(1)} %get-tuple-element.33.refs_3_) | copy-start | bytes 589828
  34.2 9.1 %copy-start.2 = (f32[3,128,128]{2,1,0:T(8,128)}, f32[3,128,128]{2,1,0:T(8,128)S(1)}, u32[]{:S(2)}) copy-start(f32[3,128,128]{2,1,0:T(8,128)S(1)} %get-tuple-element.34.refs_2_) | copy-start | bytes 589828

commit v18 on v16

--- a/solution.py
+++ b/solution.py
@@ -16,7 +16,7 @@
 LPAD = 8
 RING = 32
 ROWS = 16
-SCALE_ROWS = 64
+SCALE_ROWS = 128
 DIRS = ((1, 0), (-1, 0), (0, 1), (0, -1), (1, 1), (1, -1), (-1, 1), (-1, -1))
 DIAGONALS = DIRS[4:]
 VERTICAL = ((1, 0), (-1, 0)) + DIAGONALS

time: 105 us -> 107 us (1.019)
  Pallas kernels: 79.6 us -> 81 us
    pallas_call x1, Pallas kernels: 5.87 us -> 7.32 us  [scale_rows(): pl.pallas_call(scale_kernel, grid=(cx // SCALE_ROWS,), in_specs=[pl.Block...]
where the time goes in v18:
time: 107 us; the launch traced here: 106 us
  Pallas kernels  81 us (76%)
  local copies, waits for them, and re-layouts  18.4 us (17%)
  other arithmetic  6.48 us (6%)
    pallas_call x1, Pallas kernels, run_stencil(): pl.pallas_call(functools.partial(stencil_kernel, nw, nn, float(total_cell...  56.1 us
    pallas_call x1, Pallas kernels, gather_tiles(): pl.pallas_call(functools.partial(gather_kernel, nw, nn, ccx), in_specs=[v...  17.6 us
    pallas_call x1, Pallas kernels, scale_rows(): pl.pallas_call(scale_kernel, grid=(cx // SCALE_ROWS,), in_specs=[pl.Block...  7.32 us
    broadcast_in_dim x1, local copies, waits for them, and re-layouts, local(): jnp.broadcast_to(gh_ext[0][:, :, None], (cells_x + 2 * h, width, columns))  6.86 us

profile of v18, /device:TPU:1, one launch (start us, length us, event | category | flops | bytes accessed | tf_op | source)
XLA Modules:
  0.0 106.2 jit_solution(18424910707519272629)
XLA Ops:
  0.0 1.3 %reshape.52.refs_0_ = s32[1,256]{1,0:T(1,128)} reshape(s32[16,16]{1,0:T(8,128)} %param.8) | data formatting | bytes 2048 | tf_op jit(solution)/shard_map/reshape | solution.py:332
  1.3 0.7 convert_element_type.36
  2.0 0.1 broadcast_in_dim.54
  2.1 0.1 broadcast_in_dim.55
  2.2 0.1 broadcast_in_dim.52
  2.3 0.1 broadcast_in_dim.53
  2.4 0.1 copy.31
  2.5 0.1 copy.32
  2.6 0.1 copy.35
  2.6 0.1 copy.36
  2.7 0.1 copy.33
  2.8 0.1 copy.34
  2.9 0.9 multiply_bitcast_fusion
  3.8 0.6 fusion.4
  4.4 0.7 fusion.8
  5.1 0.1 fusion.13
  5.2 0.1 copy.44
  5.2 0.1 copy.42
  5.3 0.1 fusion.12
  5.4 0.7 copy.38.refs_5_
  6.1 0.7 copy.37.refs_4_
  6.8 17.6 %shard_map.55 = (f32[128,256]{1,0:T(8,128)}, f32[2,3,128]{2,1,0:T(4,128)}, f32[2,3,128]{2,1,0:T(4,128)}, f32[2,3,128]{2,1,0:T(4,128)}, f32[2,3,128]{2,1,0:T(4,12...) custom-call(s32[1,256]{1,0:T(1,128)} %reshape.52.refs_0_, ...), custom_call_target="tpu_custom_call" | custom-call | tf_op jit(solution)/shard_map/pallas_call | solution.py:336
  24.4 1.0 copy.39
  25.4 0.8 pad_add_fusion.1
  26.2 0.8 copy.46
  27.0 0.8 copy.47
  27.8 0.2 add_bitcast_fusion
  28.2 1.1 %fusion.9 = (bf16[128,3,128]{2,1,0:T(4,128)(2,1)S(1)}, bf16[128,3,128]{2,1,0:T(4,128)(2,1)S(1)}) fusion(bf16[128,128,128]{2,1,0:T(8,128)(2,1)} %refs_0_.1), kind=kLoop, calls=%fused_computation.48 | loop fusion | bytes 393216 | tf_op jit(solution)/shard_map/slice | solution.py:415
  29.3 0.3 bitcast_multiply_fusion.refs_1_
  29.6 0.0 copy-start
  29.7 1.3 %multiply_add_fusion = (f32[3,128,128]{2,1,0:T(8,128)S(1)}, f32[3,128,128]{2,1,0:T(8,128)S(1)}) fusion(bf16[128,128,128]{2,1,0:T(8,128)(2,1)} %refs_0_.1, f32[128]{0:T(128)S(1)} %broadcast_in_dim.55, f32[128,128]{1,0:T(8,128)S(1)} %get-tuple-element.33, f32[128]{0:T(128)S(1)} %broadcast_in_dim.53, f32[128,128]{1,0:T(8,128)S(1)} %get-tuple-element.34), kind=kLoop, calls=%fused_computation.21 | loop fusion | flops 294912 | bytes 721920 | tf_op jit(solution)/shard_map/add | solution.py:411
  31.0 0.0 copy-start.1
  31.0 0.0 copy-start.2
  31.0 0.7 fusion.10
  31.7 0.6 copy.40
  32.3 1.5 %broadcast_in_dim.59.refs_11_ = f32[18,144,128]{2,1,0:T(8,128)} broadcast(f32[18,144]{1,0:T(8,128)S(1)} %pad_maximum_fusion.1), dimensions={0,1} | broadcast | bytes 1337472 | tf_op jit(solution)/shard_map/broadcast_in_dim | solution.py:441
  33.8 1.1 %broadcast_bitcast_fusion = f32[128,128,128]{2,0,1:T(8,128)S(1)} fusion(f32[16,128,128]{2,0,1:T(8,128)S(1)} %copy.40), kind=kLoop, calls=%fused_computation | loop fusion | bytes 9437184 | tf_op jit(solution)/shard_map/reshape | solution.py:413
  34.9 0.9 fusion
  35.8 6.9 %broadcast_in_dim.58.refs_10_ = f32[134,144,128]{2,1,0:T(8,128)} broadcast(f32[134,144]{1,0:T(8,128)S(1)} %get-tuple-element.38), dimensions={0,1} | broadcast | bytes 9956736 | tf_op jit(solution)/shard_map/broadcast_in_dim | solution.py:438
  42.7 0.0 copy-done
  42.7 0.0 copy-done.1
  42.7 0.0 copy-done.2
  42.7 56.1 %shard_map.56 = (f32[128,128,128]{2,1,0:T(8,128)}, f32[1,128]{1,0:T(1,128)}) custom-call(bf16[128,128,128]{2,1,0:T(8,128)(2,1)} %refs_0_.1, f32[16,128,128]{2,1,0:T(8,128)} %copy-done, f32[3,128,128]{2,1,0:T(8,128)} %copy-done.2, f32[3,128,128]{2,1,0:T(8,128)} %copy-done.1, f32[3,128,128]{2,1,0:T(8,128)} %get-tuple-element.28.refs_4_, ...), custom_call_target="tpu_custom_call" | custom-call | flops 75497472 | bytes 22462464 | tf_op jit(solution)/shard_map/pallas_call | solution.py:228
  98.8 7.3 %shard_map.57 = f32[128,128,128]{2,1,0:T(8,128)} custom-call(f32[128,128,128]{2,1,0:T(8,128)} %get-tuple-element.25.x_ref, f32[1,128]{1,0:T(1,128)} %get-tuple-element.26.s_ref), custom_call_target="tpu_custom_call" | custom-call | flops 2097152 | bytes 16777216 | tf_op jit(solution)/shard_map/pallas_call | solution.py:363
  (14 shorter events, 0.2 us)
Async XLA Ops:
  29.6 13.1 %copy-start = (f32[16,128,128]{2,1,0:T(8,128)}, f32[16,128,128]{2,1,0:T(8,128)S(1)}, u32[]{:S(2)}) copy-start(f32[16,128,128]{2,1,0:T(8,128)S(1)} %bitcast_multiply_fusion.refs_1_) | copy-start | bytes 3145732
  31.0 11.7 %copy-start.1 = (f32[3,128,128]{2,1,0:T(8,128)}, f32[3,128,128]{2,1,0:T(8,128)S(1)}, u32[]{:S(2)}) copy-start(f32[3,128,128]{2,1,0:T(8,128)S(1)} %get-tuple-element.31.refs_3_) | copy-start | bytes 589828
  31.0 11.7 %copy-start.2 = (f32[3,128,128]{2,1,0:T(8,128)}, f32[3,128,128]{2,1,0:T(8,128)S(1)}, u32[]{:S(2)}) copy-start(f32[3,128,128]{2,1,0:T(8,128)S(1)} %get-tuple-element.32.refs_2_) | copy-start | bytes 589828

commit v19 on v16

--- a/solution.py
+++ b/solution.py
@@ -395,7 +395,8 @@
             idx[cols_axis] = slice(0, h)
         return a[tuple(idx)]
 
-    gh_t = gh.transpose(0, 2, 1)
+    cell_mask_t = cell_mask.T
+    gh_t = jnp.stack([(cell_mask_t * (4.0 + diagonal.T) - CENTER) / HALF_WIDTH, cell_mask_t / HALF_WIDTH])
     gh_pieces = []
     for dw, dn in DIRS:
         gh_pieces.append(edge(gh_t, dn, dw, 1, 2) if dw == 0 else edge(gh, dw, dn, 1, 2))

time: 105 us -> 105 us (level)
    another operation x3 -> x1, other arithmetic: 2.13 us -> 0.67 us  [local(): gh = jnp.stack([g_own, h_own])]
where the time goes in v19:
time: 105 us
  Pallas kernels  79.6 us (76%)
  local copies, waits for them, and re-layouts  18.4 us (18%)
  other arithmetic  6.62 us (6%)
    pallas_call x1, Pallas kernels, run_stencil(): pl.pallas_call(functools.partial(stencil_kernel, nw, nn, float(total_cell...  56.1 us
    pallas_call x1, Pallas kernels, gather_tiles(): pl.pallas_call(functools.partial(gather_kernel, nw, nn, ccx), in_specs=[v...  17.6 us
    broadcast_in_dim x1, local copies, waits for them, and re-layouts, local(): jnp.broadcast_to(gh_ext[0][:, :, None], (cells_x + 2 * h, width, columns))  6.97 us
    pallas_call x1, Pallas kernels, scale_rows(): pl.pallas_call(scale_kernel, grid=(cx // SCALE_ROWS,), in_specs=[pl.Block...  5.87 us

profile of v19, /device:TPU:1, one launch (start us, length us, event | category | flops | bytes accessed | tf_op | source)
XLA Modules:
  0.0 104.8 jit_solution(5169179847219248087)
XLA Ops:
  0.0 1.3 %reshape.52.refs_0_ = s32[1,256]{1,0:T(1,128)} reshape(s32[16,16]{1,0:T(8,128)} %param.8) | data formatting | bytes 2048 | tf_op jit(solution)/shard_map/reshape | solution.py:332
  1.3 0.7 convert_element_type.36
  2.0 0.1 broadcast_in_dim.54
  2.1 0.1 broadcast_in_dim.55
  2.2 0.1 broadcast_in_dim.52
  2.3 0.1 broadcast_in_dim.53
  2.3 0.1 copy.32
  2.4 0.1 copy.33
  2.5 0.1 copy.36
  2.6 0.1 copy.37
  2.7 0.1 copy.34
  2.8 0.1 copy.35
  2.9 0.1 fusion.9
  3.0 0.1 copy.46
  3.0 0.1 copy.44
  3.1 0.9 fusion.4
  4.0 0.6 pad_maximum_fusion.6
  4.6 0.7 pad_maximum_fusion.2
  5.3 0.1 fusion.3
  5.4 0.7 copy.40.refs_5_
  6.1 0.7 copy.39.refs_4_
  6.7 17.6 %shard_map.55 = (f32[128,256]{1,0:T(8,128)}, f32[2,3,128]{2,1,0:T(4,128)}, f32[2,3,128]{2,1,0:T(4,128)}, f32[2,3,128]{2,1,0:T(4,128)}, f32[2,3,128]{2,1,0:T(4,12...) custom-call(s32[1,256]{1,0:T(1,128)} %reshape.52.refs_0_, ...), custom_call_target="tpu_custom_call" | custom-call | tf_op jit(solution)/shard_map/pallas_call | solution.py:336
  24.4 1.0 copy.41
  25.4 0.8 pad_add_fusion.1
  26.2 0.8 copy.48
  27.0 0.8 copy.49
  27.8 0.2 add_bitcast_fusion
  28.2 1.1 %fusion.6 = (bf16[128,3,128]{2,1,0:T(4,128)(2,1)S(1)}, bf16[128,3,128]{2,1,0:T(4,128)(2,1)S(1)}) fusion(bf16[128,128,128]{2,1,0:T(8,128)(2,1)} %refs_0_.1), kind=kLoop, calls=%fused_computation.44 | loop fusion | bytes 393216 | tf_op jit(solution)/shard_map/slice | solution.py:416
  29.3 0.3 bitcast_multiply_fusion.refs_1_
  29.7 0.0 copy-start
  29.7 1.3 %multiply_add_fusion = (f32[3,128,128]{2,1,0:T(8,128)S(1)}, f32[3,128,128]{2,1,0:T(8,128)S(1)}) fusion(bf16[128,128,128]{2,1,0:T(8,128)(2,1)} %refs_0_.1, f32[128]{0:T(128)S(1)} %broadcast_in_dim.55, f32[128,128]{1,0:T(8,128)S(1)} %get-tuple-element.33, f32[128]{0:T(128)S(1)} %broadcast_in_dim.53, f32[128,128]{1,0:T(8,128)S(1)} %get-tuple-element.34), kind=kLoop, calls=%fused_computation.8 | loop fusion | flops 294912 | bytes 721920 | tf_op jit(solution)/shard_map/add | solution.py:412
  31.0 0.0 copy-start.1
  31.0 0.0 copy-start.2
  31.0 0.7 fusion.7
  31.7 0.6 copy.42
  32.3 1.5 %broadcast_in_dim.59.refs_11_ = f32[18,144,128]{2,1,0:T(8,128)} broadcast(f32[18,144]{1,0:T(8,128)S(1)} %pad_maximum_fusion.1), dimensions={0,1} | broadcast | bytes 1337472 | tf_op jit(solution)/shard_map/broadcast_in_dim | solution.py:442
  33.8 1.1 %broadcast_bitcast_fusion = f32[128,128,128]{2,0,1:T(8,128)S(1)} fusion(f32[16,128,128]{2,0,1:T(8,128)S(1)} %copy.42), kind=kLoop, calls=%fused_computation | loop fusion | bytes 9437184 | tf_op jit(solution)/shard_map/reshape | solution.py:414
  34.9 0.9 fusion
  35.9 7.0 %broadcast_in_dim.58.refs_10_ = f32[134,144,128]{2,1,0:T(8,128)} broadcast(f32[134,144]{1,0:T(8,128)S(1)} %get-tuple-element.38), dimensions={0,1} | broadcast | bytes 9956736 | tf_op jit(solution)/shard_map/broadcast_in_dim | solution.py:439
  42.8 0.0 copy-done
  42.8 0.0 copy-done.1
  42.8 0.0 copy-done.2
  42.8 56.1 %shard_map.56 = (f32[128,128,128]{2,1,0:T(8,128)}, f32[1,128]{1,0:T(1,128)}) custom-call(bf16[128,128,128]{2,1,0:T(8,128)(2,1)} %refs_0_.1, f32[16,128,128]{2,1,0:T(8,128)} %copy-done, f32[3,128,128]{2,1,0:T(8,128)} %copy-done.2, f32[3,128,128]{2,1,0:T(8,128)} %copy-done.1, f32[3,128,128]{2,1,0:T(8,128)} %get-tuple-element.28.refs_4_, ...), custom_call_target="tpu_custom_call" | custom-call | flops 75497472 | bytes 22462464 | tf_op jit(solution)/shard_map/pallas_call | solution.py:228
  99.0 5.9 %shard_map.57 = f32[128,128,128]{2,1,0:T(8,128)} custom-call(f32[128,128,128]{2,1,0:T(8,128)} %get-tuple-element.25.x_ref, f32[1,128]{1,0:T(1,128)} %get-tuple-element.26.s_ref), custom_call_target="tpu_custom_call" | custom-call | flops 2097152 | bytes 16777216 | tf_op jit(solution)/shard_map/pallas_call | solution.py:363
  (14 shorter events, 0.2 us)
Async XLA Ops:
  29.7 13.2 %copy-start = (f32[16,128,128]{2,1,0:T(8,128)}, f32[16,128,128]{2,1,0:T(8,128)S(1)}, u32[]{:S(2)}) copy-start(f32[16,128,128]{2,1,0:T(8,128)S(1)} %bitcast_multiply_fusion.refs_1_) | copy-start | bytes 3145732
  31.0 11.9 %copy-start.1 = (f32[3,128,128]{2,1,0:T(8,128)}, f32[3,128,128]{2,1,0:T(8,128)S(1)}, u32[]{:S(2)}) copy-start(f32[3,128,128]{2,1,0:T(8,128)S(1)} %get-tuple-element.31.refs_3_) | copy-start | bytes 589828
  31.0 11.8 %copy-start.2 = (f32[3,128,128]{2,1,0:T(8,128)}, f32[3,128,128]{2,1,0:T(8,128)S(1)}, u32[]{:S(2)}) copy-start(f32[3,128,128]{2,1,0:T(8,128)S(1)} %get-tuple-element.32.refs_2_) | copy-start | bytes 589828
